TPU v7x, 256 devices: a whole 4x4x8 slice. The times are simulated.
256 devices in a mesh: section: 4 (over y), depth: 64 (over x, z, core).
Axes of the slice: x: 4, y: 4, z: 8, core: 2. Of those that a mesh axis runs over, the one named last changes fastest.
Arguments:
- alignment_input: bfloat16 [4, 2048, 32, 768], P('section', 'depth'), may hold values from -6 to 6
- target_slot: int32 [4, 2048], P('section', 'depth'), may hold values from -1 to 2047, as said below
- device_alignment: int32 [4, 64], P('section'), may hold values from 0 to 31, never falling along the last dimension, each value on 1 to 4 neighbouring positions
- layer_norm_gain: float32 [4, 768], P('section'), may hold values from 0.5 to 1.5
- layer_norm_bias: float32 [4, 768], P('section'), may hold values from -3 to 3
- query_key_value_weight: bfloat16 [4, 768, 2304], P('section'), may hold values from -1.25 to 1.25
- output_weight: bfloat16 [4, 768, 768], P('section'), may hold values from -0.21875 to 0.21875
Outputs:
- handed: bfloat16 [4, 2048, 32, 768], P('section', 'depth')
Inputs may be any that keep to these rules, and one draw needn't show every extreme that they name: `target_slot`: within a section no slot is named twice. The input slots of one device map to 16 devices, 2 consecutive slots each, at offsets along depth that are the same for every device of the section; empty slots carry -1. Every device receives at least 2 rows, in every draw some device sends 2 live rows to one device and some device receives 32 rows. `device_alignment`: an alignment's devices are consecutive, at most 4 of them, and every alignment holds at least one device.
All inputs are finite; a program needn't handle non-finite values.
Results may differ from a plain program's by a relative error of at most 0.0065.
Values may be sent and summed in bfloat16 or wider, within the bound.
No kernel may reach another device: no remote copies, remote signals or barrier semaphores. Data moves between devices by JAX's collectives and lax.ppermute only.
A program may use at most 128 MiB of HBM per device.

v0:
```python
import functools

import jax
import jax.numpy as jnp
from jax import lax
from jax.experimental import pallas as pl
from jax.experimental.pallas import tpu as pltpu
from jax.sharding import PartitionSpec as P


H = 12
DH = 64
PAIRS = H // 2
EPSILON = 1e-05
CHUNK_ROWS = 8
PARTS = 2
INTERPRET = False


def spread_kernel(slot_ref, rows_ref, out_ref, sem):
    count = rows_ref.shape[0]

    def copy_of(i):
        return pltpu.make_async_copy(
            rows_ref.at[i], out_ref.at[jnp.maximum(slot_ref[i], 0)], sem.at[i]
        )

    def begin(i, carry):
        @pl.when(slot_ref[i] >= 0)
        def _():
            copy_of(i).start()

        return carry

    def finish(i, carry):
        @pl.when(slot_ref[i] >= 0)
        def _():
            copy_of(i).wait()

        return carry

    lax.fori_loop(0, count, begin, 0)
    lax.fori_loop(0, count, finish, 0)


def spread(rows, slots, slot_count):
    return pl.pallas_call(
        spread_kernel,
        out_shape=jax.ShapeDtypeStruct((slot_count,) + rows.shape[1:], rows.dtype),
        in_specs=[
            pl.BlockSpec(memory_space=pltpu.SMEM),
            pl.BlockSpec(memory_space=pltpu.VMEM),
        ],
        out_specs=pl.BlockSpec(memory_space=pltpu.HBM),
        scratch_shapes=[pltpu.SemaphoreType.DMA((rows.shape[0],))],
        name="spread",
        interpret=INTERPRET,
    )(slots, rows)


def settle_kernel(source_ref, rows_ref, *refs):
    outs, (landed, in_sem, out_sem) = refs[:PARTS], refs[PARTS:]
    row_count = landed.shape[0]
    part = row_count // PARTS

    def arrival(m):
        return pltpu.make_async_copy(
            rows_ref.at[jnp.maximum(source_ref[m], 0)], landed.at[m], in_sem.at[m]
        )

    def begin(m, carry):
        arrival(m).start()
        return carry

    def empty(m, carry):
        arrival(m).wait()

        @pl.when(source_ref[m] < 0)
        def _():
            landed[m] = jnp.zeros_like(landed[m])

        return carry

    lax.fori_loop(0, row_count, begin, 0)
    lax.fori_loop(0, row_count, empty, 0)
    leaving = [
        pltpu.make_async_copy(landed.at[pl.ds(k * part, part)], out, out_sem.at[k])
        for k, out in enumerate(outs)
    ]
    for copy in leaving:
        copy.start()
    for copy in leaving:
        copy.wait()


def settle(source, rows):
    row_count = source.shape[0]
    length, width = rows.shape[1:]
    return pl.pallas_call(
        settle_kernel,
        out_shape=(jax.ShapeDtypeStruct((row_count // PARTS, length, width), rows.dtype),) * PARTS,
        in_specs=[
            pl.BlockSpec(memory_space=pltpu.SMEM),
            pl.BlockSpec(memory_space=pl.ANY),
        ],
        out_specs=(pl.BlockSpec(memory_space=pltpu.HBM),) * PARTS,
        scratch_shapes=[
            pltpu.VMEM((row_count, length, width), rows.dtype),
            pltpu.SemaphoreType.DMA((row_count,)),
            pltpu.SemaphoreType.DMA((PARTS,)),
        ],
        name="settle",
        interpret=INTERPRET,
    )(source, rows)


def lane_mask(shape):
    return lax.broadcasted_iota(jnp.int32, shape, len(shape) - 1) % 128 < DH


def normalized(block, gain, bias):
    widened = block.astype(jnp.float32)
    average = jnp.mean(widened, axis=-1, keepdims=True)
    centred = widened - average
    spread_of = jnp.mean(centred * centred, axis=-1, keepdims=True)
    return (centred * lax.rsqrt(spread_of + EPSILON) * gain + bias).astype(jnp.bfloat16)


def front_kernel(
    live_ref,
    rows_0_ref,
    rows_1_ref,
    gain_ref,
    bias_ref,
    weight_ref,
    tied_ref,
    tied_low_ref,
    landed,
    acc,
    sem,
):
    row_count = live_ref.shape[0]
    width = rows_0_ref.shape[1]
    length = rows_0_ref.shape[0] * PARTS // row_count
    span = CHUNK_ROWS * length
    chunks = row_count // CHUNK_ROWS
    each = chunks // PARTS
    copies = [
        pltpu.make_async_copy(
            (rows_0_ref, rows_1_ref)[c // each].at[pl.ds(c % each * span, span), :],
            landed.at[c],
            sem.at[c],
        )
        for c in range(chunks)
    ]
    for copy in copies:
        copy.start()
    gain = gain_ref[...]
    bias = bias_ref[...]
    weight = weight_ref[:, : 2 * width]
    first = lane_mask((length, 256))
    acc[...] = jnp.zeros_like(acc)

    def step(c, carry):
        pltpu.make_async_copy(rows_0_ref.at[pl.ds(0, span), :], landed.at[c], sem.at[c]).wait()
        start = c * CHUNK_ROWS
        normed = normalized(landed[c], gain, bias)
        packed = jnp.dot(normed, weight, preferred_element_type=jnp.float32).astype(jnp.bfloat16)
        for pair in range(PAIRS):
            lanes = slice(pair * 128, pair * 128 + 128)
            key_lanes = slice(width + pair * 128, width + pair * 128 + 128)
            total = None
            for r in range(0, CHUNK_ROWS, 2):
                query_parts = []
                key_parts = []
                for k in (r, r + 1):
                    own = slice(k * length, (k + 1) * length)
                    query = packed[own, lanes]
                    query_parts.append(
                        jnp.where(live_ref[start + k] > 0, query, jnp.zeros_like(query))
                    )
                    key_parts.append(packed[own, key_lanes])
                query = jnp.concatenate(query_parts, axis=1)
                key = jnp.concatenate(key_parts, axis=1)
                zero = jnp.zeros_like(query)
                both = jnp.concatenate(
                    [jnp.where(first, query, zero), jnp.where(first, zero, query)], axis=0
                )
                part = lax.dot_general(
                    both, key, (((1,), (1,)), ((), ())), preferred_element_type=jnp.float32
                )
                total = part if total is None else total + part
            acc[pl.ds(pair * 2 * length, 2 * length), :] += total
        return carry

    lax.fori_loop(0, chunks, step, 0)
    quarter = H * length // 4
    tied = jnp.concatenate([acc[pl.ds(q * quarter, quarter), :] for q in range(4)], axis=1)
    tied_ref[...] = tied
    tied_low_ref[...] = tied.astype(jnp.bfloat16)


def front(live, rows, gain, bias, weight):
    row_count = live.shape[0]
    width = rows[0].shape[1]
    length = rows[0].shape[0] * PARTS // row_count
    quarter = H * length // 4
    vmem = pl.BlockSpec(memory_space=pltpu.VMEM)
    smem = pl.BlockSpec(memory_space=pltpu.SMEM)
    return pl.pallas_call(
        front_kernel,
        out_shape=(
            jax.ShapeDtypeStruct((quarter, 4 * length), jnp.float32),
            jax.ShapeDtypeStruct((quarter, 4 * length), jnp.bfloat16),
        ),
        in_specs=[smem] + [pl.BlockSpec(memory_space=pltpu.HBM)] * PARTS + [vmem, vmem, vmem],
        out_specs=(vmem, vmem),
        scratch_shapes=[
            pltpu.VMEM((row_count // CHUNK_ROWS, CHUNK_ROWS * length, width), jnp.bfloat16),
            pltpu.VMEM((H * length, length), jnp.float32),
            pltpu.SemaphoreType.DMA((row_count // CHUNK_ROWS,)),
        ],
        compiler_params=pltpu.CompilerParams(vmem_limit_bytes=40 << 20),
        name="front",
        interpret=INTERPRET,
    )(live, *rows, gain, bias, weight)


def belongs(meta_ref, step):
    other = meta_ref[0] + step
    return jnp.logical_and(other >= meta_ref[1], other < meta_ref[2])


def join_kernel(meta_ref, tied_ref, below_ref, above_ref, sum_ref, up_ref, down_ref):
    tied = tied_ref[...]
    below = jnp.where(belongs(meta_ref, -1), below_ref[...].astype(jnp.float32), 0.0)
    above = jnp.where(belongs(meta_ref, 1), above_ref[...].astype(jnp.float32), 0.0)
    sum_ref[...] = tied + below + above
    up_ref[...] = (tied + below).astype(jnp.bfloat16)
    down_ref[...] = (tied + above).astype(jnp.bfloat16)


def join(meta, tied, below, above):
    vmem = pl.BlockSpec(memory_space=pltpu.VMEM)
    return pl.pallas_call(
        join_kernel,
        out_shape=(
            jax.ShapeDtypeStruct(tied.shape, jnp.float32),
            jax.ShapeDtypeStruct(tied.shape, jnp.bfloat16),
            jax.ShapeDtypeStruct(tied.shape, jnp.bfloat16),
        ),
        in_specs=[pl.BlockSpec(memory_space=pltpu.SMEM), vmem, vmem, vmem],
        out_specs=(vmem, vmem, vmem),
        name="join",
        interpret=INTERPRET,
    )(meta, tied, below, above)


def middle_kernel(live_ref, meta_ref, tied_ref, below_ref, above_ref, out_ref):
    length = tied_ref.shape[1] // 4
    tied = tied_ref[...]
    tied = tied + jnp.where(belongs(meta_ref, -2), below_ref[...].astype(jnp.float32), 0.0)
    tied = tied + jnp.where(belongs(meta_ref, 2), above_ref[...].astype(jnp.float32), 0.0)
    quarter = tied.shape[0]
    count = jnp.full((1, length), meta_ref[3], jnp.int32).astype(jnp.float32)
    scale = DH ** (-0.5) / jnp.sqrt(count)
    logits = (
        jnp.concatenate([tied[:, q * length : (q + 1) * length] for q in range(4)], axis=0) * scale
    )
    top = jnp.max(logits, axis=-1, keepdims=True)
    raised = jnp.exp(logits - top)
    attention = raised / jnp.sum(raised, axis=-1, keepdims=True)
    out_ref[pl.ds(0, quarter), :] = jnp.concatenate(
        [attention[q * quarter : (q + 1) * quarter] for q in range(4)], axis=1
    ).astype(jnp.bfloat16)
    lane = lax.broadcasted_iota(jnp.int32, (16, 4 * length), 1)
    live = jnp.zeros((16, 4 * length), jnp.float32)
    for m in range(live_ref.shape[0]):
        live = jnp.where(jnp.logical_and(lane == m, live_ref[m] > 0), 1.0, live)
    out_ref[pl.ds(quarter, 16), :] = live.astype(jnp.bfloat16)


def middle(live, meta, tied, neighbours):
    vmem = pl.BlockSpec(memory_space=pltpu.VMEM)
    smem = pl.BlockSpec(memory_space=pltpu.SMEM)
    return pl.pallas_call(
        middle_kernel,
        out_shape=jax.ShapeDtypeStruct((tied.shape[0] + 16, tied.shape[1]), jnp.bfloat16),
        in_specs=[smem, smem] + [vmem] * (1 + len(neighbours)),
        out_specs=vmem,
        name="middle",
        interpret=INTERPRET,
    )(live, meta, tied, *neighbours)


def back_kernel(offset, attention_ref, rows_ref, bundle_ref, *refs):
    out_ref, landed, ready, mask, in_sem, out_sem = refs[-6:]
    chunks = landed.shape[0]
    span, width = landed.shape[1:]
    length = span // CHUNK_ROWS
    quarter = H * length // 4

    def arrival(c):
        return pltpu.make_async_copy(
            rows_ref.at[pl.ds(c * span, span), :], landed.at[c], in_sem.at[c]
        )

    def leaving(c):
        return pltpu.make_async_copy(
            ready.at[c], out_ref.at[pl.ds((offset + c) * span, span), :], out_sem.at[c]
        )

    for c in range(chunks):
        arrival(c).start()
    packed = attention_ref[pl.ds(0, quarter), :]
    attention = jnp.concatenate(
        [packed[:, q * length : (q + 1) * length] for q in range(4)], axis=0
    )
    live = attention_ref[pl.ds(quarter, 16), :].astype(jnp.float32)
    for c in range(chunks):
        for k in range(CHUNK_ROWS):
            m = (offset + c) * CHUNK_ROWS + k
            mask[c, pl.ds(k * length, length), :] = jnp.broadcast_to(
                live[0:1, m : m + 1], (length, 128)
            )
    wide = jnp.concatenate([attention] * CHUNK_ROWS, axis=1)
    diagonal = (
        lax.broadcasted_iota(jnp.int32, (span, span), 0) // length
        == lax.broadcasted_iota(jnp.int32, (span, span), 1) // length
    )
    first = lane_mask((span, 128))
    mixers = []
    for h in range(H):
        tall = jnp.concatenate([wide[h * length : (h + 1) * length]] * CHUNK_ROWS, axis=0)
        mixers.append(jnp.where(diagonal, tall, jnp.zeros_like(tall)))
    affine = bundle_ref[pl.ds(2 * width, 16), :].astype(jnp.float32)
    gain = (affine[0:1] + affine[1:2]) + affine[2:3]
    bias = (affine[3:4] + affine[4:5]) + affine[5:6]
    value_weight = bundle_ref[pl.ds(0, width), :]
    weight = bundle_ref[pl.ds(width, width), :]

    def step(c, carry):
        arrival(c).wait()
        block = landed[c]
        values = jnp.dot(
            normalized(block, gain, bias), value_weight, preferred_element_type=jnp.float32
        ).astype(jnp.bfloat16)
        parts = []
        for pair in range(PAIRS):
            lanes = values[:, pair * 128 : pair * 128 + 128]
            low = jnp.dot(mixers[2 * pair], lanes, preferred_element_type=jnp.float32)
            high = jnp.dot(mixers[2 * pair + 1], lanes, preferred_element_type=jnp.float32)
            parts.append(jnp.where(first, low, high).astype(jnp.bfloat16))
        attended = jnp.concatenate(parts, axis=1)
        mixed = jnp.dot(attended, weight, preferred_element_type=jnp.float32)
        mixed = mixed + block.astype(jnp.float32)
        ready[c] = (mixed * jnp.concatenate([mask[c]] * (width // 128), axis=1)).astype(
            jnp.bfloat16
        )
        leaving(c).start()
        return carry

    lax.fori_loop(0, chunks, step, 0)
    for c in range(chunks):
        leaving(c).wait()


def back(index, attention, rows, bundled, row_count, begun):
    vmem = pl.BlockSpec(memory_space=pltpu.VMEM)
    anywhere = pl.BlockSpec(memory_space=pltpu.HBM)
    tokens, width = rows.shape
    chunks = row_count // PARTS // CHUNK_ROWS
    span = tokens // chunks
    return pl.pallas_call(
        functools.partial(back_kernel, index * chunks),
        out_shape=jax.ShapeDtypeStruct((tokens * PARTS, width), jnp.bfloat16),
        in_specs=[vmem, anywhere, vmem] + [anywhere] * len(begun),
        out_specs=anywhere,
        scratch_shapes=[
            pltpu.VMEM((chunks, span, width), jnp.bfloat16),
            pltpu.VMEM((chunks, span, width), jnp.bfloat16),
            pltpu.VMEM((chunks, span, 128), jnp.float32),
            pltpu.SemaphoreType.DMA((chunks,)),
            pltpu.SemaphoreType.DMA((chunks,)),
        ],
        input_output_aliases={3: 0} if begun else {},
        compiler_params=pltpu.CompilerParams(vmem_limit_bytes=40 << 20),
        name="back",
        interpret=INTERPRET,
    )(attention, rows, bundled, *begun)


def shifted(value, axis, steps, wrap):
    count = lax.axis_size(axis)
    if wrap:
        route = [(i, (i + steps) % count) for i in range(count)]
    else:
        route = [(i, i + steps) for i in range(count) if 0 <= i + steps < count]
    return lax.ppermute(value, axis, route)


ROUTE = ((11, 9, 6, 4), (10, 5), 12)
Z_STAY = 8
RING_Z = 8
RING_X = 4


def plan_kernel(
    position_ref, groups_ref, targets_ref, partner_ref, table_ref, meta_ref, pick_ref
):
    peers, row_count = targets_ref.shape
    pair_count = row_count // 2
    position = position_ref[0]
    shape = (peers, 128)
    down = lax.broadcasted_iota(jnp.int32, shape, 0)
    across = lax.broadcasted_iota(jnp.int32, shape, 1)
    zero = jnp.zeros(shape, jnp.int32)

    def over_lanes(value):
        return jnp.broadcast_to(jnp.sum(value, axis=1, keepdims=True), shape)

    def over_rows(value):
        return jnp.broadcast_to(jnp.sum(value, axis=0, keepdims=True), shape)

    def top_rows(value):
        return jnp.max(value, axis=0, keepdims=True)

    def flag(condition):
        return jnp.where(condition, 1, zero)

    def to_lanes(value):
        return over_rows(jnp.where(down == across, value, zero))

    def to_rows(value):
        return over_lanes(jnp.where(down == across, value, zero))

    targets = jnp.concatenate(
        [targets_ref[...], jnp.full((peers, 128 - row_count), -1, jnp.int32)], axis=1
    )
    device = targets >> 5
    offset = jnp.where(targets >= 0, (device - down) & (peers - 1), -1)
    seen = zero
    for i in range(row_count):
        seen = seen | flag(jnp.broadcast_to(offset[:, i : i + 1], shape) == across)
    present_l = flag(over_rows(seen) > 0)
    present = to_rows(present_l)
    odd = down & 1
    odd_l = across & 1

    def turns(core):
        step = ((down + odd * (1 - 2 * core)) >> 1) & 31
        step_l = ((across + odd_l * (1 - 2 * core)) >> 1) & 31
        u, u_l = step & 7, step_l & 7
        order = u * 64 + down
        order_l = u_l * 64 + across
        moving = present * flag(u > 0)
        moving_l = present_l * flag(u_l > 0)
        rank = over_lanes(moving_l * flag(order_l < order))
        rest = over_lanes((present_l - moving_l) * flag(order_l < order))
        return step >> 3, u, moving, rank, rest

    def split_of(core):
        caps = ROUTE[0]
        _, u, moving, rank, _ = turns(core)
        early = moving * flag(rank < across)
        late = moving - early
        good = flag(across <= pair_count)
        for h in range(1, 6):
            cap = caps[h - 1] if h <= len(caps) else 0
            good = good * flag(over_rows(early * flag(u >= h)) <= cap)
            good = good * flag(over_rows(late * flag(RING_Z - u >= h)) <= cap)
        split = jnp.min(jnp.where(good > 0, across, 127), axis=1, keepdims=True)
        return jnp.broadcast_to(split, shape)

    def z_lanes(core, split):
        (z1, z2, z3, z4) = ROUTE[0]
        _, u, moving, rank, rest = turns(core)
        plus = moving * flag(rank < split)
        staying = present - moving
        hops = jnp.where(plus > 0, u, RING_Z - u)
        place = jnp.where(plus > 0, split - 1 - rank, rank - split)
        base = jnp.where(
            hops == 1, 0, jnp.where(hops == 2, z1, jnp.where(hops == 3, z1 + z2, z1 + z2 + z3))
        )
        side = moving - plus
        z_all = z1 + z2 + z3 + z4
        z_leave = jnp.where(staying > 0, 2 * z1 + rest, side * z1 + place)
        z_land = jnp.where(staying > 0, 2 * z_all + rest, side * z_all + base + place)
        return jnp.where(present > 0, z_leave, -1), jnp.where(present > 0, z_land, -1)

    def x_counts(core, line):
        high, u, _, _, _ = turns(core)
        turn = (high + flag(line < u)) & (RING_X - 1)
        turn = jnp.where(present > 0, turn, -1)
        count = [over_rows(flag(turn == v)) for v in range(RING_X)]
        x2 = ROUTE[1][1]
        ahead = (count[2] + count[3] - count[1] + 1) >> 1
        ahead = jnp.minimum(
            jnp.maximum(ahead, jnp.maximum(count[2] - x2, 0)), jnp.minimum(count[2], x2)
        )
        return turn, count, ahead

    def fits(core):
        x1, x2 = ROUTE[1]
        _, count, ahead = x_counts(core, across)
        behind = count[2] - ahead
        good = (
            flag(ahead <= x2)
            * flag(behind <= x2)
            * flag(ahead + count[1] <= x1)
            * flag(behind + count[3] <= x1)
            * flag(count[0] <= ROUTE[2])
        )
        return jnp.min(jnp.where(across < RING_Z, good, 1))

    def x_lanes(core, line):
        x1, x2 = ROUTE[1]
        turn, count, ahead = x_counts(core, line)
        turn_l = to_lanes(turn)
        level = over_lanes(present_l * flag(turn_l == turn) * flag(across < down))
        double = flag(turn == 2)
        near = double * flag(level < ahead)
        forward = flag(turn == 1) + near
        spot = jnp.where(
            double > 0,
            level - jnp.where(near > 0, 0, ahead),
            level + jnp.where(turn == 1, ahead, count[2] - ahead),
        )
        side = 1 - forward
        x_leave = jnp.where(turn == 0, 2 * x1 + level, side * x1 + spot)
        x_land = jnp.where(
            turn == 0, 2 * (x1 + x2) + level, side * (x1 + x2) + double * x1 + spot
        )
        return jnp.where(present > 0, x_leave, -1), jnp.where(present > 0, x_land, -1)

    core = position & 1
    split = split_of(core)
    z_leave, z_land = z_lanes(core, split)
    line = (position >> 1) & (RING_Z - 1)
    x_leave_a, x_land_a = x_lanes(core, line)
    x_leave_b, x_land_b = x_lanes(core, RING_Z - 1 - line)
    other_split = split_of(1 - core)
    good = jnp.where(
        jnp.max(jnp.maximum(split, other_split)) <= pair_count, fits(core) * fits(1 - core), 0
    )

    lane_row = lax.broadcasted_iota(jnp.int32, (1, 128), 1)
    origin = -1 + zero
    for b in range(2):
        sender = position if b == 0 else position ^ 1
        mine = targets_ref[pl.ds(sender, 1), :]
        mine = jnp.concatenate([mine, jnp.full((1, 128 - row_count), -1, jnp.int32)], axis=1)
        away = ((mine >> 5) - sender) & (peers - 1)
        away = jnp.where(mine >= 0, away, -1)
        away = jnp.where((away & 1) == b, away, -1)
        hit = jnp.broadcast_to(away, shape) == down
        code = b * pair_count + (jnp.broadcast_to(lane_row, shape) >> 1)
        found = jnp.max(jnp.where(hit, code, -1), axis=1, keepdims=True)
        origin = jnp.maximum(origin, jnp.broadcast_to(found, shape))

    def gathered(slot_of, value):
        return top_rows(jnp.where(slot_of == across, value, -1))

    local = targets - position * row_count
    here = jnp.logical_and(local >= 0, local < row_count)
    settled_a = jnp.full((1, 128), -1, jnp.int32)
    settled_b = settled_a
    lane_full = across & 1
    for r in range(2):
        slot = jnp.max(
            jnp.where(jnp.logical_and(here, lane_full == r), local, -1), axis=1, keepdims=True
        )
        slot = jnp.broadcast_to(slot, shape)
        slot_l = over_rows(jnp.where(down == across, slot + 1, zero)) - 1
        match = across == ((position - down) & (peers - 1))
        slot_by_offset = over_lanes(jnp.where(match, slot_l + 1, zero)) - 1
        settled_a = jnp.maximum(settled_a, gathered(slot_by_offset, x_land_a * 2 + r))
        settled_b = jnp.maximum(settled_b, gathered(slot_by_offset, z_land * 2 + r))
    empty = jnp.full((1, 128), -1, jnp.int32)
    table_ref[...] = jnp.concatenate(
        [
            gathered(z_leave, origin),
            gathered(x_leave_b, origin),
            gathered(x_leave_a, z_land),
            gathered(z_leave, x_land_b),
            settled_a,
            settled_b,
            empty,
            empty,
        ],
        axis=0,
    )
    groups = groups_ref[...]
    lane = lax.broadcasted_iota(jnp.int32, groups.shape, 1)
    own_group = jnp.sum(jnp.where(lane == position, groups, 0))
    low = jnp.sum(jnp.where(groups < own_group, 1, 0))
    high = low + jnp.sum(jnp.where(groups == own_group, 1, 0))
    inside = jnp.logical_and(targets >= low * row_count, targets < high * row_count)
    meta_ref[0] = position
    meta_ref[1] = low
    meta_ref[2] = high
    meta_ref[3] = jnp.sum(jnp.where(inside, 1, 0))
    pick_ref[0] = good


def plan(position, groups, targets, partner):
    vmem = pl.BlockSpec(memory_space=pltpu.VMEM)
    smem = pl.BlockSpec(memory_space=pltpu.SMEM)
    return pl.pallas_call(
        plan_kernel,
        out_shape=(
            jax.ShapeDtypeStruct((8, 128), jnp.int32),
            jax.ShapeDtypeStruct((4,), jnp.int32),
            jax.ShapeDtypeStruct((1,), jnp.int32),
        ),
        in_specs=[smem, vmem, vmem, pl.BlockSpec(memory_space=pltpu.HBM)],
        out_specs=(vmem, smem, smem),
        name="plan",
        interpret=INTERPRET,
    )(position.reshape(1), groups, targets, partner)


def pieces(value):
    parts = []
    for _ in range(3):
        part = value.astype(jnp.bfloat16)
        parts.append(part.astype(jnp.float32))
        value = value - parts[-1]
    return parts


def bundle_kernel(weight_ref, out_weight_ref, gain_ref, bias_ref, out_ref, held, sem):
    width = held.shape[1]
    loads = [
        pltpu.make_async_copy(
            weight_ref.at[:, pl.ds(2 * width, width)], held.at[pl.ds(0, width), :], sem.at[0]
        ),
        pltpu.make_async_copy(out_weight_ref, held.at[pl.ds(width, width), :], sem.at[1]),
    ]
    for load in loads:
        load.start()
    rows = pieces(gain_ref[...]) + pieces(bias_ref[...])
    rows.append(jnp.zeros((16 - len(rows), width), jnp.float32))
    held[pl.ds(2 * width, 16), :] = jnp.concatenate(rows, axis=0).astype(jnp.bfloat16)
    for load in loads:
        load.wait()
    store = pltpu.make_async_copy(held, out_ref, sem.at[2])
    store.start()
    store.wait()


def bundle(weight, out_weight, gain, bias):
    width = weight.shape[0]
    vmem = pl.BlockSpec(memory_space=pltpu.VMEM)
    hbm = pl.BlockSpec(memory_space=pltpu.HBM)
    shape = (2 * width + 16, width)
    return pl.pallas_call(
        bundle_kernel,
        out_shape=jax.ShapeDtypeStruct(shape, weight.dtype),
        in_specs=[hbm, hbm, vmem, vmem],
        out_specs=hbm,
        scratch_shapes=[pltpu.VMEM(shape, weight.dtype), pltpu.SemaphoreType.DMA((3,))],
        name="bundle",
        interpret=INTERPRET,
    )(weight, out_weight, gain, bias)


def deal(table_ref, row, pool, outs):
    lane = 0
    for out in outs:

        def step(k, carry, out=out, lane=lane):
            out[k] = pool[jnp.maximum(table_ref[row, lane + k], 0)]
            return carry

        lax.fori_loop(0, out.shape[0], step, 0)
        lane += out.shape[0]


def leave_kernel(table_ref, own_ref, partner_ref, *refs):
    outs, (pool, sem) = refs[:-2], refs[-2:]
    pairs = own_ref.shape[0]
    half = own_ref.shape[2] // 2
    copies = []
    for part in range(2):
        for b, ref in enumerate((own_ref, partner_ref)):
            copies.append(
                pltpu.make_async_copy(
                    ref.at[:, :, pl.ds(part * half, half), :],
                    pool.at[part, pl.ds(b * pairs, pairs)],
                    sem.at[len(copies)],
                )
            )
    for copy in copies:
        copy.start()
    for part in range(2):
        copies[2 * part].wait()
        copies[2 * part + 1].wait()
        deal(table_ref, part, pool.at[part], outs[3 * part : 3 * part + 3])


def leave(table, own, partner, route):
    (z1, _, _, _), (x1, _), x_stay = route
    pairs, two, length, width = own.shape
    vmem = pl.BlockSpec(memory_space=pltpu.VMEM)
    anywhere = pl.BlockSpec(memory_space=pl.ANY)
    sizes = (z1, z1, Z_STAY, x1, x1, x_stay)
    return pl.pallas_call(
        leave_kernel,
        out_shape=tuple(
            jax.ShapeDtypeStruct((n, two, length // 2, width), own.dtype) for n in sizes
        ),
        in_specs=[pl.BlockSpec(memory_space=pltpu.SMEM), anywhere, anywhere],
        out_specs=(vmem,) * len(sizes),
        scratch_shapes=[
            pltpu.VMEM((2, 2 * pairs, two, length // 2, width), own.dtype),
            pltpu.SemaphoreType.DMA((4,)),
        ],
        compiler_params=pltpu.CompilerParams(vmem_limit_bytes=40 << 20),
        name="leave",
        interpret=INTERPRET,
    )(table, own, partner)


def pooled(refs, pool, sem):
    copies = []
    start = 0
    for ref in refs:
        count = ref.shape[0]
        copies.append(
            pltpu.make_async_copy(ref, pool.at[pl.ds(start, count)], sem.at[len(copies)])
        )
        start += count
    return copies


def turn_kernel(row, count, table_ref, *refs):
    sources, outs, (pool, sem) = refs[:count], refs[count:-2], refs[-2:]
    copies = pooled(sources, pool, sem)
    for copy in copies:
        copy.start()
    for copy in copies:
        copy.wait()
    deal(table_ref, row, pool, outs)


def turn_over(table, row, sources, sizes):
    vmem = pl.BlockSpec(memory_space=pltpu.VMEM)
    anywhere = pl.BlockSpec(memory_space=pl.ANY)
    payload = sources[0].shape[1:]
    return pl.pallas_call(
        functools.partial(turn_kernel, row, len(sources)),
        out_shape=tuple(jax.ShapeDtypeStruct((n,) + payload, sources[0].dtype) for n in sizes),
        in_specs=[pl.BlockSpec(memory_space=pltpu.SMEM)] + [anywhere] * len(sources),
        out_specs=(vmem,) * len(sizes),
        scratch_shapes=[
            pltpu.VMEM((sum(s.shape[0] for s in sources),) + payload, sources[0].dtype),
            pltpu.SemaphoreType.DMA((len(sources),)),
        ],
        compiler_params=pltpu.CompilerParams(vmem_limit_bytes=40 << 20),
        name="turn_over",
        interpret=INTERPRET,
    )(table, *sources)


def land_kernel(count_a, count_b, table_ref, *refs):
    sources_a, sources_b = refs[:count_a], refs[count_a : count_a + count_b]
    outs = refs[count_a + count_b : count_a + count_b + PARTS]
    live_ref, pool_a, pool_b, done, sem_a, sem_b, out_sem = refs[count_a + count_b + PARTS :]
    row_count, length, _ = done.shape
    half = length // 2
    copies = pooled(sources_a, pool_a, sem_a) + pooled(sources_b, pool_b, sem_b)
    for copy in copies:
        copy.start()
    for copy in copies:
        copy.wait()

    def step(m, carry):
        live = table_ref[4, m] >= 0
        live_ref[m] = jnp.where(live, 1, 0)
        for part, pool in ((0, pool_a), (1, pool_b)):
            code = jnp.maximum(table_ref[4 + part, m], 0)
            value = pool[code >> 1, code & 1]
            done[m, pl.ds(part * half, half), :] = jnp.where(live, value, jnp.zeros_like(value))
        return carry

    rows = row_count // PARTS
    leaving = [
        pltpu.make_async_copy(done.at[pl.ds(k * rows, rows)], out, out_sem.at[k])
        for k, out in enumerate(outs)
    ]
    for k in range(PARTS):
        lax.fori_loop(k * rows, (k + 1) * rows, step, 0)
        leaving[k].start()
    for copy in leaving:
        copy.wait()


def land(table, sources_a, sources_b, row_count, length):
    anywhere = pl.BlockSpec(memory_space=pl.ANY)
    smem = pl.BlockSpec(memory_space=pltpu.SMEM)
    two, half, width = sources_a[0].shape[1:]
    dtype = sources_a[0].dtype
    return pl.pallas_call(
        functools.partial(land_kernel, len(sources_a), len(sources_b)),
        out_shape=(jax.ShapeDtypeStruct((row_count // PARTS, length, width), dtype),) * PARTS
        + (jax.ShapeDtypeStruct((row_count,), jnp.int32),),
        in_specs=[smem] + [anywhere] * (len(sources_a) + len(sources_b)),
        out_specs=(pl.BlockSpec(memory_space=pltpu.HBM),) * PARTS + (smem,),
        scratch_shapes=[
            pltpu.VMEM((sum(s.shape[0] for s in sources_a), two, half, width), dtype),
            pltpu.VMEM((sum(s.shape[0] for s in sources_b), two, half, width), dtype),
            pltpu.VMEM((row_count, length, width), dtype),
            pltpu.SemaphoreType.DMA((len(sources_a),)),
            pltpu.SemaphoreType.DMA((len(sources_b),)),
            pltpu.SemaphoreType.DMA((PARTS,)),
        ],
        compiler_params=pltpu.CompilerParams(vmem_limit_bytes=40 << 20),
        name="land",
        interpret=INTERPRET,
    )(table, *sources_a, *sources_b)


def chain(forward, backward, caps, step, ring):
    def moved(i, by):
        return (i // (step * ring)) * step * ring + (i + by * step) % (step * ring)

    devices = range(lax.axis_size("depth"))
    onward, returning = [], []
    for cap in caps:
        forward = lax.ppermute(forward[:cap], "depth", [(i, moved(i, 1)) for i in devices])
        backward = lax.ppermute(backward[:cap], "depth", [(i, moved(i, -1)) for i in devices])
        onward.append(forward)
        returning.append(backward)
    return onward + returning


def routed(route, table, own, partner):
    z_caps, x_caps, x_stay = route
    z_sizes = (z_caps[0], z_caps[0], Z_STAY)
    x_sizes = (x_caps[0], x_caps[0], x_stay)
    z_plus, z_minus, z_still, x_plus, x_minus, x_still = leave(table, own, partner, route)
    along_x = chain(x_plus, x_minus, x_caps, 2 * RING_Z, RING_X)
    along_z = chain(z_plus, z_minus, z_caps, 2, RING_Z)
    later = turn_over(table, 3, along_x + [x_still], z_sizes)
    last_b = chain(later[0], later[1], z_caps, 2, RING_Z)
    turned = turn_over(table, 2, along_z + [z_still], x_sizes)
    last_a = chain(turned[0], turned[1], x_caps, 2 * RING_Z, RING_X)
    return land(
        table,
        last_a + [turned[2]],
        last_b + [later[2]],
        own.shape[0] * own.shape[1],
        own.shape[2],
    )


def dense(targets, everywhere, own):
    row_count = targets.shape[0]
    _, _, length, width = own.shape
    peers = lax.axis_size("depth")
    position = lax.axis_index("depth")
    capacity = max(2, (row_count + peers - 1) // peers)
    slots = jnp.where(
        targets >= 0,
        targets // row_count * capacity + jnp.arange(row_count) % capacity,
        -1,
    )
    outgoing = spread(own.reshape(row_count, length, width), slots, peers * capacity)
    got = lax.all_to_all(
        outgoing.reshape((peers, capacity, length, width)),
        "depth",
        split_axis=0,
        concat_axis=0,
        tiled=True,
    ).reshape(peers * capacity, length, width)
    local = everywhere - position * row_count
    mine = jnp.logical_and(local >= 0, local < row_count)
    code = (
        lax.broadcasted_iota(jnp.int32, (peers, row_count), 0) * capacity
        + lax.broadcasted_iota(jnp.int32, (peers, row_count), 1) % capacity
    )
    wanted = jnp.where(mine, local, -1).reshape(1, -1)
    hit = jnp.arange(row_count)[:, None] == wanted
    source = jnp.max(jnp.where(hit, code.reshape(1, -1), -1), axis=1)
    return (*settle(source, got), (source >= 0).astype(jnp.int32))


def layer(
    alignment_input,
    target_slot,
    device_alignment,
    layer_norm_gain,
    layer_norm_bias,
    query_key_value_weight,
    output_weight,
):
    targets = target_slot[0]
    row_count, length, width = alignment_input.shape[1:]
    peers = lax.axis_size("depth")
    position = lax.axis_index("depth")
    own = alignment_input.reshape(row_count // 2, 2, length, width)
    everywhere = lax.all_to_all(
        jnp.broadcast_to(targets[None, None], (peers, 1, row_count)),
        "depth",
        split_axis=0,
        concat_axis=0,
        tiled=True,
    ).reshape(peers, row_count)
    partner = lax.ppermute(own, "depth", [(i, i ^ 1) for i in range(peers)])
    bundled = bundle(query_key_value_weight[0], output_weight[0], layer_norm_gain, layer_norm_bias)
    bundled = shifted(bundled, "section", 1, True)
    table, meta, pick = plan(position, device_alignment, everywhere, partner)
    *settled, live = lax.switch(
        pick[0],
        [
            lambda t, o, p, a, b: dense(a, b, o),
            lambda t, o, p, a, b: routed(ROUTE, t, o, p),
        ],
        table,
        own,
        partner,
        targets,
        everywhere,
    )
    balanced = [part.reshape(-1, width) for part in settled]
    earlier = [shifted(part, "section", 1, True) for part in balanced]
    tied, tied_low = front(
        live, balanced, layer_norm_gain, layer_norm_bias, query_key_value_weight[0]
    )
    tied, up, down = join(
        meta, tied, shifted(tied_low, "depth", 1, False), shifted(tied_low, "depth", -1, False)
    )
    neighbours = [shifted(up, "depth", 2, False), shifted(down, "depth", -2, False)]
    attention = shifted(middle(live, meta, tied, neighbours), "section", 1, True)
    begun = ()
    for index, rows in enumerate(earlier):
        begun = (
            back(
                index, attention, rows, bundled, row_count, begun
            ),
        )
    return begun[0].reshape(1, row_count, length, width)


def solution(mesh):
    placed = (
        P("section", "depth", None, None),
        P("section", "depth"),
        P("section", None),
        P("section", None),
        P("section", None),
        P("section", None, None),
        P("section", None, None),
    )
    return jax.shard_map(
        layer,
        mesh=mesh,
        in_specs=placed,
        out_specs=P("section", "depth", None, None),
        check_vma=False,
    )
```

profile of v0, /device:TPU:2, one launch (start us, length us, event | category | flops | bytes accessed | tf_op | source)
XLA Modules:
  0.0 173.0 jit_solution(15601163909231205504)
XLA Ops:
  0.0 3.9 %bundle.1 = bf16[1552,768]{1,0:T(8,128)(2,1)} custom-call(bf16[768,2304]{1,0:T(8,128)(2,1)} %bitcast.13, bf16[768,768]{1,0:T(8,128)(2,1)} %bitcast.19, f32[1,768]{1,0:T(1,128)} %gain_ref.3, f32[1,768]{1,0:T(1,128)} %bias_ref.3), custom_call_target="tpu_custom_call" | custom-call | tf_op jit(solution)/shard_map/bundle/pallas_call | solution.py:657
  6.2 12.1 %all-to-all-start.1 = ((s32[64,1,32]{2,1,0:T(1,128)}), s32[64,1,32]{2,1,0:T(1,128)S(1)}, u32[]{:S(2)}, u32[]{:S(2)}) async-start(s32[64,1,32]{2,1,0:T(1,128)} %broadcast_in_dim.27), calls=%async_computation.1 | async-start | bytes 65536 | tf_op jit(solution)/shard_map/all_to_all | solution.py:903
  18.3 8.5 %all-to-all-done.1 = s32[64,1,32]{2,1,0:T(1,128)S(1)} async-done(((s32[64,1,32]{2,1,0:T(1,128)}), s32[64,1,32]{2,1,0:T(1,128)S(1)}, u32[]{:S(2)}, u32[]{:S(2)}) %all-to-all-start.1) | async-done | bytes 8224 | tf_op jit(solution)/shard_map/all_to_all | solution.py:903
  30.0 90.3 %conditional.1 = ((bf16[16,32,768]{2,1,0:T(8,128)(2,1)}, bf16[16,32,768]{2,1,0:T(8,128)(2,1)}, s32[32]{0:T(128)S(1)})) conditional(s32[]{:T(128)} %bitcast.7, (s32[64,32]{1,0:T(8,128)}, s32[32]{0:T(128)S(1)}, bf16[1,32,32,768]{3,2,1,0:T(8,128)(2,1)}) %tuple.22, (s32[8,128]{1,0:T(8,128)S(1)}, bf16[16,2,32,768]{3,2,1,0:T(8,128)(2,1)}, ...), branch_computations={%region_0.2_spmd, %region_2.3_spmd} | conditional | flops 212035 | bytes 44827592 | solution.py:914
  30.0 3.2 %leave.1 = (bf16[11,2,16,768]{3,2,1,0:T(8,128)(2,1)S(1)}, bf16[11,2,16,768]{3,2,1,0:T(8,128)(2,1)S(1)}, bf16[8,2,16,768]{3,2,1,0:T(8,128)(2,1)S(1)}, bf16[10,2,1...) custom-call(s32[8,128]{1,0:T(8,128)S(1)} %get-tuple-element.22.table_ref, ...), custom_call_target="tpu_custom_call" | custom-call | tf_op jit(solution)/shard_map/cond/branch_1_fun/leave/pallas_call | solution.py:708
  38.6 8.1 %collective-permute-done.12.refs_0_ = bf16[10,2,16,768]{3,2,1,0:T(8,128)(2,1)S(1)} collective-permute-done((bf16[10,2,16,768]{3,2,1,0:T(8,128)(2,1)S(1)}, bf16[10,2,16,768]{3,2,1,0:T(8,128)(2,1)S(1)}, u32[]{:S(2)}, u32[]{:S(2)}) %collective-permute-start.12) | collective-permute-done | bytes 491552 | tf_op jit(solution)/shard_map/cond/branch_1_fun/ppermute | solution.py:831
  51.0 3.3 %collective-permute-start.5 = (bf16[9,2,16,768]{3,2,1,0:T(8,128)(2,1)S(1)}, bf16[9,2,16,768]{3,2,1,0:T(8,128)(2,1)S(1)}, u32[]{:S(2)}, u32[]{:S(2)}) collective-permute-start(bf16[9,2,16,768]{3,2,1,0:T(8,128)(2,1)S(1)} %slice.51), channel_id=1, source_target_pairs={{0,14},{1,15},{2,0},{3,1},{4,2},{5,3},{6,4},{7,5},{8,6},{9,7},{10,... | collective-permute-start | bytes 1327112 | tf_op jit(solution)/shard_map/cond/branch_1_fun/ppermute | solution.py:832
  58.3 3.2 %collective-permute-start.20 = (bf16[11,2,16,768]{3,2,1,0:T(8,128)(2,1)S(1)}, bf16[11,2,16,768]{3,2,1,0:T(8,128)(2,1)S(1)}, u32[]{:S(2)}, u32[]{:S(2)}) collective-permute-start(bf16[11,2,16,768]{3,2,1,0:T(8,128)(2,1)S(1)} %get-tuple-element.35), channel_id=1, source_target_pairs={{0,14},{1,15},{2,0},{3,1},{4,2},{5,3},{6,4},{7,5},{8,6},{9,7},{10,... | collective-permute-start | bytes 1622024 | tf_op jit(solution)/shard_map/cond/branch_1_fun/ppermute | solution.py:832
  61.6 3.0 %collective-permute-done.1.refs_1_ = bf16[9,2,16,768]{3,2,1,0:T(8,128)(2,1)S(1)} collective-permute-done((bf16[9,2,16,768]{3,2,1,0:T(8,128)(2,1)S(1)}, bf16[9,2,16,768]{3,2,1,0:T(8,128)(2,1)S(1)}, u32[]{:S(2)}, u32[]{:S(2)}) %collective-permute-start.1) | collective-permute-done | bytes 442400 | tf_op jit(solution)/shard_map/cond/branch_1_fun/ppermute | solution.py:831
  64.7 3.3 %collective-permute-start.6 = (bf16[6,2,16,768]{3,2,1,0:T(8,128)(2,1)S(1)}, bf16[6,2,16,768]{3,2,1,0:T(8,128)(2,1)S(1)}, u32[]{:S(2)}, u32[]{:S(2)}) collective-permute-start(bf16[6,2,16,768]{3,2,1,0:T(8,128)(2,1)S(1)} %slice.52), channel_id=1, source_target_pairs={{0,14},{1,15},{2,0},{3,1},{4,2},{5,3},{6,4},{7,5},{8,6},{9,7},{10,... | collective-permute-start | bytes 884744 | tf_op jit(solution)/shard_map/cond/branch_1_fun/ppermute | solution.py:832
  68.0 12.0 %collective-permute-done.2.refs_2_ = bf16[6,2,16,768]{3,2,1,0:T(8,128)(2,1)S(1)} collective-permute-done((bf16[6,2,16,768]{3,2,1,0:T(8,128)(2,1)S(1)}, bf16[6,2,16,768]{3,2,1,0:T(8,128)(2,1)S(1)}, u32[]{:S(2)}, u32[]{:S(2)}) %collective-permute-start.2) | collective-permute-done | bytes 294944 | tf_op jit(solution)/shard_map/cond/branch_1_fun/ppermute | solution.py:831
  80.2 3.3 %collective-permute-start.7 = (bf16[4,2,16,768]{3,2,1,0:T(8,128)(2,1)S(1)}, bf16[4,2,16,768]{3,2,1,0:T(8,128)(2,1)S(1)}, u32[]{:S(2)}, u32[]{:S(2)}) collective-permute-start(bf16[4,2,16,768]{3,2,1,0:T(8,128)(2,1)S(1)} %slice.53), channel_id=1, source_target_pairs={{0,14},{1,15},{2,0},{3,1},{4,2},{5,3},{6,4},{7,5},{8,6},{9,7},{10,... | collective-permute-start | bytes 589832 | tf_op jit(solution)/shard_map/cond/branch_1_fun/ppermute | solution.py:832
  83.7 3.3 %collective-permute-start.21 = (bf16[9,2,16,768]{3,2,1,0:T(8,128)(2,1)S(1)}, bf16[9,2,16,768]{3,2,1,0:T(8,128)(2,1)S(1)}, u32[]{:S(2)}, u32[]{:S(2)}) collective-permute-start(bf16[9,2,16,768]{3,2,1,0:T(8,128)(2,1)S(1)} %slice.61), channel_id=1, source_target_pairs={{0,14},{1,15},{2,0},{3,1},{4,2},{5,3},{6,4},{7,5},{8,6},{9,7},{10,... | collective-permute-start | bytes 1327112 | tf_op jit(solution)/shard_map/cond/branch_1_fun/ppermute | solution.py:832
  91.7 3.9 %collective-permute-start.10 = (bf16[10,2,16,768]{3,2,1,0:T(8,128)(2,1)S(1)}, bf16[10,2,16,768]{3,2,1,0:T(8,128)(2,1)S(1)}, u32[]{:S(2)}, u32[]{:S(2)}) collective-permute-start(bf16[10,2,16,768]{3,2,1,0:T(8,128)(2,1)S(1)} %get-tuple-element.29), channel_id=1, source_target_pairs={{0,48},{1,49},{2,50},{3,51},{4,52},{5,53},{6,54},{7,55},{8,56},{9,... | collective-permute-start | bytes 1474568 | tf_op jit(solution)/shard_map/cond/branch_1_fun/ppermute | solution.py:832
  96.3 3.3 %collective-permute-start.22 = (bf16[6,2,16,768]{3,2,1,0:T(8,128)(2,1)S(1)}, bf16[6,2,16,768]{3,2,1,0:T(8,128)(2,1)S(1)}, u32[]{:S(2)}, u32[]{:S(2)}) collective-permute-start(bf16[6,2,16,768]{3,2,1,0:T(8,128)(2,1)S(1)} %slice.62), channel_id=1, source_target_pairs={{0,14},{1,15},{2,0},{3,1},{4,2},{5,3},{6,4},{7,5},{8,6},{9,7},{10,... | collective-permute-start | bytes 884744 | tf_op jit(solution)/shard_map/cond/branch_1_fun/ppermute | solution.py:832
  99.6 4.7 %collective-permute-done.10.refs_2_ = bf16[10,2,16,768]{3,2,1,0:T(8,128)(2,1)S(1)} collective-permute-done((bf16[10,2,16,768]{3,2,1,0:T(8,128)(2,1)S(1)}, bf16[10,2,16,768]{3,2,1,0:T(8,128)(2,1)S(1)}, u32[]{:S(2)}, u32[]{:S(2)}) %collective-permute-start.10) | collective-permute-done | bytes 491552 | tf_op jit(solution)/shard_map/cond/branch_1_fun/ppermute | solution.py:832
  107.2 3.6 %collective-permute-start.23 = (bf16[4,2,16,768]{3,2,1,0:T(8,128)(2,1)S(1)}, bf16[4,2,16,768]{3,2,1,0:T(8,128)(2,1)S(1)}, u32[]{:S(2)}, u32[]{:S(2)}) collective-permute-start(bf16[4,2,16,768]{3,2,1,0:T(8,128)(2,1)S(1)} %slice.63), channel_id=1, source_target_pairs={{0,14},{1,15},{2,0},{3,1},{4,2},{5,3},{6,4},{7,5},{8,6},{9,7},{10,... | collective-permute-start | bytes 589832 | tf_op jit(solution)/shard_map/cond/branch_1_fun/ppermute | solution.py:832
  114.3 5.8 %land.1 = (bf16[16,32,768]{2,1,0:T(8,128)(2,1)}, bf16[16,32,768]{2,1,0:T(8,128)(2,1)}, s32[32]{0:T(128)S(1)}) custom-call(s32[8,128]{1,0:T(8,128)S(1)} %get-tuple-element.22.table_ref, bf16[10,2,16,768]{3,2,1,0:T(8,128)(2,1)S(1)} %collective-permute-done.8.refs_0_, bf16[5,2,16,768]{3,2,1,0:T(8,128)(2,1)S(1)} %collective-permute-done.9.refs_1_, ...), custom_call_target="tpu_custom_call" | custom-call | tf_op jit(solution)/shard_map/cond/branch_1_fun/land/pallas_call | solution.py:804
  123.1 6.7 %front.1 = (f32[96,128]{1,0:T(8,128)S(1)}, bf16[96,128]{1,0:T(8,128)(2,1)S(1)}) custom-call(s32[32]{0:T(128)S(1)} %get-tuple-element.50.live_ref, bf16[512,768]{1,0:T(8,128)(2,1)} %bitcast.21, bf16[512,768]{1,0:T(8,128)(2,1)} %bitcast.23, f32[1,768]{1,0:T(1,128)S(1)} %copy-done.2, f32[1,768]{1,0:T(1,128)S(1)} %copy-done.3, bf16[768,2304]{1,0:T(8,128)(2,1)S(1)} %bitcast.14), custom_call_target="tpu_custom_call" | custom-call | tf_op jit(solution)/shard_map/front/pallas_call | solution.py:210
  132.3 5.8 %collective-permute-start.26 = (bf16[96,128]{1,0:T(8,128)(2,1)S(1)}, bf16[96,128]{1,0:T(8,128)(2,1)S(1)}, u32[]{:S(2)}, u32[]{:S(2)}) collective-permute-start(bf16[96,128]{1,0:T(8,128)(2,1)S(1)} %get-tuple-element.55), channel_id=1, source_target_pairs={{1,0},{2,1},{3,2},{4,3},{5,4},{6,5},{7,6},{8,7},{9,8},{10,9},{11,1... | collective-permute-start | bytes 73736 | tf_op jit(solution)/shard_map/ppermute | solution.py:399
  143.6 6.0 %collective-permute-start.28 = (bf16[96,128]{1,0:T(8,128)(2,1)}, bf16[96,128]{1,0:T(8,128)(2,1)S(1)}, u32[]{:S(2)}, u32[]{:S(2)}) collective-permute-start(bf16[96,128]{1,0:T(8,128)(2,1)} %get-tuple-element.58), channel_id=1, source_target_pairs={{2,0},{3,1},{4,2},{5,3},{6,4},{7,5},{8,6},{9,7},{10,8},{11,9},{12,... | collective-permute-start | bytes 73736 | tf_op jit(solution)/shard_map/ppermute | solution.py:399
  154.0 5.1 %collective-permute-done.29.attention_ref = bf16[112,128]{1,0:T(8,128)(2,1)S(1)} collective-permute-done((bf16[112,128]{1,0:T(8,128)(2,1)}, bf16[112,128]{1,0:T(8,128)(2,1)S(1)}, u32[]{:S(2)}, u32[]{:S(2)}) %collective-permute-start.29) | collective-permute-done | bytes 28704 | tf_op jit(solution)/shard_map/ppermute | solution.py:399
  159.0 6.9 %back.2.refs_0_ = bf16[1024,768]{1,0:T(8,128)(2,1)} custom-call(bf16[112,128]{1,0:T(8,128)(2,1)S(1)} %collective-permute-done.29.attention_ref, bf16[512,768]{1,0:T(8,128)(2,1)} %collective-permute-done.32.rows_ref, bf16[1552,768]{1,0:T(8,128)(2,1)} %collective-permute-done.31.bundle_ref), custom_call_target="tpu_custom_call" | custom-call | tf_op jit(solution)/shard_map/back/pallas_call | solution.py:374
  166.0 6.8 %back.3 = bf16[1024,768]{1,0:T(8,128)(2,1)} custom-call(bf16[112,128]{1,0:T(8,128)(2,1)S(1)} %collective-permute-done.29.attention_ref, bf16[512,768]{1,0:T(8,128)(2,1)} %collective-permute-done.30.rows_ref, bf16[1552,768]{1,0:T(8,128)(2,1)} %collective-permute-done.31.bundle_ref, bf16[1024,768]{1,0:T(8,128)(2,1)} %back.2.refs_0_), custom_call_target="tpu_custom_call", output_to_operand_aliasing={{}: (3, {})} | custom-call | tf_op jit(solution)/shard_map/back/pallas_call | solution.py:374
  (97 shorter events, 45.9 us)
Async XLA Ops:
  3.9 155.1 %collective-permute-start.31 = (bf16[1552,768]{1,0:T(8,128)(2,1)}, bf16[1552,768]{1,0:T(8,128)(2,1)}, u32[]{:S(2)}, u32[]{:S(2)}) collective-permute-start(bf16[1552,768]{1,0:T(8,128)(2,1)} %bundle.1), channel_id=1, source_target_pairs={{0,64},{64,128},{128,192},{192,0},{1,65},{65,129},{129,193},{193,1... | collective-permute-start | bytes 7151624 | tf_op jit(solution)/shard_map/ppermute | solution.py:399
  5.5 21.3 %collective-permute-start.24 = (bf16[16,2,32,768]{3,2,1,0:T(8,128)(2,1)S(1)}, bf16[16,2,32,768]{3,2,1,0:T(8,128)(2,1)S(1)}, u32[]{:S(2)}, u32[]{:S(2)}) collective-permute-start(bf16[16,2,32,768]{3,2,1,0:T(8,128)(2,1)S(1)} %bitcast.17), channel_id=1, source_target_pairs={{0,1},{1,0},{2,3},{3,2},{4,5},{5,4},{6,7},{7,6},{8,9},{9,8},{10,11... | collective-permute-start | bytes 4718600 | tf_op jit(solution)/shard_map/ppermute | solution.py:910
  6.2 20.7 %all-to-all-start.1 = ((s32[64,1,32]{2,1,0:T(1,128)}), s32[64,1,32]{2,1,0:T(1,128)S(1)}, u32[]{:S(2)}, u32[]{:S(2)}) async-start(s32[64,1,32]{2,1,0:T(1,128)} %broadcast_in_dim.27), calls=%async_computation.1 | async-start | bytes 65536 | tf_op jit(solution)/shard_map/all_to_all | solution.py:903
  33.2 17.7 %collective-permute-start = (bf16[11,2,16,768]{3,2,1,0:T(8,128)(2,1)S(1)}, bf16[11,2,16,768]{3,2,1,0:T(8,128)(2,1)S(1)}, u32[]{:S(2)}, u32[]{:S(2)}) collective-permute-start(bf16[11,2,16,768]{3,2,1,0:T(8,128)(2,1)S(1)} %get-tuple-element.25), channel_id=1, source_target_pairs={{0,2},{1,3},{2,4},{3,5},{4,6},{5,7},{6,8},{7,9},{8,10},{9,11},{10,... | collective-permute-start | bytes 1622024 | tf_op jit(solution)/shard_map/cond/branch_1_fun/ppermute | solution.py:831
  33.9 12.7 %collective-permute-start.12 = (bf16[10,2,16,768]{3,2,1,0:T(8,128)(2,1)S(1)}, bf16[10,2,16,768]{3,2,1,0:T(8,128)(2,1)S(1)}, u32[]{:S(2)}, u32[]{:S(2)}) collective-permute-start(bf16[10,2,16,768]{3,2,1,0:T(8,128)(2,1)S(1)} %get-tuple-element.31), channel_id=1, source_target_pairs={{0,16},{1,17},{2,18},{3,19},{4,20},{5,21},{6,22},{7,23},{8,24},{9,... | collective-permute-start | bytes 1474568 | tf_op jit(solution)/shard_map/cond/branch_1_fun/ppermute | solution.py:831
  34.6 16.4 %collective-permute-start.4 = (bf16[11,2,16,768]{3,2,1,0:T(8,128)(2,1)S(1)}, bf16[11,2,16,768]{3,2,1,0:T(8,128)(2,1)S(1)}, u32[]{:S(2)}, u32[]{:S(2)}) collective-permute-start(bf16[11,2,16,768]{3,2,1,0:T(8,128)(2,1)S(1)} %get-tuple-element.26), channel_id=1, source_target_pairs={{0,14},{1,15},{2,0},{3,1},{4,2},{5,3},{6,4},{7,5},{8,6},{9,7},{10,... | collective-permute-start | bytes 1622024 | tf_op jit(solution)/shard_map/cond/branch_1_fun/ppermute | solution.py:832
  37.2 12.1 %collective-permute-start.14 = (bf16[10,2,16,768]{3,2,1,0:T(8,128)(2,1)S(1)}, bf16[10,2,16,768]{3,2,1,0:T(8,128)(2,1)S(1)}, u32[]{:S(2)}, u32[]{:S(2)}) collective-permute-start(bf16[10,2,16,768]{3,2,1,0:T(8,128)(2,1)S(1)} %get-tuple-element.32), channel_id=1, source_target_pairs={{0,48},{1,49},{2,50},{3,51},{4,52},{5,53},{6,54},{7,55},{8,56},{9,... | collective-permute-start | bytes 1474568 | tf_op jit(solution)/shard_map/cond/branch_1_fun/ppermute | solution.py:832
  50.9 13.7 %collective-permute-start.1 = (bf16[9,2,16,768]{3,2,1,0:T(8,128)(2,1)S(1)}, bf16[9,2,16,768]{3,2,1,0:T(8,128)(2,1)S(1)}, u32[]{:S(2)}, u32[]{:S(2)}) collective-permute-start(bf16[9,2,16,768]{3,2,1,0:T(8,128)(2,1)S(1)} %slice.48), channel_id=1, source_target_pairs={{0,2},{1,3},{2,4},{3,5},{4,6},{5,7},{6,8},{7,9},{8,10},{9,11},{10,... | collective-permute-start | bytes 1327112 | tf_op jit(solution)/shard_map/cond/branch_1_fun/ppermute | solution.py:831
  51.0 13.7 %collective-permute-start.5 = (bf16[9,2,16,768]{3,2,1,0:T(8,128)(2,1)S(1)}, bf16[9,2,16,768]{3,2,1,0:T(8,128)(2,1)S(1)}, u32[]{:S(2)}, u32[]{:S(2)}) collective-permute-start(bf16[9,2,16,768]{3,2,1,0:T(8,128)(2,1)S(1)} %slice.51), channel_id=1, source_target_pairs={{0,14},{1,15},{2,0},{3,1},{4,2},{5,3},{6,4},{7,5},{8,6},{9,7},{10,... | collective-permute-start | bytes 1327112 | tf_op jit(solution)/shard_map/cond/branch_1_fun/ppermute | solution.py:832
  58.1 25.4 %collective-permute-start.16 = (bf16[11,2,16,768]{3,2,1,0:T(8,128)(2,1)S(1)}, bf16[11,2,16,768]{3,2,1,0:T(8,128)(2,1)S(1)}, u32[]{:S(2)}, u32[]{:S(2)}) collective-permute-start(bf16[11,2,16,768]{3,2,1,0:T(8,128)(2,1)S(1)} %get-tuple-element.34), channel_id=1, source_target_pairs={{0,2},{1,3},{2,4},{3,5},{4,6},{5,7},{6,8},{7,9},{8,10},{9,11},{10,... | collective-permute-start | bytes 1622024 | tf_op jit(solution)/shard_map/cond/branch_1_fun/ppermute | solution.py:831
  58.3 25.3 %collective-permute-start.20 = (bf16[11,2,16,768]{3,2,1,0:T(8,128)(2,1)S(1)}, bf16[11,2,16,768]{3,2,1,0:T(8,128)(2,1)S(1)}, u32[]{:S(2)}, u32[]{:S(2)}) collective-permute-start(bf16[11,2,16,768]{3,2,1,0:T(8,128)(2,1)S(1)} %get-tuple-element.35), channel_id=1, source_target_pairs={{0,14},{1,15},{2,0},{3,1},{4,2},{5,3},{6,4},{7,5},{8,6},{9,7},{10,... | collective-permute-start | bytes 1622024 | tf_op jit(solution)/shard_map/cond/branch_1_fun/ppermute | solution.py:832
  64.6 15.5 %collective-permute-start.2 = (bf16[6,2,16,768]{3,2,1,0:T(8,128)(2,1)S(1)}, bf16[6,2,16,768]{3,2,1,0:T(8,128)(2,1)S(1)}, u32[]{:S(2)}, u32[]{:S(2)}) collective-permute-start(bf16[6,2,16,768]{3,2,1,0:T(8,128)(2,1)S(1)} %slice.49), channel_id=1, source_target_pairs={{0,2},{1,3},{2,4},{3,5},{4,6},{5,7},{6,8},{7,9},{8,10},{9,11},{10,... | collective-permute-start | bytes 884744 | tf_op jit(solution)/shard_map/cond/branch_1_fun/ppermute | solution.py:831
  64.7 15.4 %collective-permute-start.6 = (bf16[6,2,16,768]{3,2,1,0:T(8,128)(2,1)S(1)}, bf16[6,2,16,768]{3,2,1,0:T(8,128)(2,1)S(1)}, u32[]{:S(2)}, u32[]{:S(2)}) collective-permute-start(bf16[6,2,16,768]{3,2,1,0:T(8,128)(2,1)S(1)} %slice.52), channel_id=1, source_target_pairs={{0,14},{1,15},{2,0},{3,1},{4,2},{5,3},{6,4},{7,5},{8,6},{9,7},{10,... | collective-permute-start | bytes 884744 | tf_op jit(solution)/shard_map/cond/branch_1_fun/ppermute | solution.py:832
  80.1 9.1 %collective-permute-start.3 = (bf16[4,2,16,768]{3,2,1,0:T(8,128)(2,1)S(1)}, bf16[4,2,16,768]{3,2,1,0:T(8,128)(2,1)S(1)}, u32[]{:S(2)}, u32[]{:S(2)}) collective-permute-start(bf16[4,2,16,768]{3,2,1,0:T(8,128)(2,1)S(1)} %slice.50), channel_id=1, source_target_pairs={{0,2},{1,3},{2,4},{3,5},{4,6},{5,7},{6,8},{7,9},{8,10},{9,11},{10,... | collective-permute-start | bytes 589832 | tf_op jit(solution)/shard_map/cond/branch_1_fun/ppermute | solution.py:831
  80.2 8.9 %collective-permute-start.7 = (bf16[4,2,16,768]{3,2,1,0:T(8,128)(2,1)S(1)}, bf16[4,2,16,768]{3,2,1,0:T(8,128)(2,1)S(1)}, u32[]{:S(2)}, u32[]{:S(2)}) collective-permute-start(bf16[4,2,16,768]{3,2,1,0:T(8,128)(2,1)S(1)} %slice.53), channel_id=1, source_target_pairs={{0,14},{1,15},{2,0},{3,1},{4,2},{5,3},{6,4},{7,5},{8,6},{9,7},{10,... | collective-permute-start | bytes 589832 | tf_op jit(solution)/shard_map/cond/branch_1_fun/ppermute | solution.py:832
  83.5 12.6 %collective-permute-start.17 = (bf16[9,2,16,768]{3,2,1,0:T(8,128)(2,1)S(1)}, bf16[9,2,16,768]{3,2,1,0:T(8,128)(2,1)S(1)}, u32[]{:S(2)}, u32[]{:S(2)}) collective-permute-start(bf16[9,2,16,768]{3,2,1,0:T(8,128)(2,1)S(1)} %slice.58), channel_id=1, source_target_pairs={{0,2},{1,3},{2,4},{3,5},{4,6},{5,7},{6,8},{7,9},{8,10},{9,11},{10,... | collective-permute-start | bytes 1327112 | tf_op jit(solution)/shard_map/cond/branch_1_fun/ppermute | solution.py:831
  83.7 12.6 %collective-permute-start.21 = (bf16[9,2,16,768]{3,2,1,0:T(8,128)(2,1)S(1)}, bf16[9,2,16,768]{3,2,1,0:T(8,128)(2,1)S(1)}, u32[]{:S(2)}, u32[]{:S(2)}) collective-permute-start(bf16[9,2,16,768]{3,2,1,0:T(8,128)(2,1)S(1)} %slice.61), channel_id=1, source_target_pairs={{0,14},{1,15},{2,0},{3,1},{4,2},{5,3},{6,4},{7,5},{8,6},{9,7},{10,... | collective-permute-start | bytes 1327112 | tf_op jit(solution)/shard_map/cond/branch_1_fun/ppermute | solution.py:832
  91.7 12.6 %collective-permute-start.10 = (bf16[10,2,16,768]{3,2,1,0:T(8,128)(2,1)S(1)}, bf16[10,2,16,768]{3,2,1,0:T(8,128)(2,1)S(1)}, u32[]{:S(2)}, u32[]{:S(2)}) collective-permute-start(bf16[10,2,16,768]{3,2,1,0:T(8,128)(2,1)S(1)} %get-tuple-element.29), channel_id=1, source_target_pairs={{0,48},{1,49},{2,50},{3,51},{4,52},{5,53},{6,54},{7,55},{8,56},{9,... | collective-permute-start | bytes 1474568 | tf_op jit(solution)/shard_map/cond/branch_1_fun/ppermute | solution.py:832
  95.5 11.4 %collective-permute-start.8 = (bf16[10,2,16,768]{3,2,1,0:T(8,128)(2,1)S(1)}, bf16[10,2,16,768]{3,2,1,0:T(8,128)(2,1)S(1)}, u32[]{:S(2)}, u32[]{:S(2)}) collective-permute-start(bf16[10,2,16,768]{3,2,1,0:T(8,128)(2,1)S(1)} %get-tuple-element.28), channel_id=1, source_target_pairs={{0,16},{1,17},{2,18},{3,19},{4,20},{5,21},{6,22},{7,23},{8,24},{9,... | collective-permute-start | bytes 1474568 | tf_op jit(solution)/shard_map/cond/branch_1_fun/ppermute | solution.py:831
  96.2 10.9 %collective-permute-start.18 = (bf16[6,2,16,768]{3,2,1,0:T(8,128)(2,1)S(1)}, bf16[6,2,16,768]{3,2,1,0:T(8,128)(2,1)S(1)}, u32[]{:S(2)}, u32[]{:S(2)}) collective-permute-start(bf16[6,2,16,768]{3,2,1,0:T(8,128)(2,1)S(1)} %slice.59), channel_id=1, source_target_pairs={{0,2},{1,3},{2,4},{3,5},{4,6},{5,7},{6,8},{7,9},{8,10},{9,11},{10,... | collective-permute-start | bytes 884744 | tf_op jit(solution)/shard_map/cond/branch_1_fun/ppermute | solution.py:831
  96.3 10.9 %collective-permute-start.22 = (bf16[6,2,16,768]{3,2,1,0:T(8,128)(2,1)S(1)}, bf16[6,2,16,768]{3,2,1,0:T(8,128)(2,1)S(1)}, u32[]{:S(2)}, u32[]{:S(2)}) collective-permute-start(bf16[6,2,16,768]{3,2,1,0:T(8,128)(2,1)S(1)} %slice.62), channel_id=1, source_target_pairs={{0,14},{1,15},{2,0},{3,1},{4,2},{5,3},{6,4},{7,5},{8,6},{9,7},{10,... | collective-permute-start | bytes 884744 | tf_op jit(solution)/shard_map/cond/branch_1_fun/ppermute | solution.py:832
  120.3 38.7 %collective-permute-start.32 = (bf16[512,768]{1,0:T(8,128)(2,1)}, bf16[512,768]{1,0:T(8,128)(2,1)}, u32[]{:S(2)}, u32[]{:S(2)}) collective-permute-start(bf16[512,768]{1,0:T(8,128)(2,1)} %bitcast.20), channel_id=1, source_target_pairs={{0,64},{64,128},{128,192},{192,0},{1,65},{65,129},{129,193},{193,1... | collective-permute-start | bytes 2359304 | tf_op jit(solution)/shard_map/ppermute | solution.py:399
  121.8 44.1 %collective-permute-start.30 = (bf16[512,768]{1,0:T(8,128)(2,1)}, bf16[512,768]{1,0:T(8,128)(2,1)}, u32[]{:S(2)}, u32[]{:S(2)}) collective-permute-start(bf16[512,768]{1,0:T(8,128)(2,1)} %bitcast.22), channel_id=1, source_target_pairs={{0,64},{64,128},{128,192},{192,0},{1,65},{65,129},{129,193},{193,1... | collective-permute-start | bytes 2359304 | tf_op jit(solution)/shard_map/ppermute | solution.py:399
  141.7 8.0 %collective-permute-start.27 = (bf16[96,128]{1,0:T(8,128)(2,1)}, bf16[96,128]{1,0:T(8,128)(2,1)S(1)}, u32[]{:S(2)}, u32[]{:S(2)}) collective-permute-start(bf16[96,128]{1,0:T(8,128)(2,1)} %get-tuple-element.57), channel_id=1, source_target_pairs={{0,2},{1,3},{2,4},{3,5},{4,6},{5,7},{6,8},{7,9},{8,10},{9,11},{10,... | collective-permute-start | bytes 73736 | tf_op jit(solution)/shard_map/ppermute | solution.py:399
  (22 other events, 370.6 us)
where the time goes:
time: 175 us; the launch traced here: 173 us
  starting transfers between devices  70.5 us (40%)
  waiting for transfers between devices  54.3 us (31%)
  Pallas kernels  43.8 us (25%)
  local copies, waits for them, and re-layouts  2.82 us (2%)
    ppermute x12, starting transfers between devices, chain(): lax.ppermute(backward[:cap], 'depth', [(i, moved(i, -1)) for i in devices])  35.1 us
    ppermute x12, waiting for transfers between devices, chain(): lax.ppermute(forward[:cap], 'depth', [(i, moved(i, 1)) for i in devices])  29.5 us
    ppermute x8, starting transfers between devices, shifted(): return lax.ppermute(value, axis, route)  20.3 us
    pallas_call x2, Pallas kernels, back(): pl.pallas_call(functools.partial(back_kernel, index * chunks), out_shape=...  13.7 us
    all_to_all x1, starting transfers between devices, layer(): lax.all_to_all(jnp.broadcast_to(targets[None, None], (peers, 1, row_count...  12.1 us
    all_to_all x1, waiting for transfers between devices, layer(): lax.all_to_all(jnp.broadcast_to(targets[None, None], (peers, 1, row_count...  8.54 us
    ppermute x8, waiting for transfers between devices, shifted(): return lax.ppermute(value, axis, route)  8.26 us
    ppermute x12, waiting for transfers between devices, chain(): lax.ppermute(backward[:cap], 'depth', [(i, moved(i, -1)) for i in devices])  7.99 us
  transfers between devices with their start and end apart: 34, of which 16 were waited for; matrix products, arithmetic and copies ran while one was open for 1% of the time, Pallas kernels for 19%

commit v1 on v0

--- a/solution.py
+++ b/solution.py
@@ -293,36 +293,78 @@
     )(live, meta, tied, *neighbours)
 
 
-def back_kernel(offset, attention_ref, rows_ref, bundle_ref, *refs):
-    out_ref, landed, ready, mask, in_sem, out_sem = refs[-6:]
+def values_kernel(rows_ref, bundle_ref, out_ref, landed, sem):
+    chunks = landed.shape[0]
+    span, width = landed.shape[1:]
+
+    def arrival(c):
+        return pltpu.make_async_copy(
+            rows_ref.at[pl.ds(c * span, span), :], landed.at[c], sem.at[c]
+        )
+
+    for c in range(chunks):
+        arrival(c).start()
+    affine = bundle_ref[pl.ds(2 * width, 16), :].astype(jnp.float32)
+    gain = (affine[0:1] + affine[1:2]) + affine[2:3]
+    bias = (affine[3:4] + affine[4:5]) + affine[5:6]
+    weight = bundle_ref[pl.ds(0, width), :]
+
+    def step(c, carry):
+        arrival(c).wait()
+        out_ref[c] = jnp.dot(
+            normalized(landed[c], gain, bias), weight, preferred_element_type=jnp.float32
+        ).astype(jnp.bfloat16)
+        return carry
+
+    lax.fori_loop(0, chunks, step, 0)
+
+
+def values_of(rows, bundled, row_count):
+    vmem = pl.BlockSpec(memory_space=pltpu.VMEM)
+    tokens, width = rows.shape
+    chunks = row_count // PARTS // CHUNK_ROWS
+    shape = (chunks, tokens // chunks, width)
+    return pl.pallas_call(
+        values_kernel,
+        out_shape=jax.ShapeDtypeStruct(shape, jnp.bfloat16),
+        in_specs=[pl.BlockSpec(memory_space=pltpu.HBM), vmem],
+        out_specs=vmem,
+        scratch_shapes=[pltpu.VMEM(shape, jnp.bfloat16), pltpu.SemaphoreType.DMA((chunks,))],
+        compiler_params=pltpu.CompilerParams(vmem_limit_bytes=40 << 20),
+        name="values",
+        interpret=INTERPRET,
+    )(rows, bundled)
+
+
+def finish_kernel(attention_ref, bundle_ref, *refs):
+    rows_refs, values_refs = refs[:PARTS], refs[PARTS : 2 * PARTS]
+    out_ref, landed, held, mask, row_sem, value_sem, out_sem = refs[2 * PARTS :]
     chunks = landed.shape[0]
     span, width = landed.shape[1:]
     length = span // CHUNK_ROWS
     quarter = H * length // 4
-
-    def arrival(c):
-        return pltpu.make_async_copy(
-            rows_ref.at[pl.ds(c * span, span), :], landed.at[c], in_sem.at[c]
-        )
+    each = chunks // PARTS
+    for c in range(chunks):
+        part = c // each
+        pltpu.make_async_copy(values_refs[part].at[c % each], held.at[c], value_sem.at[c]).start()
+        pltpu.make_async_copy(
+            rows_refs[part].at[pl.ds(c % each * span, span), :], landed.at[c], row_sem.at[c]
+        ).start()
 
     def leaving(c):
         return pltpu.make_async_copy(
-            ready.at[c], out_ref.at[pl.ds((offset + c) * span, span), :], out_sem.at[c]
-        )
-
-    for c in range(chunks):
-        arrival(c).start()
+            held.at[c], out_ref.at[pl.ds(c * span, span), :], out_sem.at[c]
+        )
+
     packed = attention_ref[pl.ds(0, quarter), :]
     attention = jnp.concatenate(
         [packed[:, q * length : (q + 1) * length] for q in range(4)], axis=0
     )
     live = attention_ref[pl.ds(quarter, 16), :].astype(jnp.float32)
-    for c in range(chunks):
-        for k in range(CHUNK_ROWS):
-            m = (offset + c) * CHUNK_ROWS + k
-            mask[c, pl.ds(k * length, length), :] = jnp.broadcast_to(
-                live[0:1, m : m + 1], (length, 128)
-            )
+    for m in range(chunks * CHUNK_ROWS):
+        mask[m // CHUNK_ROWS, pl.ds(m % CHUNK_ROWS * length, length), :] = jnp.broadcast_to(
+            live[0:1, m : m + 1], (length, 128)
+        )
     wide = jnp.concatenate([attention] * CHUNK_ROWS, axis=1)
     diagonal = (
         lax.broadcasted_iota(jnp.int32, (span, span), 0) // length
@@ -333,18 +375,11 @@
     for h in range(H):
         tall = jnp.concatenate([wide[h * length : (h + 1) * length]] * CHUNK_ROWS, axis=0)
         mixers.append(jnp.where(diagonal, tall, jnp.zeros_like(tall)))
-    affine = bundle_ref[pl.ds(2 * width, 16), :].astype(jnp.float32)
-    gain = (affine[0:1] + affine[1:2]) + affine[2:3]
-    bias = (affine[3:4] + affine[4:5]) + affine[5:6]
-    value_weight = bundle_ref[pl.ds(0, width), :]
     weight = bundle_ref[pl.ds(width, width), :]
 
     def step(c, carry):
-        arrival(c).wait()
-        block = landed[c]
-        values = jnp.dot(
-            normalized(block, gain, bias), value_weight, preferred_element_type=jnp.float32
-        ).astype(jnp.bfloat16)
+        pltpu.make_async_copy(values_refs[0].at[0], held.at[c], value_sem.at[c]).wait()
+        values = held[c]
         parts = []
         for pair in range(PAIRS):
             lanes = values[:, pair * 128 : pair * 128 + 128]
@@ -353,8 +388,11 @@
             parts.append(jnp.where(first, low, high).astype(jnp.bfloat16))
         attended = jnp.concatenate(parts, axis=1)
         mixed = jnp.dot(attended, weight, preferred_element_type=jnp.float32)
-        mixed = mixed + block.astype(jnp.float32)
-        ready[c] = (mixed * jnp.concatenate([mask[c]] * (width // 128), axis=1)).astype(
+        pltpu.make_async_copy(
+            rows_refs[0].at[pl.ds(0, span), :], landed.at[c], row_sem.at[c]
+        ).wait()
+        mixed = mixed + landed[c].astype(jnp.float32)
+        held[c] = (mixed * jnp.concatenate([mask[c]] * (width // 128), axis=1)).astype(
             jnp.bfloat16
         )
         leaving(c).start()
@@ -365,29 +403,30 @@
         leaving(c).wait()
 
 
-def back(index, attention, rows, bundled, row_count, begun):
+def finish(attention, bundled, rows, values):
     vmem = pl.BlockSpec(memory_space=pltpu.VMEM)
-    anywhere = pl.BlockSpec(memory_space=pltpu.HBM)
-    tokens, width = rows.shape
-    chunks = row_count // PARTS // CHUNK_ROWS
-    span = tokens // chunks
-    return pl.pallas_call(
-        functools.partial(back_kernel, index * chunks),
+    hbm = pl.BlockSpec(memory_space=pltpu.HBM)
+    anywhere = pl.BlockSpec(memory_space=pl.ANY)
+    tokens, width = rows[0].shape
+    each, span, _ = values[0].shape
+    shape = (each * PARTS, span, width)
+    return pl.pallas_call(
+        finish_kernel,
         out_shape=jax.ShapeDtypeStruct((tokens * PARTS, width), jnp.bfloat16),
-        in_specs=[vmem, anywhere, vmem] + [anywhere] * len(begun),
-        out_specs=anywhere,
+        in_specs=[vmem, vmem] + [hbm] * PARTS + [anywhere] * PARTS,
+        out_specs=hbm,
         scratch_shapes=[
-            pltpu.VMEM((chunks, span, width), jnp.bfloat16),
-            pltpu.VMEM((chunks, span, width), jnp.bfloat16),
-            pltpu.VMEM((chunks, span, 128), jnp.float32),
-            pltpu.SemaphoreType.DMA((chunks,)),
-            pltpu.SemaphoreType.DMA((chunks,)),
+            pltpu.VMEM(shape, jnp.bfloat16),
+            pltpu.VMEM(shape, jnp.bfloat16),
+            pltpu.VMEM((each * PARTS, span, 128), jnp.float32),
+            pltpu.SemaphoreType.DMA((each * PARTS,)),
+            pltpu.SemaphoreType.DMA((each * PARTS,)),
+            pltpu.SemaphoreType.DMA((each * PARTS,)),
         ],
-        input_output_aliases={3: 0} if begun else {},
         compiler_params=pltpu.CompilerParams(vmem_limit_bytes=40 << 20),
-        name="back",
-        interpret=INTERPRET,
-    )(attention, rows, bundled, *begun)
+        name="finish",
+        interpret=INTERPRET,
+    )(attention, bundled, *rows, *values)
 
 
 def shifted(value, axis, steps, wrap):
@@ -677,44 +716,39 @@
         lane += out.shape[0]
 
 
-def leave_kernel(table_ref, own_ref, partner_ref, *refs):
+def leave_kernel(part, table_ref, own_ref, partner_ref, *refs):
     outs, (pool, sem) = refs[:-2], refs[-2:]
     pairs = own_ref.shape[0]
     half = own_ref.shape[2] // 2
-    copies = []
-    for part in range(2):
-        for b, ref in enumerate((own_ref, partner_ref)):
-            copies.append(
-                pltpu.make_async_copy(
-                    ref.at[:, :, pl.ds(part * half, half), :],
-                    pool.at[part, pl.ds(b * pairs, pairs)],
-                    sem.at[len(copies)],
-                )
-            )
+    copies = [
+        pltpu.make_async_copy(
+            ref.at[:, :, pl.ds(part * half, half), :],
+            pool.at[pl.ds(b * pairs, pairs)],
+            sem.at[b],
+        )
+        for b, ref in enumerate((own_ref, partner_ref))
+    ]
     for copy in copies:
         copy.start()
-    for part in range(2):
-        copies[2 * part].wait()
-        copies[2 * part + 1].wait()
-        deal(table_ref, part, pool.at[part], outs[3 * part : 3 * part + 3])
-
-
-def leave(table, own, partner, route):
-    (z1, _, _, _), (x1, _), x_stay = route
+    for copy in copies:
+        copy.wait()
+    deal(table_ref, part, pool, outs)
+
+
+def leave(part, table, own, partner, sizes):
     pairs, two, length, width = own.shape
     vmem = pl.BlockSpec(memory_space=pltpu.VMEM)
     anywhere = pl.BlockSpec(memory_space=pl.ANY)
-    sizes = (z1, z1, Z_STAY, x1, x1, x_stay)
-    return pl.pallas_call(
-        leave_kernel,
+    return pl.pallas_call(
+        functools.partial(leave_kernel, part),
         out_shape=tuple(
             jax.ShapeDtypeStruct((n, two, length // 2, width), own.dtype) for n in sizes
         ),
         in_specs=[pl.BlockSpec(memory_space=pltpu.SMEM), anywhere, anywhere],
         out_specs=(vmem,) * len(sizes),
         scratch_shapes=[
-            pltpu.VMEM((2, 2 * pairs, two, length // 2, width), own.dtype),
-            pltpu.SemaphoreType.DMA((4,)),
+            pltpu.VMEM((2 * pairs, two, length // 2, width), own.dtype),
+            pltpu.SemaphoreType.DMA((2,)),
         ],
         compiler_params=pltpu.CompilerParams(vmem_limit_bytes=40 << 20),
         name="leave",
@@ -763,30 +797,32 @@
     )(table, *sources)
 
 
-def land_kernel(count_a, count_b, table_ref, *refs):
-    sources_a, sources_b = refs[:count_a], refs[count_a : count_a + count_b]
-    outs = refs[count_a + count_b : count_a + count_b + PARTS]
-    live_ref, pool_a, pool_b, done, sem_a, sem_b, out_sem = refs[count_a + count_b + PARTS :]
-    row_count, length, _ = done.shape
-    half = length // 2
-    copies = pooled(sources_a, pool_a, sem_a) + pooled(sources_b, pool_b, sem_b)
+def land_kernel(part, count, table_ref, *refs):
+    sources = refs[:count]
+    outs = refs[-PARTS - 5 : -5]
+    live_ref, pool, done, in_sem, out_sem = refs[-5:]
+    row_count, half, _ = done.shape
+    copies = pooled(sources, pool, in_sem)
     for copy in copies:
         copy.start()
     for copy in copies:
         copy.wait()
 
     def step(m, carry):
-        live = table_ref[4, m] >= 0
+        live = table_ref[4 + part, m] >= 0
         live_ref[m] = jnp.where(live, 1, 0)
-        for part, pool in ((0, pool_a), (1, pool_b)):
-            code = jnp.maximum(table_ref[4 + part, m], 0)
-            value = pool[code >> 1, code & 1]
-            done[m, pl.ds(part * half, half), :] = jnp.where(live, value, jnp.zeros_like(value))
+        code = jnp.maximum(table_ref[4 + part, m], 0)
+        value = pool[code >> 1, code & 1]
+        done[m] = jnp.where(live, value, jnp.zeros_like(value))
         return carry
 
     rows = row_count // PARTS
     leaving = [
-        pltpu.make_async_copy(done.at[pl.ds(k * rows, rows)], out, out_sem.at[k])
+        pltpu.make_async_copy(
+            done.at[pl.ds(k * rows, rows)],
+            out.at[:, pl.ds(part * half, half), :],
+            out_sem.at[k],
+        )
         for k, out in enumerate(outs)
     ]
     for k in range(PARTS):
@@ -796,29 +832,30 @@
         copy.wait()
 
 
-def land(table, sources_a, sources_b, row_count, length):
+def land(part, table, sources, row_count, length, begun):
     anywhere = pl.BlockSpec(memory_space=pl.ANY)
     smem = pl.BlockSpec(memory_space=pltpu.SMEM)
-    two, half, width = sources_a[0].shape[1:]
-    dtype = sources_a[0].dtype
-    return pl.pallas_call(
-        functools.partial(land_kernel, len(sources_a), len(sources_b)),
+    hbm = pl.BlockSpec(memory_space=pltpu.HBM)
+    two, half, width = sources[0].shape[1:]
+    dtype = sources[0].dtype
+    count = len(sources)
+    return pl.pallas_call(
+        functools.partial(land_kernel, part, count),
         out_shape=(jax.ShapeDtypeStruct((row_count // PARTS, length, width), dtype),) * PARTS
         + (jax.ShapeDtypeStruct((row_count,), jnp.int32),),
-        in_specs=[smem] + [anywhere] * (len(sources_a) + len(sources_b)),
-        out_specs=(pl.BlockSpec(memory_space=pltpu.HBM),) * PARTS + (smem,),
+        in_specs=[smem] + [anywhere] * count + [hbm] * len(begun),
+        out_specs=(hbm,) * PARTS + (smem,),
         scratch_shapes=[
-            pltpu.VMEM((sum(s.shape[0] for s in sources_a), two, half, width), dtype),
-            pltpu.VMEM((sum(s.shape[0] for s in sources_b), two, half, width), dtype),
-            pltpu.VMEM((row_count, length, width), dtype),
-            pltpu.SemaphoreType.DMA((len(sources_a),)),
-            pltpu.SemaphoreType.DMA((len(sources_b),)),
+            pltpu.VMEM((sum(s.shape[0] for s in sources), two, half, width), dtype),
+            pltpu.VMEM((row_count, half, width), dtype),
+            pltpu.SemaphoreType.DMA((count,)),
             pltpu.SemaphoreType.DMA((PARTS,)),
         ],
+        input_output_aliases={1 + count + k: k for k in range(len(begun))},
         compiler_params=pltpu.CompilerParams(vmem_limit_bytes=40 << 20),
         name="land",
         interpret=INTERPRET,
-    )(table, *sources_a, *sources_b)
+    )(table, *sources, *begun)
 
 
 def chain(forward, backward, caps, step, ring):
@@ -839,20 +876,17 @@
     z_caps, x_caps, x_stay = route
     z_sizes = (z_caps[0], z_caps[0], Z_STAY)
     x_sizes = (x_caps[0], x_caps[0], x_stay)
-    z_plus, z_minus, z_still, x_plus, x_minus, x_still = leave(table, own, partner, route)
+    z_plus, z_minus, z_still = leave(0, table, own, partner, z_sizes)
+    x_plus, x_minus, x_still = leave(1, table, own, partner, x_sizes)
     along_x = chain(x_plus, x_minus, x_caps, 2 * RING_Z, RING_X)
     along_z = chain(z_plus, z_minus, z_caps, 2, RING_Z)
     later = turn_over(table, 3, along_x + [x_still], z_sizes)
     last_b = chain(later[0], later[1], z_caps, 2, RING_Z)
     turned = turn_over(table, 2, along_z + [z_still], x_sizes)
     last_a = chain(turned[0], turned[1], x_caps, 2 * RING_Z, RING_X)
-    return land(
-        table,
-        last_a + [turned[2]],
-        last_b + [later[2]],
-        own.shape[0] * own.shape[1],
-        own.shape[2],
-    )
+    row_count, length = own.shape[0] * own.shape[1], own.shape[2]
+    *begun, _ = land(0, table, last_a + [turned[2]], row_count, length, ())
+    return land(1, table, last_b + [later[2]], row_count, length, begun)
 
 
 def dense(targets, everywhere, own):
@@ -932,15 +966,13 @@
         meta, tied, shifted(tied_low, "depth", 1, False), shifted(tied_low, "depth", -1, False)
     )
     neighbours = [shifted(up, "depth", 2, False), shifted(down, "depth", -2, False)]
-    attention = shifted(middle(live, meta, tied, neighbours), "section", 1, True)
-    begun = ()
-    for index, rows in enumerate(earlier):
-        begun = (
-            back(
-                index, attention, rows, bundled, row_count, begun
-            ),
-        )
-    return begun[0].reshape(1, row_count, length, width)
+    attention = middle(live, meta, tied, neighbours)
+    attention = shifted(attention, "section", 1, True)
+    values = []
+    for rows in earlier:
+        values.append(values_of(rows, bundled, row_count))
+    handed = finish(attention, bundled, earlier, values)
+    return handed.reshape(1, row_count, length, width)
 
 
 def solution(mesh):

time: 175 us -> 174 us (level)
  local copies, waits for them, and re-layouts: 2.82 us -> 4.8 us
  waiting for transfers between devices: 54.3 us -> 52.5 us
    ppermute x12, waiting for transfers between devices: 29.5 us -> 39.8 us  [chain(): lax.ppermute(forward[:cap], 'depth', [(i, moved(i, 1)) for i in devices])]
    ppermute x12, waiting for transfers between devices: 7.99 us -> 0.18 us  [chain(): lax.ppermute(backward[:cap], 'depth', [(i, moved(i, -1)) for i in devices])]
    ppermute x12, starting transfers between devices: 35.1 us -> 30.4 us  [chain(): lax.ppermute(backward[:cap], 'depth', [(i, moved(i, -1)) for i in devices])]
    ppermute x8, waiting for transfers between devices: 8.26 us -> 4.02 us  [shifted(): return lax.ppermute(value, axis, route)]
    ppermute x12, starting transfers between devices: 2.95 us -> 6.32 us  [chain(): lax.ppermute(forward[:cap], 'depth', [(i, moved(i, 1)) for i in devices])]
    unnamed x24 -> x18, local copies, waits for them, and re-layouts: 1.86 us -> 3.83 us
    pallas_call x4 -> x7, Pallas kernels: 22.7 us -> 23.6 us  [the longest x2 7.74 us: land(): pl.pallas_call(functools.partial(land_kernel, part, count), out_shape=(ja...]
  transfers between devices with their start and end apart: 34 -> 34, of which waited for: 16 -> 14; matrix products, arithmetic and copies ran while one was open for 1% -> 1% of each run, Pallas kernels for 19% -> 19%
where the time goes in v1:
time: 174 us; the launch traced here: 173 us
  starting transfers between devices  69.3 us (40%)
  waiting for transfers between devices  52.5 us (30%)
  Pallas kernels  44.6 us (26%)
  local copies, waits for them, and re-layouts  4.8 us (3%)
    ppermute x12, waiting for transfers between devices, chain(): lax.ppermute(forward[:cap], 'depth', [(i, moved(i, 1)) for i in devices])  39.8 us
    ppermute x12, starting transfers between devices, chain(): lax.ppermute(backward[:cap], 'depth', [(i, moved(i, -1)) for i in devices])  30.4 us
    ppermute x8, starting transfers between devices, shifted(): return lax.ppermute(value, axis, route)  20.4 us
    all_to_all x1, starting transfers between devices, layer(): lax.all_to_all(jnp.broadcast_to(targets[None, None], (peers, 1, row_count...  12.1 us
    all_to_all x1, waiting for transfers between devices, layer(): lax.all_to_all(jnp.broadcast_to(targets[None, None], (peers, 1, row_count...  8.54 us
    pallas_call x2, Pallas kernels, land(): pl.pallas_call(functools.partial(land_kernel, part, count), out_shape=(ja...  7.74 us
    pallas_call x1, Pallas kernels, finish(): pl.pallas_call(finish_kernel, out_shape=jax.ShapeDtypeStruct((tokens * PA...  7.18 us
    pallas_call x1, Pallas kernels, front(): pl.pallas_call(front_kernel, out_shape=(jax.ShapeDtypeStruct((quarter, 4...  6.64 us
  transfers between devices with their start and end apart: 34, of which 14 were waited for; matrix products, arithmetic and copies ran while one was open for 1% of the time, Pallas kernels for 19%

profile of v1, /device:TPU:2, one launch (start us, length us, event | category | flops | bytes accessed | tf_op | source)
XLA Modules:
  0.0 172.7 jit_solution(11904529124421559559)
XLA Ops:
  0.0 3.8 %bundle.1 = bf16[1552,768]{1,0:T(8,128)(2,1)} custom-call(bf16[768,2304]{1,0:T(8,128)(2,1)} %bitcast.13, bf16[768,768]{1,0:T(8,128)(2,1)} %bitcast.19, f32[1,768]{1,0:T(1,128)} %gain_ref.3, f32[1,768]{1,0:T(1,128)} %bias_ref.3), custom_call_target="tpu_custom_call" | custom-call | tf_op jit(solution)/shard_map/bundle/pallas_call | solution.py:696
  6.1 12.1 %all-to-all-start.1 = ((s32[64,1,32]{2,1,0:T(1,128)}), s32[64,1,32]{2,1,0:T(1,128)S(1)}, u32[]{:S(2)}, u32[]{:S(2)}) async-start(s32[64,1,32]{2,1,0:T(1,128)} %broadcast_in_dim.27), calls=%async_computation.1 | async-start | bytes 65536 | tf_op jit(solution)/shard_map/all_to_all | solution.py:937
  18.2 8.5 %all-to-all-done.1 = s32[64,1,32]{2,1,0:T(1,128)S(1)} async-done(((s32[64,1,32]{2,1,0:T(1,128)}), s32[64,1,32]{2,1,0:T(1,128)S(1)}, u32[]{:S(2)}, u32[]{:S(2)}) %all-to-all-start.1) | async-done | bytes 8224 | tf_op jit(solution)/shard_map/all_to_all | solution.py:937
  29.8 94.6 %conditional.1 = ((bf16[16,32,768]{2,1,0:T(8,128)(2,1)}, bf16[16,32,768]{2,1,0:T(8,128)(2,1)}, s32[32]{0:T(128)S(1)})) conditional(s32[]{:T(128)} %bitcast.7, (s32[64,32]{1,0:T(8,128)S(1)}, s32[32]{0:T(128)S(1)}, bf16[1,32,32,768]{3,2,1,0:T(8,128)(2,1)}) %tuple.21, (s32[8,128]{1,0:T(8,128)S(1)}, bf16[16,2,32,768]{3,2,1,0:T(8,128)(2,1)}, ...), branch_computations={%region_0.2_spmd, %region_2.3_spmd} | conditional | flops 212035 | bytes 51119076 | solution.py:948
  32.9 2.6 %collective-permute-start.16 = (bf16[11,2,16,768]{3,2,1,0:T(8,128)(2,1)S(1)}, bf16[11,2,16,768]{3,2,1,0:T(8,128)(2,1)S(1)}, u32[]{:S(2)}, u32[]{:S(2)}) collective-permute-start(bf16[11,2,16,768]{3,2,1,0:T(8,128)(2,1)S(1)} %get-tuple-element.32), channel_id=1, source_target_pairs={{0,14},{1,15},{2,0},{3,1},{4,2},{5,3},{6,4},{7,5},{8,6},{9,7},{10,... | collective-permute-start | bytes 1622024 | tf_op jit(solution)/shard_map/cond/branch_1_fun/ppermute | solution.py:869
  39.8 10.4 %collective-permute-done.refs_0_ = bf16[10,2,16,768]{3,2,1,0:T(8,128)(2,1)S(1)} collective-permute-done((bf16[10,2,16,768]{3,2,1,0:T(8,128)(2,1)S(1)}, bf16[10,2,16,768]{3,2,1,0:T(8,128)(2,1)S(1)}, u32[]{:S(2)}, u32[]{:S(2)}) %collective-permute-start) | collective-permute-done | bytes 491552 | tf_op jit(solution)/shard_map/cond/branch_1_fun/ppermute | solution.py:868
  53.1 3.3 %collective-permute-start.17 = (bf16[9,2,16,768]{3,2,1,0:T(8,128)(2,1)S(1)}, bf16[9,2,16,768]{3,2,1,0:T(8,128)(2,1)S(1)}, u32[]{:S(2)}, u32[]{:S(2)}) collective-permute-start(bf16[9,2,16,768]{3,2,1,0:T(8,128)(2,1)S(1)} %slice.59), channel_id=1, source_target_pairs={{0,14},{1,15},{2,0},{3,1},{4,2},{5,3},{6,4},{7,5},{8,6},{9,7},{10,... | collective-permute-start | bytes 1327112 | tf_op jit(solution)/shard_map/cond/branch_1_fun/ppermute | solution.py:869
  61.9 5.0 %collective-permute-done.13.refs_1_ = bf16[9,2,16,768]{3,2,1,0:T(8,128)(2,1)S(1)} collective-permute-done((bf16[9,2,16,768]{3,2,1,0:T(8,128)(2,1)S(1)}, bf16[9,2,16,768]{3,2,1,0:T(8,128)(2,1)S(1)}, u32[]{:S(2)}, u32[]{:S(2)}) %collective-permute-start.13) | collective-permute-done | bytes 442400 | tf_op jit(solution)/shard_map/cond/branch_1_fun/ppermute | solution.py:868
  67.0 3.7 %collective-permute-start.18 = (bf16[6,2,16,768]{3,2,1,0:T(8,128)(2,1)S(1)}, bf16[6,2,16,768]{3,2,1,0:T(8,128)(2,1)S(1)}, u32[]{:S(2)}, u32[]{:S(2)}) collective-permute-start(bf16[6,2,16,768]{3,2,1,0:T(8,128)(2,1)S(1)} %slice.60), channel_id=1, source_target_pairs={{0,14},{1,15},{2,0},{3,1},{4,2},{5,3},{6,4},{7,5},{8,6},{9,7},{10,... | collective-permute-start | bytes 884744 | tf_op jit(solution)/shard_map/cond/branch_1_fun/ppermute | solution.py:869
  70.7 11.6 %collective-permute-done.14.refs_2_ = bf16[6,2,16,768]{3,2,1,0:T(8,128)(2,1)S(1)} collective-permute-done((bf16[6,2,16,768]{3,2,1,0:T(8,128)(2,1)S(1)}, bf16[6,2,16,768]{3,2,1,0:T(8,128)(2,1)S(1)}, u32[]{:S(2)}, u32[]{:S(2)}) %collective-permute-start.14) | collective-permute-done | bytes 294944 | tf_op jit(solution)/shard_map/cond/branch_1_fun/ppermute | solution.py:868
  82.5 3.3 %collective-permute-start.19 = (bf16[4,2,16,768]{3,2,1,0:T(8,128)(2,1)S(1)}, bf16[4,2,16,768]{3,2,1,0:T(8,128)(2,1)S(1)}, u32[]{:S(2)}, u32[]{:S(2)}) collective-permute-start(bf16[4,2,16,768]{3,2,1,0:T(8,128)(2,1)S(1)} %slice.61), channel_id=1, source_target_pairs={{0,14},{1,15},{2,0},{3,1},{4,2},{5,3},{6,4},{7,5},{8,6},{9,7},{10,... | collective-permute-start | bytes 589832 | tf_op jit(solution)/shard_map/cond/branch_1_fun/ppermute | solution.py:869
  88.1 3.4 %collective-permute-done.15.refs_3_ = bf16[4,2,16,768]{3,2,1,0:T(8,128)(2,1)S(1)} collective-permute-done((bf16[4,2,16,768]{3,2,1,0:T(8,128)(2,1)S(1)}, bf16[4,2,16,768]{3,2,1,0:T(8,128)(2,1)S(1)}, u32[]{:S(2)}, u32[]{:S(2)}) %collective-permute-start.15) | collective-permute-done | bytes 196640 | tf_op jit(solution)/shard_map/cond/branch_1_fun/ppermute | solution.py:868
  94.1 3.0 %collective-permute-start.22 = (bf16[10,2,16,768]{3,2,1,0:T(8,128)(2,1)S(1)}, bf16[10,2,16,768]{3,2,1,0:T(8,128)(2,1)S(1)}, u32[]{:S(2)}, u32[]{:S(2)}) collective-permute-start(bf16[10,2,16,768]{3,2,1,0:T(8,128)(2,1)S(1)} %get-tuple-element.35), channel_id=1, source_target_pairs={{0,48},{1,49},{2,50},{3,51},{4,52},{5,53},{6,54},{7,55},{8,56},{9,... | collective-permute-start | bytes 1474568 | tf_op jit(solution)/shard_map/cond/branch_1_fun/ppermute | solution.py:869
  97.3 3.6 %collective-permute-start.10 = (bf16[6,2,16,768]{3,2,1,0:T(8,128)(2,1)S(1)}, bf16[6,2,16,768]{3,2,1,0:T(8,128)(2,1)S(1)}, u32[]{:S(2)}, u32[]{:S(2)}) collective-permute-start(bf16[6,2,16,768]{3,2,1,0:T(8,128)(2,1)S(1)} %slice.54), channel_id=1, source_target_pairs={{0,14},{1,15},{2,0},{3,1},{4,2},{5,3},{6,4},{7,5},{8,6},{9,7},{10,... | collective-permute-start | bytes 884744 | tf_op jit(solution)/shard_map/cond/branch_1_fun/ppermute | solution.py:869
  100.9 5.4 %collective-permute-done.20.refs_0_ = bf16[10,2,16,768]{3,2,1,0:T(8,128)(2,1)S(1)} collective-permute-done((bf16[10,2,16,768]{3,2,1,0:T(8,128)(2,1)S(1)}, bf16[10,2,16,768]{3,2,1,0:T(8,128)(2,1)S(1)}, u32[]{:S(2)}, u32[]{:S(2)}) %collective-permute-start.20) | collective-permute-done | bytes 491552 | tf_op jit(solution)/shard_map/cond/branch_1_fun/ppermute | solution.py:868
  106.5 3.5 %collective-permute-start.23 = (bf16[5,2,16,768]{3,2,1,0:T(8,128)(2,1)S(1)}, bf16[5,2,16,768]{3,2,1,0:T(8,128)(2,1)S(1)}, u32[]{:S(2)}, u32[]{:S(2)}) collective-permute-start(bf16[5,2,16,768]{3,2,1,0:T(8,128)(2,1)S(1)} %slice.63), channel_id=1, source_target_pairs={{0,48},{1,49},{2,50},{3,51},{4,52},{5,53},{6,54},{7,55},{8,56},{9,... | collective-permute-start | bytes 737288 | tf_op jit(solution)/shard_map/cond/branch_1_fun/ppermute | solution.py:869
  109.9 3.4 %collective-permute-start.11 = (bf16[4,2,16,768]{3,2,1,0:T(8,128)(2,1)S(1)}, bf16[4,2,16,768]{3,2,1,0:T(8,128)(2,1)S(1)}, u32[]{:S(2)}, u32[]{:S(2)}) collective-permute-start(bf16[4,2,16,768]{3,2,1,0:T(8,128)(2,1)S(1)} %slice.55), channel_id=1, source_target_pairs={{0,14},{1,15},{2,0},{3,1},{4,2},{5,3},{6,4},{7,5},{8,6},{9,7},{10,... | collective-permute-start | bytes 589832 | tf_op jit(solution)/shard_map/cond/branch_1_fun/ppermute | solution.py:869
  114.0 3.8 %land.2 = (bf16[16,32,768]{2,1,0:T(8,128)(2,1)}, bf16[16,32,768]{2,1,0:T(8,128)(2,1)}, s32[32]{0:T(128)}) custom-call(s32[8,128]{1,0:T(8,128)S(1)} %get-tuple-element.22.table_ref, bf16[10,2,16,768]{3,2,1,0:T(8,128)(2,1)S(1)} %collective-permute-done.20.refs_0_, bf16[5,2,16,768]{3,2,1,0:T(8,128)(2,1)S(1)} %collective-permute-done.21.refs_1_, ...), custom_call_target="tpu_custom_call" | custom-call | tf_op jit(solution)/shard_map/cond/branch_1_fun/land/pallas_call | solution.py:842
  117.8 2.5 %collective-permute-done.7.refs_3_ = bf16[4,2,16,768]{3,2,1,0:T(8,128)(2,1)S(1)} collective-permute-done((bf16[4,2,16,768]{3,2,1,0:T(8,128)(2,1)S(1)}, bf16[4,2,16,768]{3,2,1,0:T(8,128)(2,1)S(1)}, u32[]{:S(2)}, u32[]{:S(2)}) %collective-permute-start.7) | collective-permute-done | bytes 196640 | tf_op jit(solution)/shard_map/cond/branch_1_fun/ppermute | solution.py:868
  120.3 3.9 %land.3 = (bf16[16,32,768]{2,1,0:T(8,128)(2,1)}, bf16[16,32,768]{2,1,0:T(8,128)(2,1)}, s32[32]{0:T(128)S(1)}) custom-call(s32[8,128]{1,0:T(8,128)S(1)} %get-tuple-element.22.table_ref, bf16[11,2,16,768]{3,2,1,0:T(8,128)(2,1)S(1)} %collective-permute-done.4.refs_0_, ...), custom_call_target="tpu_custom_call", output_to_operand_aliasing={{0}: (10, {}), {1}: (11, {})} | custom-call | tf_op jit(solution)/shard_map/cond/branch_1_fun/land/pallas_call | solution.py:842
  129.4 6.6 %front.1 = (f32[96,128]{1,0:T(8,128)S(1)}, bf16[96,128]{1,0:T(8,128)(2,1)S(1)}) custom-call(s32[32]{0:T(128)S(1)} %get-tuple-element.52.live_ref, bf16[512,768]{1,0:T(8,128)(2,1)} %bitcast.8.rows_0_ref, bf16[512,768]{1,0:T(8,128)(2,1)} %bitcast.9.rows_1_ref, f32[1,768]{1,0:T(1,128)S(1)} %copy-done.2, f32[1,768]{1,0:T(1,128)S(1)} %copy-done.3, ...), custom_call_target="tpu_custom_call" | custom-call | tf_op jit(solution)/shard_map/front/pallas_call | solution.py:210
  138.6 5.8 %collective-permute-start.26 = (bf16[96,128]{1,0:T(8,128)(2,1)S(1)}, bf16[96,128]{1,0:T(8,128)(2,1)S(1)}, u32[]{:S(2)}, u32[]{:S(2)}) collective-permute-start(bf16[96,128]{1,0:T(8,128)(2,1)S(1)} %get-tuple-element.57), channel_id=1, source_target_pairs={{1,0},{2,1},{3,2},{4,3},{5,4},{6,5},{7,6},{8,7},{9,8},{10,9},{11,1... | collective-permute-start | bytes 73736 | tf_op jit(solution)/shard_map/ppermute | solution.py:438
  149.8 6.0 %collective-permute-start.28 = (bf16[96,128]{1,0:T(8,128)(2,1)}, bf16[96,128]{1,0:T(8,128)(2,1)S(1)}, u32[]{:S(2)}, u32[]{:S(2)}) collective-permute-start(bf16[96,128]{1,0:T(8,128)(2,1)} %get-tuple-element.60), channel_id=1, source_target_pairs={{2,0},{3,1},{4,2},{5,3},{6,4},{7,5},{8,6},{9,7},{10,8},{11,9},{12,... | collective-permute-start | bytes 73736 | tf_op jit(solution)/shard_map/ppermute | solution.py:438
  165.3 7.2 %finish.1 = bf16[1024,768]{1,0:T(8,128)(2,1)} custom-call(bf16[112,128]{1,0:T(8,128)(2,1)S(1)} %collective-permute-done.29.attention_ref, bf16[1552,768]{1,0:T(8,128)(2,1)S(1)} %collective-permute-done.30.bundle_ref, bf16[512,768]{1,0:T(8,128)(2,1)S(1)} %collective-permute-done.31.rows_ref.refs_0_, ...), custom_call_target="tpu_custom_call" | custom-call | tf_op jit(solution)/shard_map/finish/pallas_call | solution.py:413
  (96 shorter events, 48.8 us)
Async XLA Ops:
  3.8 156.5 %collective-permute-start.30 = (bf16[1552,768]{1,0:T(8,128)(2,1)}, bf16[1552,768]{1,0:T(8,128)(2,1)S(1)}, u32[]{:S(2)}, u32[]{:S(2)}) collective-permute-start(bf16[1552,768]{1,0:T(8,128)(2,1)} %bundle.1), channel_id=1, source_target_pairs={{0,64},{64,128},{128,192},{192,0},{1,65},{65,129},{129,193},{193,1... | collective-permute-start | bytes 7151624 | tf_op jit(solution)/shard_map/ppermute | solution.py:438
  5.4 21.3 %collective-permute-start.24 = (bf16[16,2,32,768]{3,2,1,0:T(8,128)(2,1)}, bf16[16,2,32,768]{3,2,1,0:T(8,128)(2,1)}, u32[]{:S(2)}, u32[]{:S(2)}) collective-permute-start(bf16[16,2,32,768]{3,2,1,0:T(8,128)(2,1)} %bitcast.16), channel_id=1, source_target_pairs={{0,1},{1,0},{2,3},{3,2},{4,5},{5,4},{6,7},{7,6},{8,9},{9,8},{10,11... | collective-permute-start | bytes 4718600 | tf_op jit(solution)/shard_map/ppermute | solution.py:944
  6.1 20.7 %all-to-all-start.1 = ((s32[64,1,32]{2,1,0:T(1,128)}), s32[64,1,32]{2,1,0:T(1,128)S(1)}, u32[]{:S(2)}, u32[]{:S(2)}) async-start(s32[64,1,32]{2,1,0:T(1,128)} %broadcast_in_dim.27), calls=%async_computation.1 | async-start | bytes 65536 | tf_op jit(solution)/shard_map/all_to_all | solution.py:937
  32.2 20.8 %collective-permute-start.12 = (bf16[11,2,16,768]{3,2,1,0:T(8,128)(2,1)S(1)}, bf16[11,2,16,768]{3,2,1,0:T(8,128)(2,1)S(1)}, u32[]{:S(2)}, u32[]{:S(2)}) collective-permute-start(bf16[11,2,16,768]{3,2,1,0:T(8,128)(2,1)S(1)} %get-tuple-element.31), channel_id=1, source_target_pairs={{0,2},{1,3},{2,4},{3,5},{4,6},{5,7},{6,8},{7,9},{8,10},{9,11},{10,... | collective-permute-start | bytes 1622024 | tf_op jit(solution)/shard_map/cond/branch_1_fun/ppermute | solution.py:868
  32.9 20.2 %collective-permute-start.16 = (bf16[11,2,16,768]{3,2,1,0:T(8,128)(2,1)S(1)}, bf16[11,2,16,768]{3,2,1,0:T(8,128)(2,1)S(1)}, u32[]{:S(2)}, u32[]{:S(2)}) collective-permute-start(bf16[11,2,16,768]{3,2,1,0:T(8,128)(2,1)S(1)} %get-tuple-element.32), channel_id=1, source_target_pairs={{0,14},{1,15},{2,0},{3,1},{4,2},{5,3},{6,4},{7,5},{8,6},{9,7},{10,... | collective-permute-start | bytes 1622024 | tf_op jit(solution)/shard_map/cond/branch_1_fun/ppermute | solution.py:869
  37.7 12.5 %collective-permute-start = (bf16[10,2,16,768]{3,2,1,0:T(8,128)(2,1)S(1)}, bf16[10,2,16,768]{3,2,1,0:T(8,128)(2,1)S(1)}, u32[]{:S(2)}, u32[]{:S(2)}) collective-permute-start(bf16[10,2,16,768]{3,2,1,0:T(8,128)(2,1)S(1)} %get-tuple-element.25), channel_id=1, source_target_pairs={{0,16},{1,17},{2,18},{3,19},{4,20},{5,21},{6,22},{7,23},{8,24},{9,... | collective-permute-start | bytes 1474568 | tf_op jit(solution)/shard_map/cond/branch_1_fun/ppermute | solution.py:868
  38.4 12.5 %collective-permute-start.2 = (bf16[10,2,16,768]{3,2,1,0:T(8,128)(2,1)S(1)}, bf16[10,2,16,768]{3,2,1,0:T(8,128)(2,1)S(1)}, u32[]{:S(2)}, u32[]{:S(2)}) collective-permute-start(bf16[10,2,16,768]{3,2,1,0:T(8,128)(2,1)S(1)} %get-tuple-element.26), channel_id=1, source_target_pairs={{0,48},{1,49},{2,50},{3,51},{4,52},{5,53},{6,54},{7,55},{8,56},{9,... | collective-permute-start | bytes 1474568 | tf_op jit(solution)/shard_map/cond/branch_1_fun/ppermute | solution.py:869
  53.0 13.9 %collective-permute-start.13 = (bf16[9,2,16,768]{3,2,1,0:T(8,128)(2,1)S(1)}, bf16[9,2,16,768]{3,2,1,0:T(8,128)(2,1)S(1)}, u32[]{:S(2)}, u32[]{:S(2)}) collective-permute-start(bf16[9,2,16,768]{3,2,1,0:T(8,128)(2,1)S(1)} %slice.56), channel_id=1, source_target_pairs={{0,2},{1,3},{2,4},{3,5},{4,6},{5,7},{6,8},{7,9},{8,10},{9,11},{10,... | collective-permute-start | bytes 1327112 | tf_op jit(solution)/shard_map/cond/branch_1_fun/ppermute | solution.py:868
  53.1 13.9 %collective-permute-start.17 = (bf16[9,2,16,768]{3,2,1,0:T(8,128)(2,1)S(1)}, bf16[9,2,16,768]{3,2,1,0:T(8,128)(2,1)S(1)}, u32[]{:S(2)}, u32[]{:S(2)}) collective-permute-start(bf16[9,2,16,768]{3,2,1,0:T(8,128)(2,1)S(1)} %slice.59), channel_id=1, source_target_pairs={{0,14},{1,15},{2,0},{3,1},{4,2},{5,3},{6,4},{7,5},{8,6},{9,7},{10,... | collective-permute-start | bytes 1327112 | tf_op jit(solution)/shard_map/cond/branch_1_fun/ppermute | solution.py:869
  59.8 26.0 %collective-permute-start.8 = (bf16[11,2,16,768]{3,2,1,0:T(8,128)(2,1)S(1)}, bf16[11,2,16,768]{3,2,1,0:T(8,128)(2,1)S(1)}, u32[]{:S(2)}, u32[]{:S(2)}) collective-permute-start(bf16[11,2,16,768]{3,2,1,0:T(8,128)(2,1)S(1)} %get-tuple-element.29), channel_id=1, source_target_pairs={{0,14},{1,15},{2,0},{3,1},{4,2},{5,3},{6,4},{7,5},{8,6},{9,7},{10,... | collective-permute-start | bytes 1622024 | tf_op jit(solution)/shard_map/cond/branch_1_fun/ppermute | solution.py:869
  60.4 25.5 %collective-permute-start.4 = (bf16[11,2,16,768]{3,2,1,0:T(8,128)(2,1)S(1)}, bf16[11,2,16,768]{3,2,1,0:T(8,128)(2,1)S(1)}, u32[]{:S(2)}, u32[]{:S(2)}) collective-permute-start(bf16[11,2,16,768]{3,2,1,0:T(8,128)(2,1)S(1)} %get-tuple-element.28), channel_id=1, source_target_pairs={{0,2},{1,3},{2,4},{3,5},{4,6},{5,7},{6,8},{7,9},{8,10},{9,11},{10,... | collective-permute-start | bytes 1622024 | tf_op jit(solution)/shard_map/cond/branch_1_fun/ppermute | solution.py:868
  66.9 15.5 %collective-permute-start.14 = (bf16[6,2,16,768]{3,2,1,0:T(8,128)(2,1)S(1)}, bf16[6,2,16,768]{3,2,1,0:T(8,128)(2,1)S(1)}, u32[]{:S(2)}, u32[]{:S(2)}) collective-permute-start(bf16[6,2,16,768]{3,2,1,0:T(8,128)(2,1)S(1)} %slice.57), channel_id=1, source_target_pairs={{0,2},{1,3},{2,4},{3,5},{4,6},{5,7},{6,8},{7,9},{8,10},{9,11},{10,... | collective-permute-start | bytes 884744 | tf_op jit(solution)/shard_map/cond/branch_1_fun/ppermute | solution.py:868
  67.0 15.4 %collective-permute-start.18 = (bf16[6,2,16,768]{3,2,1,0:T(8,128)(2,1)S(1)}, bf16[6,2,16,768]{3,2,1,0:T(8,128)(2,1)S(1)}, u32[]{:S(2)}, u32[]{:S(2)}) collective-permute-start(bf16[6,2,16,768]{3,2,1,0:T(8,128)(2,1)S(1)} %slice.60), channel_id=1, source_target_pairs={{0,14},{1,15},{2,0},{3,1},{4,2},{5,3},{6,4},{7,5},{8,6},{9,7},{10,... | collective-permute-start | bytes 884744 | tf_op jit(solution)/shard_map/cond/branch_1_fun/ppermute | solution.py:869
  82.4 9.1 %collective-permute-start.15 = (bf16[4,2,16,768]{3,2,1,0:T(8,128)(2,1)S(1)}, bf16[4,2,16,768]{3,2,1,0:T(8,128)(2,1)S(1)}, u32[]{:S(2)}, u32[]{:S(2)}) collective-permute-start(bf16[4,2,16,768]{3,2,1,0:T(8,128)(2,1)S(1)} %slice.58), channel_id=1, source_target_pairs={{0,2},{1,3},{2,4},{3,5},{4,6},{5,7},{6,8},{7,9},{8,10},{9,11},{10,... | collective-permute-start | bytes 589832 | tf_op jit(solution)/shard_map/cond/branch_1_fun/ppermute | solution.py:868
  82.5 8.9 %collective-permute-start.19 = (bf16[4,2,16,768]{3,2,1,0:T(8,128)(2,1)S(1)}, bf16[4,2,16,768]{3,2,1,0:T(8,128)(2,1)S(1)}, u32[]{:S(2)}, u32[]{:S(2)}) collective-permute-start(bf16[4,2,16,768]{3,2,1,0:T(8,128)(2,1)S(1)} %slice.61), channel_id=1, source_target_pairs={{0,14},{1,15},{2,0},{3,1},{4,2},{5,3},{6,4},{7,5},{8,6},{9,7},{10,... | collective-permute-start | bytes 589832 | tf_op jit(solution)/shard_map/cond/branch_1_fun/ppermute | solution.py:869
  85.9 11.4 %collective-permute-start.9 = (bf16[9,2,16,768]{3,2,1,0:T(8,128)(2,1)S(1)}, bf16[9,2,16,768]{3,2,1,0:T(8,128)(2,1)S(1)}, u32[]{:S(2)}, u32[]{:S(2)}) collective-permute-start(bf16[9,2,16,768]{3,2,1,0:T(8,128)(2,1)S(1)} %slice.53), channel_id=1, source_target_pairs={{0,14},{1,15},{2,0},{3,1},{4,2},{5,3},{6,4},{7,5},{8,6},{9,7},{10,... | collective-permute-start | bytes 1327112 | tf_op jit(solution)/shard_map/cond/branch_1_fun/ppermute | solution.py:869
  86.0 14.8 %collective-permute-start.5 = (bf16[9,2,16,768]{3,2,1,0:T(8,128)(2,1)S(1)}, bf16[9,2,16,768]{3,2,1,0:T(8,128)(2,1)S(1)}, u32[]{:S(2)}, u32[]{:S(2)}) collective-permute-start(bf16[9,2,16,768]{3,2,1,0:T(8,128)(2,1)S(1)} %slice.50), channel_id=1, source_target_pairs={{0,2},{1,3},{2,4},{3,5},{4,6},{5,7},{6,8},{7,9},{8,10},{9,11},{10,... | collective-permute-start | bytes 1327112 | tf_op jit(solution)/shard_map/cond/branch_1_fun/ppermute | solution.py:868
  94.0 12.3 %collective-permute-start.20 = (bf16[10,2,16,768]{3,2,1,0:T(8,128)(2,1)S(1)}, bf16[10,2,16,768]{3,2,1,0:T(8,128)(2,1)S(1)}, u32[]{:S(2)}, u32[]{:S(2)}) collective-permute-start(bf16[10,2,16,768]{3,2,1,0:T(8,128)(2,1)S(1)} %get-tuple-element.34), channel_id=1, source_target_pairs={{0,16},{1,17},{2,18},{3,19},{4,20},{5,21},{6,22},{7,23},{8,24},{9,... | collective-permute-start | bytes 1474568 | tf_op jit(solution)/shard_map/cond/branch_1_fun/ppermute | solution.py:868
  94.1 12.3 %collective-permute-start.22 = (bf16[10,2,16,768]{3,2,1,0:T(8,128)(2,1)S(1)}, bf16[10,2,16,768]{3,2,1,0:T(8,128)(2,1)S(1)}, u32[]{:S(2)}, u32[]{:S(2)}) collective-permute-start(bf16[10,2,16,768]{3,2,1,0:T(8,128)(2,1)S(1)} %get-tuple-element.35), channel_id=1, source_target_pairs={{0,48},{1,49},{2,50},{3,51},{4,52},{5,53},{6,54},{7,55},{8,56},{9,... | collective-permute-start | bytes 1474568 | tf_op jit(solution)/shard_map/cond/branch_1_fun/ppermute | solution.py:869
  97.3 12.6 %collective-permute-start.10 = (bf16[6,2,16,768]{3,2,1,0:T(8,128)(2,1)S(1)}, bf16[6,2,16,768]{3,2,1,0:T(8,128)(2,1)S(1)}, u32[]{:S(2)}, u32[]{:S(2)}) collective-permute-start(bf16[6,2,16,768]{3,2,1,0:T(8,128)(2,1)S(1)} %slice.54), channel_id=1, source_target_pairs={{0,14},{1,15},{2,0},{3,1},{4,2},{5,3},{6,4},{7,5},{8,6},{9,7},{10,... | collective-permute-start | bytes 884744 | tf_op jit(solution)/shard_map/cond/branch_1_fun/ppermute | solution.py:869
  100.9 12.5 %collective-permute-start.6 = (bf16[6,2,16,768]{3,2,1,0:T(8,128)(2,1)S(1)}, bf16[6,2,16,768]{3,2,1,0:T(8,128)(2,1)S(1)}, u32[]{:S(2)}, u32[]{:S(2)}) collective-permute-start(bf16[6,2,16,768]{3,2,1,0:T(8,128)(2,1)S(1)} %slice.51), channel_id=1, source_target_pairs={{0,2},{1,3},{2,4},{3,5},{4,6},{5,7},{6,8},{7,9},{8,10},{9,11},{10,... | collective-permute-start | bytes 884744 | tf_op jit(solution)/shard_map/cond/branch_1_fun/ppermute | solution.py:868
  124.5 35.8 %collective-permute-start.31 = (bf16[512,768]{1,0:T(8,128)(2,1)}, bf16[512,768]{1,0:T(8,128)(2,1)S(1)}, u32[]{:S(2)}, u32[]{:S(2)}) collective-permute-start(bf16[512,768]{1,0:T(8,128)(2,1)} %bitcast.8.rows_0_ref), channel_id=1, source_target_pairs={{0,64},{64,128},{128,192},{192,0},{1,65},{65,129},{129,193},{193,1... | collective-permute-start | bytes 2359304 | tf_op jit(solution)/shard_map/ppermute | solution.py:438
  126.1 36.0 %collective-permute-start.32 = (bf16[512,768]{1,0:T(8,128)(2,1)}, bf16[512,768]{1,0:T(8,128)(2,1)}, u32[]{:S(2)}, u32[]{:S(2)}) collective-permute-start(bf16[512,768]{1,0:T(8,128)(2,1)} %bitcast.9.rows_1_ref), channel_id=1, source_target_pairs={{0,64},{64,128},{128,192},{192,0},{1,65},{65,129},{129,193},{193,1... | collective-permute-start | bytes 2359304 | tf_op jit(solution)/shard_map/ppermute | solution.py:438
  147.9 8.0 %collective-permute-start.27 = (bf16[96,128]{1,0:T(8,128)(2,1)}, bf16[96,128]{1,0:T(8,128)(2,1)S(1)}, u32[]{:S(2)}, u32[]{:S(2)}) collective-permute-start(bf16[96,128]{1,0:T(8,128)(2,1)} %get-tuple-element.59), channel_id=1, source_target_pairs={{0,2},{1,3},{2,4},{3,5},{4,6},{5,7},{6,8},{7,9},{8,10},{9,11},{10,... | collective-permute-start | bytes 73736 | tf_op jit(solution)/shard_map/ppermute | solution.py:438
  (20 other events, 284.7 us)

commit v2 on v1

--- a/solution.py
+++ b/solution.py
@@ -136,8 +136,10 @@
     tied_ref,
     tied_low_ref,
     landed,
+    weight,
     acc,
     sem,
+    weight_sem,
 ):
     row_count = live_ref.shape[0]
     width = rows_0_ref.shape[1]
@@ -153,11 +155,13 @@
         )
         for c in range(chunks)
     ]
-    for copy in copies:
+    copies[0].start()
+    weights = pltpu.make_async_copy(weight_ref.at[:, pl.ds(0, 2 * width)], weight, weight_sem)
+    weights.start()
+    for copy in copies[1:]:
         copy.start()
     gain = gain_ref[...]
     bias = bias_ref[...]
-    weight = weight_ref[:, : 2 * width]
     first = lane_mask((length, 256))
     acc[...] = jnp.zeros_like(acc)
 
@@ -165,7 +169,14 @@
         pltpu.make_async_copy(rows_0_ref.at[pl.ds(0, span), :], landed.at[c], sem.at[c]).wait()
         start = c * CHUNK_ROWS
         normed = normalized(landed[c], gain, bias)
-        packed = jnp.dot(normed, weight, preferred_element_type=jnp.float32).astype(jnp.bfloat16)
+
+        @pl.when(c == 0)
+        def _():
+            weights.wait()
+
+        packed = jnp.dot(
+            normed, weight[...], preferred_element_type=jnp.float32
+        ).astype(jnp.bfloat16)
         for pair in range(PAIRS):
             lanes = slice(pair * 128, pair * 128 + 128)
             key_lanes = slice(width + pair * 128, width + pair * 128 + 128)
@@ -213,17 +224,21 @@
             jax.ShapeDtypeStruct((quarter, 4 * length), jnp.float32),
             jax.ShapeDtypeStruct((quarter, 4 * length), jnp.bfloat16),
         ),
-        in_specs=[smem] + [pl.BlockSpec(memory_space=pltpu.HBM)] * PARTS + [vmem, vmem, vmem],
+        in_specs=[smem]
+        + [pl.BlockSpec(memory_space=pltpu.HBM)] * PARTS
+        + [vmem, vmem, pl.BlockSpec(memory_space=pltpu.HBM)],
         out_specs=(vmem, vmem),
         scratch_shapes=[
             pltpu.VMEM((row_count // CHUNK_ROWS, CHUNK_ROWS * length, width), jnp.bfloat16),
+            pltpu.VMEM((width, 2 * width), jnp.bfloat16),
             pltpu.VMEM((H * length, length), jnp.float32),
             pltpu.SemaphoreType.DMA((row_count // CHUNK_ROWS,)),
+            pltpu.SemaphoreType.DMA,
         ],
         compiler_params=pltpu.CompilerParams(vmem_limit_bytes=40 << 20),
         name="front",
         interpret=INTERPRET,
-    )(live, *rows, gain, bias, weight)
+    )(live, *rows, gain, bias, pltpu.with_memory_space_constraint(weight, pltpu.HBM))
 
 
 def belongs(meta_ref, step):

time: 174 us -> 173 us (level)
  local copies, waits for them, and re-layouts: 4.8 us -> 2.8 us
    unnamed x18 -> x16, local copies, waits for them, and re-layouts: 3.83 us -> 1.83 us
  transfers between devices with their start and end apart: 34 -> 34, of which waited for: 14 -> 14; matrix products, arithmetic and copies ran while one was open for 1% -> 1% of each run, Pallas kernels for 19% -> 20%
where the time goes in v2:
time: 173 us; the launch traced here: 172 us
  starting transfers between devices  69.3 us (40%)
  waiting for transfers between devices  52.6 us (30%)
  Pallas kernels  45.6 us (26%)
  local copies, waits for them, and re-layouts  2.8 us (2%)
    ppermute x12, waiting for transfers between devices, chain(): lax.ppermute(forward[:cap], 'depth', [(i, moved(i, 1)) for i in devices])  39.8 us
    ppermute x12, starting transfers between devices, chain(): lax.ppermute(backward[:cap], 'depth', [(i, moved(i, -1)) for i in devices])  30.4 us
    ppermute x8, starting transfers between devices, shifted(): return lax.ppermute(value, axis, route)  20.4 us
    all_to_all x1, starting transfers between devices, layer(): lax.all_to_all(jnp.broadcast_to(targets[None, None], (peers, 1, row_count...  12.1 us
    all_to_all x1, waiting for transfers between devices, layer(): lax.all_to_all(jnp.broadcast_to(targets[None, None], (peers, 1, row_count...  8.54 us
    pallas_call x2, Pallas kernels, land(): pl.pallas_call(functools.partial(land_kernel, part, count), out_shape=(ja...  7.73 us
    pallas_call x1, Pallas kernels, front(): pl.pallas_call(front_kernel, out_shape=(jax.ShapeDtypeStruct((quarter, 4...  7.66 us
    pallas_call x1, Pallas kernels, finish(): pl.pallas_call(finish_kernel, out_shape=jax.ShapeDtypeStruct((tokens * PA...  7.18 us
  transfers between devices with their start and end apart: 34, of which 14 were waited for; matrix products, arithmetic and copies ran while one was open for 1% of the time, Pallas kernels for 20%

profile of v2, /device:TPU:2, one launch (start us, length us, event | category | flops | bytes accessed | tf_op | source)
XLA Modules:
  0.0 171.7 jit_solution(298946704367269130)
XLA Ops:
  0.0 3.8 %bundle.1 = bf16[1552,768]{1,0:T(8,128)(2,1)} custom-call(bf16[768,2304]{1,0:T(8,128)(2,1)} %bitcast.14, bf16[768,768]{1,0:T(8,128)(2,1)} %bitcast.19, f32[1,768]{1,0:T(1,128)} %gain_ref.3, f32[1,768]{1,0:T(1,128)} %bias_ref.3), custom_call_target="tpu_custom_call" | custom-call | tf_op jit(solution)/shard_map/bundle/pallas_call | solution.py:711
  6.1 12.1 %all-to-all-start.1 = ((s32[64,1,32]{2,1,0:T(1,128)}), s32[64,1,32]{2,1,0:T(1,128)S(1)}, u32[]{:S(2)}, u32[]{:S(2)}) async-start(s32[64,1,32]{2,1,0:T(1,128)} %broadcast_in_dim.27), calls=%async_computation.1 | async-start | bytes 65536 | tf_op jit(solution)/shard_map/all_to_all | solution.py:952
  18.2 8.5 %all-to-all-done.1 = s32[64,1,32]{2,1,0:T(1,128)S(1)} async-done(((s32[64,1,32]{2,1,0:T(1,128)}), s32[64,1,32]{2,1,0:T(1,128)S(1)}, u32[]{:S(2)}, u32[]{:S(2)}) %all-to-all-start.1) | async-done | bytes 8224 | tf_op jit(solution)/shard_map/all_to_all | solution.py:952
  29.8 94.7 %conditional.1 = ((bf16[16,32,768]{2,1,0:T(8,128)(2,1)}, bf16[16,32,768]{2,1,0:T(8,128)(2,1)}, s32[32]{0:T(128)S(1)})) conditional(s32[]{:T(128)} %bitcast.7, (s32[64,32]{1,0:T(8,128)S(1)}, s32[32]{0:T(128)S(1)}, bf16[1,32,32,768]{3,2,1,0:T(8,128)(2,1)}) %tuple.21, (s32[8,128]{1,0:T(8,128)S(1)}, bf16[16,2,32,768]{3,2,1,0:T(8,128)(2,1)}, ...), branch_computations={%region_0.2_spmd, %region_2.3_spmd} | conditional | flops 212035 | bytes 51119076 | solution.py:963
  32.9 2.6 %collective-permute-start.16 = (bf16[11,2,16,768]{3,2,1,0:T(8,128)(2,1)S(1)}, bf16[11,2,16,768]{3,2,1,0:T(8,128)(2,1)S(1)}, u32[]{:S(2)}, u32[]{:S(2)}) collective-permute-start(bf16[11,2,16,768]{3,2,1,0:T(8,128)(2,1)S(1)} %get-tuple-element.32), channel_id=1, source_target_pairs={{0,14},{1,15},{2,0},{3,1},{4,2},{5,3},{6,4},{7,5},{8,6},{9,7},{10,... | collective-permute-start | bytes 1622024 | tf_op jit(solution)/shard_map/cond/branch_1_fun/ppermute | solution.py:884
  39.8 10.4 %collective-permute-done.refs_0_ = bf16[10,2,16,768]{3,2,1,0:T(8,128)(2,1)S(1)} collective-permute-done((bf16[10,2,16,768]{3,2,1,0:T(8,128)(2,1)S(1)}, bf16[10,2,16,768]{3,2,1,0:T(8,128)(2,1)S(1)}, u32[]{:S(2)}, u32[]{:S(2)}) %collective-permute-start) | collective-permute-done | bytes 491552 | tf_op jit(solution)/shard_map/cond/branch_1_fun/ppermute | solution.py:883
  53.1 3.3 %collective-permute-start.17 = (bf16[9,2,16,768]{3,2,1,0:T(8,128)(2,1)S(1)}, bf16[9,2,16,768]{3,2,1,0:T(8,128)(2,1)S(1)}, u32[]{:S(2)}, u32[]{:S(2)}) collective-permute-start(bf16[9,2,16,768]{3,2,1,0:T(8,128)(2,1)S(1)} %slice.59), channel_id=1, source_target_pairs={{0,14},{1,15},{2,0},{3,1},{4,2},{5,3},{6,4},{7,5},{8,6},{9,7},{10,... | collective-permute-start | bytes 1327112 | tf_op jit(solution)/shard_map/cond/branch_1_fun/ppermute | solution.py:884
  61.9 5.0 %collective-permute-done.13.refs_1_ = bf16[9,2,16,768]{3,2,1,0:T(8,128)(2,1)S(1)} collective-permute-done((bf16[9,2,16,768]{3,2,1,0:T(8,128)(2,1)S(1)}, bf16[9,2,16,768]{3,2,1,0:T(8,128)(2,1)S(1)}, u32[]{:S(2)}, u32[]{:S(2)}) %collective-permute-start.13) | collective-permute-done | bytes 442400 | tf_op jit(solution)/shard_map/cond/branch_1_fun/ppermute | solution.py:883
  67.1 3.7 %collective-permute-start.18 = (bf16[6,2,16,768]{3,2,1,0:T(8,128)(2,1)S(1)}, bf16[6,2,16,768]{3,2,1,0:T(8,128)(2,1)S(1)}, u32[]{:S(2)}, u32[]{:S(2)}) collective-permute-start(bf16[6,2,16,768]{3,2,1,0:T(8,128)(2,1)S(1)} %slice.60), channel_id=1, source_target_pairs={{0,14},{1,15},{2,0},{3,1},{4,2},{5,3},{6,4},{7,5},{8,6},{9,7},{10,... | collective-permute-start | bytes 884744 | tf_op jit(solution)/shard_map/cond/branch_1_fun/ppermute | solution.py:884
  70.8 11.6 %collective-permute-done.14.refs_2_ = bf16[6,2,16,768]{3,2,1,0:T(8,128)(2,1)S(1)} collective-permute-done((bf16[6,2,16,768]{3,2,1,0:T(8,128)(2,1)S(1)}, bf16[6,2,16,768]{3,2,1,0:T(8,128)(2,1)S(1)}, u32[]{:S(2)}, u32[]{:S(2)}) %collective-permute-start.14) | collective-permute-done | bytes 294944 | tf_op jit(solution)/shard_map/cond/branch_1_fun/ppermute | solution.py:883
  82.5 3.3 %collective-permute-start.19 = (bf16[4,2,16,768]{3,2,1,0:T(8,128)(2,1)S(1)}, bf16[4,2,16,768]{3,2,1,0:T(8,128)(2,1)S(1)}, u32[]{:S(2)}, u32[]{:S(2)}) collective-permute-start(bf16[4,2,16,768]{3,2,1,0:T(8,128)(2,1)S(1)} %slice.61), channel_id=1, source_target_pairs={{0,14},{1,15},{2,0},{3,1},{4,2},{5,3},{6,4},{7,5},{8,6},{9,7},{10,... | collective-permute-start | bytes 589832 | tf_op jit(solution)/shard_map/cond/branch_1_fun/ppermute | solution.py:884
  88.1 3.4 %collective-permute-done.15.refs_3_ = bf16[4,2,16,768]{3,2,1,0:T(8,128)(2,1)S(1)} collective-permute-done((bf16[4,2,16,768]{3,2,1,0:T(8,128)(2,1)S(1)}, bf16[4,2,16,768]{3,2,1,0:T(8,128)(2,1)S(1)}, u32[]{:S(2)}, u32[]{:S(2)}) %collective-permute-start.15) | collective-permute-done | bytes 196640 | tf_op jit(solution)/shard_map/cond/branch_1_fun/ppermute | solution.py:883
  94.1 3.0 %collective-permute-start.22 = (bf16[10,2,16,768]{3,2,1,0:T(8,128)(2,1)S(1)}, bf16[10,2,16,768]{3,2,1,0:T(8,128)(2,1)S(1)}, u32[]{:S(2)}, u32[]{:S(2)}) collective-permute-start(bf16[10,2,16,768]{3,2,1,0:T(8,128)(2,1)S(1)} %get-tuple-element.35), channel_id=1, source_target_pairs={{0,48},{1,49},{2,50},{3,51},{4,52},{5,53},{6,54},{7,55},{8,56},{9,... | collective-permute-start | bytes 1474568 | tf_op jit(solution)/shard_map/cond/branch_1_fun/ppermute | solution.py:884
  97.3 3.6 %collective-permute-start.10 = (bf16[6,2,16,768]{3,2,1,0:T(8,128)(2,1)S(1)}, bf16[6,2,16,768]{3,2,1,0:T(8,128)(2,1)S(1)}, u32[]{:S(2)}, u32[]{:S(2)}) collective-permute-start(bf16[6,2,16,768]{3,2,1,0:T(8,128)(2,1)S(1)} %slice.54), channel_id=1, source_target_pairs={{0,14},{1,15},{2,0},{3,1},{4,2},{5,3},{6,4},{7,5},{8,6},{9,7},{10,... | collective-permute-start | bytes 884744 | tf_op jit(solution)/shard_map/cond/branch_1_fun/ppermute | solution.py:884
  101.0 5.4 %collective-permute-done.20.refs_0_ = bf16[10,2,16,768]{3,2,1,0:T(8,128)(2,1)S(1)} collective-permute-done((bf16[10,2,16,768]{3,2,1,0:T(8,128)(2,1)S(1)}, bf16[10,2,16,768]{3,2,1,0:T(8,128)(2,1)S(1)}, u32[]{:S(2)}, u32[]{:S(2)}) %collective-permute-start.20) | collective-permute-done | bytes 491552 | tf_op jit(solution)/shard_map/cond/branch_1_fun/ppermute | solution.py:883
  106.5 3.5 %collective-permute-start.23 = (bf16[5,2,16,768]{3,2,1,0:T(8,128)(2,1)S(1)}, bf16[5,2,16,768]{3,2,1,0:T(8,128)(2,1)S(1)}, u32[]{:S(2)}, u32[]{:S(2)}) collective-permute-start(bf16[5,2,16,768]{3,2,1,0:T(8,128)(2,1)S(1)} %slice.63), channel_id=1, source_target_pairs={{0,48},{1,49},{2,50},{3,51},{4,52},{5,53},{6,54},{7,55},{8,56},{9,... | collective-permute-start | bytes 737288 | tf_op jit(solution)/shard_map/cond/branch_1_fun/ppermute | solution.py:884
  109.9 3.4 %collective-permute-start.11 = (bf16[4,2,16,768]{3,2,1,0:T(8,128)(2,1)S(1)}, bf16[4,2,16,768]{3,2,1,0:T(8,128)(2,1)S(1)}, u32[]{:S(2)}, u32[]{:S(2)}) collective-permute-start(bf16[4,2,16,768]{3,2,1,0:T(8,128)(2,1)S(1)} %slice.55), channel_id=1, source_target_pairs={{0,14},{1,15},{2,0},{3,1},{4,2},{5,3},{6,4},{7,5},{8,6},{9,7},{10,... | collective-permute-start | bytes 589832 | tf_op jit(solution)/shard_map/cond/branch_1_fun/ppermute | solution.py:884
  114.0 3.8 %land.2 = (bf16[16,32,768]{2,1,0:T(8,128)(2,1)}, bf16[16,32,768]{2,1,0:T(8,128)(2,1)}, s32[32]{0:T(128)}) custom-call(s32[8,128]{1,0:T(8,128)S(1)} %get-tuple-element.22.table_ref, bf16[10,2,16,768]{3,2,1,0:T(8,128)(2,1)S(1)} %collective-permute-done.20.refs_0_, bf16[5,2,16,768]{3,2,1,0:T(8,128)(2,1)S(1)} %collective-permute-done.21.refs_1_, ...), custom_call_target="tpu_custom_call" | custom-call | tf_op jit(solution)/shard_map/cond/branch_1_fun/land/pallas_call | solution.py:857
  117.8 2.6 %collective-permute-done.7.refs_3_ = bf16[4,2,16,768]{3,2,1,0:T(8,128)(2,1)S(1)} collective-permute-done((bf16[4,2,16,768]{3,2,1,0:T(8,128)(2,1)S(1)}, bf16[4,2,16,768]{3,2,1,0:T(8,128)(2,1)S(1)}, u32[]{:S(2)}, u32[]{:S(2)}) %collective-permute-start.7) | collective-permute-done | bytes 196640 | tf_op jit(solution)/shard_map/cond/branch_1_fun/ppermute | solution.py:883
  120.3 4.0 %land.3 = (bf16[16,32,768]{2,1,0:T(8,128)(2,1)}, bf16[16,32,768]{2,1,0:T(8,128)(2,1)}, s32[32]{0:T(128)S(1)}) custom-call(s32[8,128]{1,0:T(8,128)S(1)} %get-tuple-element.22.table_ref, bf16[11,2,16,768]{3,2,1,0:T(8,128)(2,1)S(1)} %collective-permute-done.4.refs_0_, ...), custom_call_target="tpu_custom_call", output_to_operand_aliasing={{0}: (10, {}), {1}: (11, {})} | custom-call | tf_op jit(solution)/shard_map/cond/branch_1_fun/land/pallas_call | solution.py:857
  127.4 7.7 %front.1 = (f32[96,128]{1,0:T(8,128)S(1)}, bf16[96,128]{1,0:T(8,128)(2,1)S(1)}) custom-call(s32[32]{0:T(128)S(1)} %get-tuple-element.52.live_ref, bf16[512,768]{1,0:T(8,128)(2,1)} %bitcast.8.rows_0_ref, bf16[512,768]{1,0:T(8,128)(2,1)} %bitcast.9.rows_1_ref, f32[1,768]{1,0:T(1,128)S(1)} %copy-done.1, f32[1,768]{1,0:T(1,128)S(1)} %copy-done.2, ...), custom_call_target="tpu_custom_call" | custom-call | tf_op jit(solution)/shard_map/front/pallas_call | solution.py:221
  137.6 5.8 %collective-permute-start.26 = (bf16[96,128]{1,0:T(8,128)(2,1)S(1)}, bf16[96,128]{1,0:T(8,128)(2,1)S(1)}, u32[]{:S(2)}, u32[]{:S(2)}) collective-permute-start(bf16[96,128]{1,0:T(8,128)(2,1)S(1)} %get-tuple-element.57), channel_id=1, source_target_pairs={{1,0},{2,1},{3,2},{4,3},{5,4},{6,5},{7,6},{8,7},{9,8},{10,9},{11,1... | collective-permute-start | bytes 73736 | tf_op jit(solution)/shard_map/ppermute | solution.py:453
  148.9 6.0 %collective-permute-start.28 = (bf16[96,128]{1,0:T(8,128)(2,1)}, bf16[96,128]{1,0:T(8,128)(2,1)S(1)}, u32[]{:S(2)}, u32[]{:S(2)}) collective-permute-start(bf16[96,128]{1,0:T(8,128)(2,1)} %get-tuple-element.60), channel_id=1, source_target_pairs={{2,0},{3,1},{4,2},{5,3},{6,4},{7,5},{8,6},{9,7},{10,8},{11,9},{12,... | collective-permute-start | bytes 73736 | tf_op jit(solution)/shard_map/ppermute | solution.py:453
  164.4 7.2 %finish.1 = bf16[1024,768]{1,0:T(8,128)(2,1)} custom-call(bf16[112,128]{1,0:T(8,128)(2,1)S(1)} %collective-permute-done.29.attention_ref, bf16[1552,768]{1,0:T(8,128)(2,1)S(1)} %collective-permute-done.30.bundle_ref, bf16[512,768]{1,0:T(8,128)(2,1)S(1)} %collective-permute-done.31.rows_ref.refs_0_, ...), custom_call_target="tpu_custom_call" | custom-call | tf_op jit(solution)/shard_map/finish/pallas_call | solution.py:428
  (94 shorter events, 46.8 us)
Async XLA Ops:
  3.8 155.5 %collective-permute-start.30 = (bf16[1552,768]{1,0:T(8,128)(2,1)}, bf16[1552,768]{1,0:T(8,128)(2,1)S(1)}, u32[]{:S(2)}, u32[]{:S(2)}) collective-permute-start(bf16[1552,768]{1,0:T(8,128)(2,1)} %bundle.1), channel_id=1, source_target_pairs={{0,64},{64,128},{128,192},{192,0},{1,65},{65,129},{129,193},{193,1... | collective-permute-start | bytes 7151624 | tf_op jit(solution)/shard_map/ppermute | solution.py:453
  5.4 21.3 %collective-permute-start.24 = (bf16[16,2,32,768]{3,2,1,0:T(8,128)(2,1)}, bf16[16,2,32,768]{3,2,1,0:T(8,128)(2,1)}, u32[]{:S(2)}, u32[]{:S(2)}) collective-permute-start(bf16[16,2,32,768]{3,2,1,0:T(8,128)(2,1)} %bitcast.16), channel_id=1, source_target_pairs={{0,1},{1,0},{2,3},{3,2},{4,5},{5,4},{6,7},{7,6},{8,9},{9,8},{10,11... | collective-permute-start | bytes 4718600 | tf_op jit(solution)/shard_map/ppermute | solution.py:959
  6.1 20.7 %all-to-all-start.1 = ((s32[64,1,32]{2,1,0:T(1,128)}), s32[64,1,32]{2,1,0:T(1,128)S(1)}, u32[]{:S(2)}, u32[]{:S(2)}) async-start(s32[64,1,32]{2,1,0:T(1,128)} %broadcast_in_dim.27), calls=%async_computation.1 | async-start | bytes 65536 | tf_op jit(solution)/shard_map/all_to_all | solution.py:952
  32.2 20.8 %collective-permute-start.12 = (bf16[11,2,16,768]{3,2,1,0:T(8,128)(2,1)S(1)}, bf16[11,2,16,768]{3,2,1,0:T(8,128)(2,1)S(1)}, u32[]{:S(2)}, u32[]{:S(2)}) collective-permute-start(bf16[11,2,16,768]{3,2,1,0:T(8,128)(2,1)S(1)} %get-tuple-element.31), channel_id=1, source_target_pairs={{0,2},{1,3},{2,4},{3,5},{4,6},{5,7},{6,8},{7,9},{8,10},{9,11},{10,... | collective-permute-start | bytes 1622024 | tf_op jit(solution)/shard_map/cond/branch_1_fun/ppermute | solution.py:883
  32.9 20.2 %collective-permute-start.16 = (bf16[11,2,16,768]{3,2,1,0:T(8,128)(2,1)S(1)}, bf16[11,2,16,768]{3,2,1,0:T(8,128)(2,1)S(1)}, u32[]{:S(2)}, u32[]{:S(2)}) collective-permute-start(bf16[11,2,16,768]{3,2,1,0:T(8,128)(2,1)S(1)} %get-tuple-element.32), channel_id=1, source_target_pairs={{0,14},{1,15},{2,0},{3,1},{4,2},{5,3},{6,4},{7,5},{8,6},{9,7},{10,... | collective-permute-start | bytes 1622024 | tf_op jit(solution)/shard_map/cond/branch_1_fun/ppermute | solution.py:884
  37.7 12.5 %collective-permute-start = (bf16[10,2,16,768]{3,2,1,0:T(8,128)(2,1)S(1)}, bf16[10,2,16,768]{3,2,1,0:T(8,128)(2,1)S(1)}, u32[]{:S(2)}, u32[]{:S(2)}) collective-permute-start(bf16[10,2,16,768]{3,2,1,0:T(8,128)(2,1)S(1)} %get-tuple-element.25), channel_id=1, source_target_pairs={{0,16},{1,17},{2,18},{3,19},{4,20},{5,21},{6,22},{7,23},{8,24},{9,... | collective-permute-start | bytes 1474568 | tf_op jit(solution)/shard_map/cond/branch_1_fun/ppermute | solution.py:883
  38.4 12.5 %collective-permute-start.2 = (bf16[10,2,16,768]{3,2,1,0:T(8,128)(2,1)S(1)}, bf16[10,2,16,768]{3,2,1,0:T(8,128)(2,1)S(1)}, u32[]{:S(2)}, u32[]{:S(2)}) collective-permute-start(bf16[10,2,16,768]{3,2,1,0:T(8,128)(2,1)S(1)} %get-tuple-element.26), channel_id=1, source_target_pairs={{0,48},{1,49},{2,50},{3,51},{4,52},{5,53},{6,54},{7,55},{8,56},{9,... | collective-permute-start | bytes 1474568 | tf_op jit(solution)/shard_map/cond/branch_1_fun/ppermute | solution.py:884
  53.0 13.9 %collective-permute-start.13 = (bf16[9,2,16,768]{3,2,1,0:T(8,128)(2,1)S(1)}, bf16[9,2,16,768]{3,2,1,0:T(8,128)(2,1)S(1)}, u32[]{:S(2)}, u32[]{:S(2)}) collective-permute-start(bf16[9,2,16,768]{3,2,1,0:T(8,128)(2,1)S(1)} %slice.56), channel_id=1, source_target_pairs={{0,2},{1,3},{2,4},{3,5},{4,6},{5,7},{6,8},{7,9},{8,10},{9,11},{10,... | collective-permute-start | bytes 1327112 | tf_op jit(solution)/shard_map/cond/branch_1_fun/ppermute | solution.py:883
  53.1 13.9 %collective-permute-start.17 = (bf16[9,2,16,768]{3,2,1,0:T(8,128)(2,1)S(1)}, bf16[9,2,16,768]{3,2,1,0:T(8,128)(2,1)S(1)}, u32[]{:S(2)}, u32[]{:S(2)}) collective-permute-start(bf16[9,2,16,768]{3,2,1,0:T(8,128)(2,1)S(1)} %slice.59), channel_id=1, source_target_pairs={{0,14},{1,15},{2,0},{3,1},{4,2},{5,3},{6,4},{7,5},{8,6},{9,7},{10,... | collective-permute-start | bytes 1327112 | tf_op jit(solution)/shard_map/cond/branch_1_fun/ppermute | solution.py:884
  59.8 26.0 %collective-permute-start.8 = (bf16[11,2,16,768]{3,2,1,0:T(8,128)(2,1)S(1)}, bf16[11,2,16,768]{3,2,1,0:T(8,128)(2,1)S(1)}, u32[]{:S(2)}, u32[]{:S(2)}) collective-permute-start(bf16[11,2,16,768]{3,2,1,0:T(8,128)(2,1)S(1)} %get-tuple-element.29), channel_id=1, source_target_pairs={{0,14},{1,15},{2,0},{3,1},{4,2},{5,3},{6,4},{7,5},{8,6},{9,7},{10,... | collective-permute-start | bytes 1622024 | tf_op jit(solution)/shard_map/cond/branch_1_fun/ppermute | solution.py:884
  60.4 25.5 %collective-permute-start.4 = (bf16[11,2,16,768]{3,2,1,0:T(8,128)(2,1)S(1)}, bf16[11,2,16,768]{3,2,1,0:T(8,128)(2,1)S(1)}, u32[]{:S(2)}, u32[]{:S(2)}) collective-permute-start(bf16[11,2,16,768]{3,2,1,0:T(8,128)(2,1)S(1)} %get-tuple-element.28), channel_id=1, source_target_pairs={{0,2},{1,3},{2,4},{3,5},{4,6},{5,7},{6,8},{7,9},{8,10},{9,11},{10,... | collective-permute-start | bytes 1622024 | tf_op jit(solution)/shard_map/cond/branch_1_fun/ppermute | solution.py:883
  66.9 15.5 %collective-permute-start.14 = (bf16[6,2,16,768]{3,2,1,0:T(8,128)(2,1)S(1)}, bf16[6,2,16,768]{3,2,1,0:T(8,128)(2,1)S(1)}, u32[]{:S(2)}, u32[]{:S(2)}) collective-permute-start(bf16[6,2,16,768]{3,2,1,0:T(8,128)(2,1)S(1)} %slice.57), channel_id=1, source_target_pairs={{0,2},{1,3},{2,4},{3,5},{4,6},{5,7},{6,8},{7,9},{8,10},{9,11},{10,... | collective-permute-start | bytes 884744 | tf_op jit(solution)/shard_map/cond/branch_1_fun/ppermute | solution.py:883
  67.1 15.4 %collective-permute-start.18 = (bf16[6,2,16,768]{3,2,1,0:T(8,128)(2,1)S(1)}, bf16[6,2,16,768]{3,2,1,0:T(8,128)(2,1)S(1)}, u32[]{:S(2)}, u32[]{:S(2)}) collective-permute-start(bf16[6,2,16,768]{3,2,1,0:T(8,128)(2,1)S(1)} %slice.60), channel_id=1, source_target_pairs={{0,14},{1,15},{2,0},{3,1},{4,2},{5,3},{6,4},{7,5},{8,6},{9,7},{10,... | collective-permute-start | bytes 884744 | tf_op jit(solution)/shard_map/cond/branch_1_fun/ppermute | solution.py:884
  82.4 9.1 %collective-permute-start.15 = (bf16[4,2,16,768]{3,2,1,0:T(8,128)(2,1)S(1)}, bf16[4,2,16,768]{3,2,1,0:T(8,128)(2,1)S(1)}, u32[]{:S(2)}, u32[]{:S(2)}) collective-permute-start(bf16[4,2,16,768]{3,2,1,0:T(8,128)(2,1)S(1)} %slice.58), channel_id=1, source_target_pairs={{0,2},{1,3},{2,4},{3,5},{4,6},{5,7},{6,8},{7,9},{8,10},{9,11},{10,... | collective-permute-start | bytes 589832 | tf_op jit(solution)/shard_map/cond/branch_1_fun/ppermute | solution.py:883
  82.5 8.9 %collective-permute-start.19 = (bf16[4,2,16,768]{3,2,1,0:T(8,128)(2,1)S(1)}, bf16[4,2,16,768]{3,2,1,0:T(8,128)(2,1)S(1)}, u32[]{:S(2)}, u32[]{:S(2)}) collective-permute-start(bf16[4,2,16,768]{3,2,1,0:T(8,128)(2,1)S(1)} %slice.61), channel_id=1, source_target_pairs={{0,14},{1,15},{2,0},{3,1},{4,2},{5,3},{6,4},{7,5},{8,6},{9,7},{10,... | collective-permute-start | bytes 589832 | tf_op jit(solution)/shard_map/cond/branch_1_fun/ppermute | solution.py:884
  85.9 11.4 %collective-permute-start.9 = (bf16[9,2,16,768]{3,2,1,0:T(8,128)(2,1)S(1)}, bf16[9,2,16,768]{3,2,1,0:T(8,128)(2,1)S(1)}, u32[]{:S(2)}, u32[]{:S(2)}) collective-permute-start(bf16[9,2,16,768]{3,2,1,0:T(8,128)(2,1)S(1)} %slice.53), channel_id=1, source_target_pairs={{0,14},{1,15},{2,0},{3,1},{4,2},{5,3},{6,4},{7,5},{8,6},{9,7},{10,... | collective-permute-start | bytes 1327112 | tf_op jit(solution)/shard_map/cond/branch_1_fun/ppermute | solution.py:884
  86.0 14.8 %collective-permute-start.5 = (bf16[9,2,16,768]{3,2,1,0:T(8,128)(2,1)S(1)}, bf16[9,2,16,768]{3,2,1,0:T(8,128)(2,1)S(1)}, u32[]{:S(2)}, u32[]{:S(2)}) collective-permute-start(bf16[9,2,16,768]{3,2,1,0:T(8,128)(2,1)S(1)} %slice.50), channel_id=1, source_target_pairs={{0,2},{1,3},{2,4},{3,5},{4,6},{5,7},{6,8},{7,9},{8,10},{9,11},{10,... | collective-permute-start | bytes 1327112 | tf_op jit(solution)/shard_map/cond/branch_1_fun/ppermute | solution.py:883
  94.0 12.3 %collective-permute-start.20 = (bf16[10,2,16,768]{3,2,1,0:T(8,128)(2,1)S(1)}, bf16[10,2,16,768]{3,2,1,0:T(8,128)(2,1)S(1)}, u32[]{:S(2)}, u32[]{:S(2)}) collective-permute-start(bf16[10,2,16,768]{3,2,1,0:T(8,128)(2,1)S(1)} %get-tuple-element.34), channel_id=1, source_target_pairs={{0,16},{1,17},{2,18},{3,19},{4,20},{5,21},{6,22},{7,23},{8,24},{9,... | collective-permute-start | bytes 1474568 | tf_op jit(solution)/shard_map/cond/branch_1_fun/ppermute | solution.py:883
  94.1 12.3 %collective-permute-start.22 = (bf16[10,2,16,768]{3,2,1,0:T(8,128)(2,1)S(1)}, bf16[10,2,16,768]{3,2,1,0:T(8,128)(2,1)S(1)}, u32[]{:S(2)}, u32[]{:S(2)}) collective-permute-start(bf16[10,2,16,768]{3,2,1,0:T(8,128)(2,1)S(1)} %get-tuple-element.35), channel_id=1, source_target_pairs={{0,48},{1,49},{2,50},{3,51},{4,52},{5,53},{6,54},{7,55},{8,56},{9,... | collective-permute-start | bytes 1474568 | tf_op jit(solution)/shard_map/cond/branch_1_fun/ppermute | solution.py:884
  97.3 12.6 %collective-permute-start.10 = (bf16[6,2,16,768]{3,2,1,0:T(8,128)(2,1)S(1)}, bf16[6,2,16,768]{3,2,1,0:T(8,128)(2,1)S(1)}, u32[]{:S(2)}, u32[]{:S(2)}) collective-permute-start(bf16[6,2,16,768]{3,2,1,0:T(8,128)(2,1)S(1)} %slice.54), channel_id=1, source_target_pairs={{0,14},{1,15},{2,0},{3,1},{4,2},{5,3},{6,4},{7,5},{8,6},{9,7},{10,... | collective-permute-start | bytes 884744 | tf_op jit(solution)/shard_map/cond/branch_1_fun/ppermute | solution.py:884
  100.9 12.5 %collective-permute-start.6 = (bf16[6,2,16,768]{3,2,1,0:T(8,128)(2,1)S(1)}, bf16[6,2,16,768]{3,2,1,0:T(8,128)(2,1)S(1)}, u32[]{:S(2)}, u32[]{:S(2)}) collective-permute-start(bf16[6,2,16,768]{3,2,1,0:T(8,128)(2,1)S(1)} %slice.51), channel_id=1, source_target_pairs={{0,2},{1,3},{2,4},{3,5},{4,6},{5,7},{6,8},{7,9},{8,10},{9,11},{10,... | collective-permute-start | bytes 884744 | tf_op jit(solution)/shard_map/cond/branch_1_fun/ppermute | solution.py:883
  124.5 34.8 %collective-permute-start.31 = (bf16[512,768]{1,0:T(8,128)(2,1)}, bf16[512,768]{1,0:T(8,128)(2,1)S(1)}, u32[]{:S(2)}, u32[]{:S(2)}) collective-permute-start(bf16[512,768]{1,0:T(8,128)(2,1)} %bitcast.8.rows_0_ref), channel_id=1, source_target_pairs={{0,64},{64,128},{128,192},{192,0},{1,65},{65,129},{129,193},{193,1... | collective-permute-start | bytes 2359304 | tf_op jit(solution)/shard_map/ppermute | solution.py:453
  126.2 35.0 %collective-permute-start.32 = (bf16[512,768]{1,0:T(8,128)(2,1)}, bf16[512,768]{1,0:T(8,128)(2,1)}, u32[]{:S(2)}, u32[]{:S(2)}) collective-permute-start(bf16[512,768]{1,0:T(8,128)(2,1)} %bitcast.9.rows_1_ref), channel_id=1, source_target_pairs={{0,64},{64,128},{128,192},{192,0},{1,65},{65,129},{129,193},{193,1... | collective-permute-start | bytes 2359304 | tf_op jit(solution)/shard_map/ppermute | solution.py:453
  147.0 8.0 %collective-permute-start.27 = (bf16[96,128]{1,0:T(8,128)(2,1)}, bf16[96,128]{1,0:T(8,128)(2,1)S(1)}, u32[]{:S(2)}, u32[]{:S(2)}) collective-permute-start(bf16[96,128]{1,0:T(8,128)(2,1)} %get-tuple-element.59), channel_id=1, source_target_pairs={{0,2},{1,3},{2,4},{3,5},{4,6},{5,7},{6,8},{7,9},{8,10},{9,11},{10,... | collective-permute-start | bytes 73736 | tf_op jit(solution)/shard_map/ppermute | solution.py:453
  (19 other events, 282.7 us)

commit v3 on v2

--- a/solution.py
+++ b/solution.py
@@ -812,32 +812,30 @@
     )(table, *sources)
 
 
-def land_kernel(part, count, table_ref, *refs):
-    sources = refs[:count]
-    outs = refs[-PARTS - 5 : -5]
-    live_ref, pool, done, in_sem, out_sem = refs[-5:]
-    row_count, half, _ = done.shape
-    copies = pooled(sources, pool, in_sem)
+def land_kernel(count_a, count_b, table_ref, *refs):
+    sources_a, sources_b = refs[:count_a], refs[count_a : count_a + count_b]
+    outs = refs[count_a + count_b : count_a + count_b + PARTS]
+    live_ref, pool_a, pool_b, done, sem_a, sem_b, out_sem = refs[count_a + count_b + PARTS :]
+    row_count, length, _ = done.shape
+    half = length // 2
+    copies = pooled(sources_a, pool_a, sem_a) + pooled(sources_b, pool_b, sem_b)
     for copy in copies:
         copy.start()
     for copy in copies:
         copy.wait()
 
     def step(m, carry):
-        live = table_ref[4 + part, m] >= 0
+        live = table_ref[4, m] >= 0
         live_ref[m] = jnp.where(live, 1, 0)
-        code = jnp.maximum(table_ref[4 + part, m], 0)
-        value = pool[code >> 1, code & 1]
-        done[m] = jnp.where(live, value, jnp.zeros_like(value))
+        for part, pool in ((0, pool_a), (1, pool_b)):
+            code = jnp.maximum(table_ref[4 + part, m], 0)
+            value = pool[code >> 1, code & 1]
+            done[m, pl.ds(part * half, half), :] = jnp.where(live, value, jnp.zeros_like(value))
         return carry
 
     rows = row_count // PARTS
     leaving = [
-        pltpu.make_async_copy(
-            done.at[pl.ds(k * rows, rows)],
-            out.at[:, pl.ds(part * half, half), :],
-            out_sem.at[k],
-        )
+        pltpu.make_async_copy(done.at[pl.ds(k * rows, rows)], out, out_sem.at[k])
         for k, out in enumerate(outs)
     ]
     for k in range(PARTS):
@@ -847,30 +845,29 @@
         copy.wait()
 
 
-def land(part, table, sources, row_count, length, begun):
+def land(table, sources_a, sources_b, row_count, length):
     anywhere = pl.BlockSpec(memory_space=pl.ANY)
     smem = pl.BlockSpec(memory_space=pltpu.SMEM)
-    hbm = pl.BlockSpec(memory_space=pltpu.HBM)
-    two, half, width = sources[0].shape[1:]
-    dtype = sources[0].dtype
-    count = len(sources)
-    return pl.pallas_call(
-        functools.partial(land_kernel, part, count),
+    two, half, width = sources_a[0].shape[1:]
+    dtype = sources_a[0].dtype
+    return pl.pallas_call(
+        functools.partial(land_kernel, len(sources_a), len(sources_b)),
         out_shape=(jax.ShapeDtypeStruct((row_count // PARTS, length, width), dtype),) * PARTS
         + (jax.ShapeDtypeStruct((row_count,), jnp.int32),),
-        in_specs=[smem] + [anywhere] * count + [hbm] * len(begun),
-        out_specs=(hbm,) * PARTS + (smem,),
+        in_specs=[smem] + [anywhere] * (len(sources_a) + len(sources_b)),
+        out_specs=(pl.BlockSpec(memory_space=pltpu.HBM),) * PARTS + (smem,),
         scratch_shapes=[
-            pltpu.VMEM((sum(s.shape[0] for s in sources), two, half, width), dtype),
-            pltpu.VMEM((row_count, half, width), dtype),
-            pltpu.SemaphoreType.DMA((count,)),
+            pltpu.VMEM((sum(s.shape[0] for s in sources_a), two, half, width), dtype),
+            pltpu.VMEM((sum(s.shape[0] for s in sources_b), two, half, width), dtype),
+            pltpu.VMEM((row_count, length, width), dtype),
+            pltpu.SemaphoreType.DMA((len(sources_a),)),
+            pltpu.SemaphoreType.DMA((len(sources_b),)),
             pltpu.SemaphoreType.DMA((PARTS,)),
         ],
-        input_output_aliases={1 + count + k: k for k in range(len(begun))},
         compiler_params=pltpu.CompilerParams(vmem_limit_bytes=40 << 20),
         name="land",
         interpret=INTERPRET,
-    )(table, *sources, *begun)
+    )(table, *sources_a, *sources_b)
 
 
 def chain(forward, backward, caps, step, ring):
@@ -899,9 +896,13 @@
     last_b = chain(later[0], later[1], z_caps, 2, RING_Z)
     turned = turn_over(table, 2, along_z + [z_still], x_sizes)
     last_a = chain(turned[0], turned[1], x_caps, 2 * RING_Z, RING_X)
-    row_count, length = own.shape[0] * own.shape[1], own.shape[2]
-    *begun, _ = land(0, table, last_a + [turned[2]], row_count, length, ())
-    return land(1, table, last_b + [later[2]], row_count, length, begun)
+    return land(
+        table,
+        last_a + [turned[2]],
+        last_b + [later[2]],
+        own.shape[0] * own.shape[1],
+        own.shape[2],
+    )
 
 
 def dense(targets, everywhere, own):

time: 173 us -> 170 us (0.983)
  waiting for transfers between devices: 52.6 us -> 50.4 us
  Pallas kernels: 45.6 us -> 43.5 us
    ppermute x12, waiting for transfers between devices: 39.8 us -> 29.3 us  [chain(): lax.ppermute(forward[:cap], 'depth', [(i, moved(i, 1)) for i in devices])]
    ppermute x12, waiting for transfers between devices: 0.18 us -> 8.49 us  [chain(): lax.ppermute(backward[:cap], 'depth', [(i, moved(i, -1)) for i in devices])]
    ppermute x12, starting transfers between devices: 30.4 us -> 34.9 us  [chain(): lax.ppermute(backward[:cap], 'depth', [(i, moved(i, -1)) for i in devices])]
    ppermute x12, starting transfers between devices: 6.32 us -> 2.85 us  [chain(): lax.ppermute(forward[:cap], 'depth', [(i, moved(i, 1)) for i in devices])]
    pallas_call x2 -> x1, Pallas kernels: 7.73 us -> 5.66 us  [land(): pl.pallas_call(functools.partial(land_kernel, len(sources_a), len(sources...]
  transfers between devices with their start and end apart: 34 -> 34, of which waited for: 14 -> 15; matrix products, arithmetic and copies ran while one was open for 1% -> 1% of each run, Pallas kernels for 20% -> 19%
where the time goes in v3:
time: 170 us; the launch traced here: 168 us
  starting transfers between devices  70.3 us (41%)
  waiting for transfers between devices  50.4 us (30%)
  Pallas kernels  43.5 us (26%)
  local copies, waits for them, and re-layouts  2.8 us (2%)
    ppermute x12, starting transfers between devices, chain(): lax.ppermute(backward[:cap], 'depth', [(i, moved(i, -1)) for i in devices])  34.9 us
    ppermute x12, waiting for transfers between devices, chain(): lax.ppermute(forward[:cap], 'depth', [(i, moved(i, 1)) for i in devices])  29.3 us
    ppermute x8, starting transfers between devices, shifted(): return lax.ppermute(value, axis, route)  20.4 us
    all_to_all x1, starting transfers between devices, layer(): lax.all_to_all(jnp.broadcast_to(targets[None, None], (peers, 1, row_count...  12.1 us
    all_to_all x1, waiting for transfers between devices, layer(): lax.all_to_all(jnp.broadcast_to(targets[None, None], (peers, 1, row_count...  8.54 us
    ppermute x12, waiting for transfers between devices, chain(): lax.ppermute(backward[:cap], 'depth', [(i, moved(i, -1)) for i in devices])  8.49 us
    pallas_call x1, Pallas kernels, front(): pl.pallas_call(front_kernel, out_shape=(jax.ShapeDtypeStruct((quarter, 4...  7.66 us
    pallas_call x1, Pallas kernels, finish(): pl.pallas_call(finish_kernel, out_shape=jax.ShapeDtypeStruct((tokens * PA...  7.16 us
  transfers between devices with their start and end apart: 34, of which 15 were waited for; matrix products, arithmetic and copies ran while one was open for 1% of the time, Pallas kernels for 19%

profile of v3, /device:TPU:2, one launch (start us, length us, event | category | flops | bytes accessed | tf_op | source)
XLA Modules:
  0.0 168.5 jit_solution(5036735977940812344)
XLA Ops:
  0.0 3.7 %bundle.1 = bf16[1552,768]{1,0:T(8,128)(2,1)} custom-call(bf16[768,2304]{1,0:T(8,128)(2,1)} %bitcast.14, bf16[768,768]{1,0:T(8,128)(2,1)} %bitcast.19, f32[1,768]{1,0:T(1,128)} %gain_ref.3, f32[1,768]{1,0:T(1,128)} %bias_ref.3), custom_call_target="tpu_custom_call" | custom-call | tf_op jit(solution)/shard_map/bundle/pallas_call | solution.py:711
  6.1 12.1 %all-to-all-start.1 = ((s32[64,1,32]{2,1,0:T(1,128)}), s32[64,1,32]{2,1,0:T(1,128)S(1)}, u32[]{:S(2)}, u32[]{:S(2)}) async-start(s32[64,1,32]{2,1,0:T(1,128)} %broadcast_in_dim.27), calls=%async_computation.1 | async-start | bytes 65536 | tf_op jit(solution)/shard_map/all_to_all | solution.py:953
  18.2 8.5 %all-to-all-done.1 = s32[64,1,32]{2,1,0:T(1,128)S(1)} async-done(((s32[64,1,32]{2,1,0:T(1,128)}), s32[64,1,32]{2,1,0:T(1,128)S(1)}, u32[]{:S(2)}, u32[]{:S(2)}) %all-to-all-start.1) | async-done | bytes 8224 | tf_op jit(solution)/shard_map/all_to_all | solution.py:953
  29.8 91.4 %conditional.1 = ((bf16[16,32,768]{2,1,0:T(8,128)(2,1)}, bf16[16,32,768]{2,1,0:T(8,128)(2,1)}, s32[32]{0:T(128)S(1)})) conditional(s32[]{:T(128)} %bitcast.7, (s32[64,32]{1,0:T(8,128)S(1)}, s32[32]{0:T(128)S(1)}, bf16[1,32,32,768]{3,2,1,0:T(8,128)(2,1)}) %tuple.21, (s32[8,128]{1,0:T(8,128)S(1)}, bf16[16,2,32,768]{3,2,1,0:T(8,128)(2,1)}, ...), branch_computations={%region_0.2_spmd, %region_2.3_spmd} | conditional | flops 212035 | bytes 51119076 | solution.py:964
  35.8 2.6 %collective-permute-start.4 = (bf16[11,2,16,768]{3,2,1,0:T(8,128)(2,1)S(1)}, bf16[11,2,16,768]{3,2,1,0:T(8,128)(2,1)S(1)}, u32[]{:S(2)}, u32[]{:S(2)}) collective-permute-start(bf16[11,2,16,768]{3,2,1,0:T(8,128)(2,1)S(1)} %get-tuple-element.26), channel_id=1, source_target_pairs={{0,14},{1,15},{2,0},{3,1},{4,2},{5,3},{6,4},{7,5},{8,6},{9,7},{10,... | collective-permute-start | bytes 1622024 | tf_op jit(solution)/shard_map/cond/branch_1_fun/ppermute | solution.py:881
  39.8 8.1 %collective-permute-done.12.refs_0_ = bf16[10,2,16,768]{3,2,1,0:T(8,128)(2,1)S(1)} collective-permute-done((bf16[10,2,16,768]{3,2,1,0:T(8,128)(2,1)S(1)}, bf16[10,2,16,768]{3,2,1,0:T(8,128)(2,1)S(1)}, u32[]{:S(2)}, u32[]{:S(2)}) %collective-permute-start.12) | collective-permute-done | bytes 491552 | tf_op jit(solution)/shard_map/cond/branch_1_fun/ppermute | solution.py:880
  52.2 3.3 %collective-permute-start.5 = (bf16[9,2,16,768]{3,2,1,0:T(8,128)(2,1)S(1)}, bf16[9,2,16,768]{3,2,1,0:T(8,128)(2,1)S(1)}, u32[]{:S(2)}, u32[]{:S(2)}) collective-permute-start(bf16[9,2,16,768]{3,2,1,0:T(8,128)(2,1)S(1)} %slice.51), channel_id=1, source_target_pairs={{0,14},{1,15},{2,0},{3,1},{4,2},{5,3},{6,4},{7,5},{8,6},{9,7},{10,... | collective-permute-start | bytes 1327112 | tf_op jit(solution)/shard_map/cond/branch_1_fun/ppermute | solution.py:881
  59.3 3.2 %collective-permute-start.20 = (bf16[11,2,16,768]{3,2,1,0:T(8,128)(2,1)S(1)}, bf16[11,2,16,768]{3,2,1,0:T(8,128)(2,1)S(1)}, u32[]{:S(2)}, u32[]{:S(2)}) collective-permute-start(bf16[11,2,16,768]{3,2,1,0:T(8,128)(2,1)S(1)} %get-tuple-element.35), channel_id=1, source_target_pairs={{0,14},{1,15},{2,0},{3,1},{4,2},{5,3},{6,4},{7,5},{8,6},{9,7},{10,... | collective-permute-start | bytes 1622024 | tf_op jit(solution)/shard_map/cond/branch_1_fun/ppermute | solution.py:881
  62.6 3.6 %collective-permute-done.1.refs_1_ = bf16[9,2,16,768]{3,2,1,0:T(8,128)(2,1)S(1)} collective-permute-done((bf16[9,2,16,768]{3,2,1,0:T(8,128)(2,1)S(1)}, bf16[9,2,16,768]{3,2,1,0:T(8,128)(2,1)S(1)}, u32[]{:S(2)}, u32[]{:S(2)}) %collective-permute-start.1) | collective-permute-done | bytes 442400 | tf_op jit(solution)/shard_map/cond/branch_1_fun/ppermute | solution.py:880
  66.3 3.3 %collective-permute-start.6 = (bf16[6,2,16,768]{3,2,1,0:T(8,128)(2,1)S(1)}, bf16[6,2,16,768]{3,2,1,0:T(8,128)(2,1)S(1)}, u32[]{:S(2)}, u32[]{:S(2)}) collective-permute-start(bf16[6,2,16,768]{3,2,1,0:T(8,128)(2,1)S(1)} %slice.52), channel_id=1, source_target_pairs={{0,14},{1,15},{2,0},{3,1},{4,2},{5,3},{6,4},{7,5},{8,6},{9,7},{10,... | collective-permute-start | bytes 884744 | tf_op jit(solution)/shard_map/cond/branch_1_fun/ppermute | solution.py:881
  69.6 11.7 %collective-permute-done.2.refs_2_ = bf16[6,2,16,768]{3,2,1,0:T(8,128)(2,1)S(1)} collective-permute-done((bf16[6,2,16,768]{3,2,1,0:T(8,128)(2,1)S(1)}, bf16[6,2,16,768]{3,2,1,0:T(8,128)(2,1)S(1)}, u32[]{:S(2)}, u32[]{:S(2)}) %collective-permute-start.2) | collective-permute-done | bytes 294944 | tf_op jit(solution)/shard_map/cond/branch_1_fun/ppermute | solution.py:880
  81.4 3.3 %collective-permute-start.7 = (bf16[4,2,16,768]{3,2,1,0:T(8,128)(2,1)S(1)}, bf16[4,2,16,768]{3,2,1,0:T(8,128)(2,1)S(1)}, u32[]{:S(2)}, u32[]{:S(2)}) collective-permute-start(bf16[4,2,16,768]{3,2,1,0:T(8,128)(2,1)S(1)} %slice.53), channel_id=1, source_target_pairs={{0,14},{1,15},{2,0},{3,1},{4,2},{5,3},{6,4},{7,5},{8,6},{9,7},{10,... | collective-permute-start | bytes 589832 | tf_op jit(solution)/shard_map/cond/branch_1_fun/ppermute | solution.py:881
  84.8 3.3 %collective-permute-start.21 = (bf16[9,2,16,768]{3,2,1,0:T(8,128)(2,1)S(1)}, bf16[9,2,16,768]{3,2,1,0:T(8,128)(2,1)S(1)}, u32[]{:S(2)}, u32[]{:S(2)}) collective-permute-start(bf16[9,2,16,768]{3,2,1,0:T(8,128)(2,1)S(1)} %slice.61), channel_id=1, source_target_pairs={{0,14},{1,15},{2,0},{3,1},{4,2},{5,3},{6,4},{7,5},{8,6},{9,7},{10,... | collective-permute-start | bytes 1327112 | tf_op jit(solution)/shard_map/cond/branch_1_fun/ppermute | solution.py:881
  92.8 3.8 %collective-permute-start.10 = (bf16[10,2,16,768]{3,2,1,0:T(8,128)(2,1)S(1)}, bf16[10,2,16,768]{3,2,1,0:T(8,128)(2,1)S(1)}, u32[]{:S(2)}, u32[]{:S(2)}) collective-permute-start(bf16[10,2,16,768]{3,2,1,0:T(8,128)(2,1)S(1)} %get-tuple-element.29), channel_id=1, source_target_pairs={{0,48},{1,49},{2,50},{3,51},{4,52},{5,53},{6,54},{7,55},{8,56},{9,... | collective-permute-start | bytes 1474568 | tf_op jit(solution)/shard_map/cond/branch_1_fun/ppermute | solution.py:881
  97.1 3.3 %collective-permute-start.22 = (bf16[6,2,16,768]{3,2,1,0:T(8,128)(2,1)S(1)}, bf16[6,2,16,768]{3,2,1,0:T(8,128)(2,1)S(1)}, u32[]{:S(2)}, u32[]{:S(2)}) collective-permute-start(bf16[6,2,16,768]{3,2,1,0:T(8,128)(2,1)S(1)} %slice.62), channel_id=1, source_target_pairs={{0,14},{1,15},{2,0},{3,1},{4,2},{5,3},{6,4},{7,5},{8,6},{9,7},{10,... | collective-permute-start | bytes 884744 | tf_op jit(solution)/shard_map/cond/branch_1_fun/ppermute | solution.py:881
  100.4 5.2 %collective-permute-done.10.refs_2_ = bf16[10,2,16,768]{3,2,1,0:T(8,128)(2,1)S(1)} collective-permute-done((bf16[10,2,16,768]{3,2,1,0:T(8,128)(2,1)S(1)}, bf16[10,2,16,768]{3,2,1,0:T(8,128)(2,1)S(1)}, u32[]{:S(2)}, u32[]{:S(2)}) %collective-permute-start.10) | collective-permute-done | bytes 491552 | tf_op jit(solution)/shard_map/cond/branch_1_fun/ppermute | solution.py:881
  105.6 2.6 %collective-permute-start.11 = (bf16[5,2,16,768]{3,2,1,0:T(8,128)(2,1)S(1)}, bf16[5,2,16,768]{3,2,1,0:T(8,128)(2,1)S(1)}, u32[]{:S(2)}, u32[]{:S(2)}) collective-permute-start(bf16[5,2,16,768]{3,2,1,0:T(8,128)(2,1)S(1)} %slice.55), channel_id=1, source_target_pairs={{0,48},{1,49},{2,50},{3,51},{4,52},{5,53},{6,54},{7,55},{8,56},{9,... | collective-permute-start | bytes 737288 | tf_op jit(solution)/shard_map/cond/branch_1_fun/ppermute | solution.py:881
  108.4 3.4 %collective-permute-start.23 = (bf16[4,2,16,768]{3,2,1,0:T(8,128)(2,1)S(1)}, bf16[4,2,16,768]{3,2,1,0:T(8,128)(2,1)S(1)}, u32[]{:S(2)}, u32[]{:S(2)}) collective-permute-start(bf16[4,2,16,768]{3,2,1,0:T(8,128)(2,1)S(1)} %slice.63), channel_id=1, source_target_pairs={{0,14},{1,15},{2,0},{3,1},{4,2},{5,3},{6,4},{7,5},{8,6},{9,7},{10,... | collective-permute-start | bytes 589832 | tf_op jit(solution)/shard_map/cond/branch_1_fun/ppermute | solution.py:881
  111.9 2.6 %collective-permute-done.9.refs_1_ = bf16[5,2,16,768]{3,2,1,0:T(8,128)(2,1)S(1)} collective-permute-done((bf16[5,2,16,768]{3,2,1,0:T(8,128)(2,1)S(1)}, bf16[5,2,16,768]{3,2,1,0:T(8,128)(2,1)S(1)}, u32[]{:S(2)}, u32[]{:S(2)}) %collective-permute-start.9) | collective-permute-done | bytes 245792 | tf_op jit(solution)/shard_map/cond/branch_1_fun/ppermute | solution.py:880
  115.4 5.7 %land.1 = (bf16[16,32,768]{2,1,0:T(8,128)(2,1)}, bf16[16,32,768]{2,1,0:T(8,128)(2,1)}, s32[32]{0:T(128)S(1)}) custom-call(s32[8,128]{1,0:T(8,128)S(1)} %get-tuple-element.22.table_ref, bf16[10,2,16,768]{3,2,1,0:T(8,128)(2,1)S(1)} %collective-permute-done.8.refs_0_, bf16[5,2,16,768]{3,2,1,0:T(8,128)(2,1)S(1)} %collective-permute-done.9.refs_1_, ...), custom_call_target="tpu_custom_call" | custom-call | tf_op jit(solution)/shard_map/cond/branch_1_fun/land/pallas_call | solution.py:853
  124.2 7.7 %front.1 = (f32[96,128]{1,0:T(8,128)S(1)}, bf16[96,128]{1,0:T(8,128)(2,1)S(1)}) custom-call(s32[32]{0:T(128)S(1)} %get-tuple-element.50.live_ref, bf16[512,768]{1,0:T(8,128)(2,1)} %bitcast.21, bf16[512,768]{1,0:T(8,128)(2,1)} %bitcast.23, f32[1,768]{1,0:T(1,128)S(1)} %copy-done.1, f32[1,768]{1,0:T(1,128)S(1)} %copy-done.2, bf16[768,2304]{1,0:T(8,128)(2,1)} %bitcast.15), custom_call_target="tpu_custom_call" | custom-call | tf_op jit(solution)/shard_map/front/pallas_call | solution.py:221
  134.4 5.8 %collective-permute-start.26 = (bf16[96,128]{1,0:T(8,128)(2,1)S(1)}, bf16[96,128]{1,0:T(8,128)(2,1)S(1)}, u32[]{:S(2)}, u32[]{:S(2)}) collective-permute-start(bf16[96,128]{1,0:T(8,128)(2,1)S(1)} %get-tuple-element.55), channel_id=1, source_target_pairs={{1,0},{2,1},{3,2},{4,3},{5,4},{6,5},{7,6},{8,7},{9,8},{10,9},{11,1... | collective-permute-start | bytes 73736 | tf_op jit(solution)/shard_map/ppermute | solution.py:453
  145.7 6.0 %collective-permute-start.28 = (bf16[96,128]{1,0:T(8,128)(2,1)}, bf16[96,128]{1,0:T(8,128)(2,1)S(1)}, u32[]{:S(2)}, u32[]{:S(2)}) collective-permute-start(bf16[96,128]{1,0:T(8,128)(2,1)} %get-tuple-element.58), channel_id=1, source_target_pairs={{2,0},{3,1},{4,2},{5,3},{6,4},{7,5},{8,6},{9,7},{10,8},{11,9},{12,... | collective-permute-start | bytes 73736 | tf_op jit(solution)/shard_map/ppermute | solution.py:453
  161.1 7.2 %finish.1 = bf16[1024,768]{1,0:T(8,128)(2,1)} custom-call(bf16[112,128]{1,0:T(8,128)(2,1)S(1)} %collective-permute-done.29.attention_ref, bf16[1552,768]{1,0:T(8,128)(2,1)S(1)} %collective-permute-done.30.bundle_ref, bf16[512,768]{1,0:T(8,128)(2,1)S(1)} %collective-permute-done.31.rows_ref.refs_0_, ...), custom_call_target="tpu_custom_call" | custom-call | tf_op jit(solution)/shard_map/finish/pallas_call | solution.py:428
  (93 shorter events, 47.2 us)
Async XLA Ops:
  3.8 152.3 %collective-permute-start.30 = (bf16[1552,768]{1,0:T(8,128)(2,1)}, bf16[1552,768]{1,0:T(8,128)(2,1)S(1)}, u32[]{:S(2)}, u32[]{:S(2)}) collective-permute-start(bf16[1552,768]{1,0:T(8,128)(2,1)} %bundle.1), channel_id=1, source_target_pairs={{0,64},{64,128},{128,192},{192,0},{1,65},{65,129},{129,193},{193,1... | collective-permute-start | bytes 7151624 | tf_op jit(solution)/shard_map/ppermute | solution.py:453
  5.4 21.3 %collective-permute-start.24 = (bf16[16,2,32,768]{3,2,1,0:T(8,128)(2,1)}, bf16[16,2,32,768]{3,2,1,0:T(8,128)(2,1)}, u32[]{:S(2)}, u32[]{:S(2)}) collective-permute-start(bf16[16,2,32,768]{3,2,1,0:T(8,128)(2,1)} %bitcast.16), channel_id=1, source_target_pairs={{0,1},{1,0},{2,3},{3,2},{4,5},{5,4},{6,7},{7,6},{8,9},{9,8},{10,11... | collective-permute-start | bytes 4718600 | tf_op jit(solution)/shard_map/ppermute | solution.py:960
  6.1 20.7 %all-to-all-start.1 = ((s32[64,1,32]{2,1,0:T(1,128)}), s32[64,1,32]{2,1,0:T(1,128)S(1)}, u32[]{:S(2)}, u32[]{:S(2)}) async-start(s32[64,1,32]{2,1,0:T(1,128)} %broadcast_in_dim.27), calls=%async_computation.1 | async-start | bytes 65536 | tf_op jit(solution)/shard_map/all_to_all | solution.py:953
  32.1 19.9 %collective-permute-start = (bf16[11,2,16,768]{3,2,1,0:T(8,128)(2,1)S(1)}, bf16[11,2,16,768]{3,2,1,0:T(8,128)(2,1)S(1)}, u32[]{:S(2)}, u32[]{:S(2)}) collective-permute-start(bf16[11,2,16,768]{3,2,1,0:T(8,128)(2,1)S(1)} %get-tuple-element.25), channel_id=1, source_target_pairs={{0,2},{1,3},{2,4},{3,5},{4,6},{5,7},{6,8},{7,9},{8,10},{9,11},{10,... | collective-permute-start | bytes 1622024 | tf_op jit(solution)/shard_map/cond/branch_1_fun/ppermute | solution.py:880
  35.0 12.8 %collective-permute-start.12 = (bf16[10,2,16,768]{3,2,1,0:T(8,128)(2,1)S(1)}, bf16[10,2,16,768]{3,2,1,0:T(8,128)(2,1)S(1)}, u32[]{:S(2)}, u32[]{:S(2)}) collective-permute-start(bf16[10,2,16,768]{3,2,1,0:T(8,128)(2,1)S(1)} %get-tuple-element.31), channel_id=1, source_target_pairs={{0,16},{1,17},{2,18},{3,19},{4,20},{5,21},{6,22},{7,23},{8,24},{9,... | collective-permute-start | bytes 1474568 | tf_op jit(solution)/shard_map/cond/branch_1_fun/ppermute | solution.py:880
  35.8 16.4 %collective-permute-start.4 = (bf16[11,2,16,768]{3,2,1,0:T(8,128)(2,1)S(1)}, bf16[11,2,16,768]{3,2,1,0:T(8,128)(2,1)S(1)}, u32[]{:S(2)}, u32[]{:S(2)}) collective-permute-start(bf16[11,2,16,768]{3,2,1,0:T(8,128)(2,1)S(1)} %get-tuple-element.26), channel_id=1, source_target_pairs={{0,14},{1,15},{2,0},{3,1},{4,2},{5,3},{6,4},{7,5},{8,6},{9,7},{10,... | collective-permute-start | bytes 1622024 | tf_op jit(solution)/shard_map/cond/branch_1_fun/ppermute | solution.py:881
  38.4 12.1 %collective-permute-start.14 = (bf16[10,2,16,768]{3,2,1,0:T(8,128)(2,1)S(1)}, bf16[10,2,16,768]{3,2,1,0:T(8,128)(2,1)S(1)}, u32[]{:S(2)}, u32[]{:S(2)}) collective-permute-start(bf16[10,2,16,768]{3,2,1,0:T(8,128)(2,1)S(1)} %get-tuple-element.32), channel_id=1, source_target_pairs={{0,48},{1,49},{2,50},{3,51},{4,52},{5,53},{6,54},{7,55},{8,56},{9,... | collective-permute-start | bytes 1474568 | tf_op jit(solution)/shard_map/cond/branch_1_fun/ppermute | solution.py:881
  52.1 14.0 %collective-permute-start.1 = (bf16[9,2,16,768]{3,2,1,0:T(8,128)(2,1)S(1)}, bf16[9,2,16,768]{3,2,1,0:T(8,128)(2,1)S(1)}, u32[]{:S(2)}, u32[]{:S(2)}) collective-permute-start(bf16[9,2,16,768]{3,2,1,0:T(8,128)(2,1)S(1)} %slice.48), channel_id=1, source_target_pairs={{0,2},{1,3},{2,4},{3,5},{4,6},{5,7},{6,8},{7,9},{8,10},{9,11},{10,... | collective-permute-start | bytes 1327112 | tf_op jit(solution)/shard_map/cond/branch_1_fun/ppermute | solution.py:880
  52.2 14.0 %collective-permute-start.5 = (bf16[9,2,16,768]{3,2,1,0:T(8,128)(2,1)S(1)}, bf16[9,2,16,768]{3,2,1,0:T(8,128)(2,1)S(1)}, u32[]{:S(2)}, u32[]{:S(2)}) collective-permute-start(bf16[9,2,16,768]{3,2,1,0:T(8,128)(2,1)S(1)} %slice.51), channel_id=1, source_target_pairs={{0,14},{1,15},{2,0},{3,1},{4,2},{5,3},{6,4},{7,5},{8,6},{9,7},{10,... | collective-permute-start | bytes 1327112 | tf_op jit(solution)/shard_map/cond/branch_1_fun/ppermute | solution.py:881
  59.2 25.4 %collective-permute-start.16 = (bf16[11,2,16,768]{3,2,1,0:T(8,128)(2,1)S(1)}, bf16[11,2,16,768]{3,2,1,0:T(8,128)(2,1)S(1)}, u32[]{:S(2)}, u32[]{:S(2)}) collective-permute-start(bf16[11,2,16,768]{3,2,1,0:T(8,128)(2,1)S(1)} %get-tuple-element.34), channel_id=1, source_target_pairs={{0,2},{1,3},{2,4},{3,5},{4,6},{5,7},{6,8},{7,9},{8,10},{9,11},{10,... | collective-permute-start | bytes 1622024 | tf_op jit(solution)/shard_map/cond/branch_1_fun/ppermute | solution.py:880
  59.3 25.5 %collective-permute-start.20 = (bf16[11,2,16,768]{3,2,1,0:T(8,128)(2,1)S(1)}, bf16[11,2,16,768]{3,2,1,0:T(8,128)(2,1)S(1)}, u32[]{:S(2)}, u32[]{:S(2)}) collective-permute-start(bf16[11,2,16,768]{3,2,1,0:T(8,128)(2,1)S(1)} %get-tuple-element.35), channel_id=1, source_target_pairs={{0,14},{1,15},{2,0},{3,1},{4,2},{5,3},{6,4},{7,5},{8,6},{9,7},{10,... | collective-permute-start | bytes 1622024 | tf_op jit(solution)/shard_map/cond/branch_1_fun/ppermute | solution.py:881
  66.2 15.1 %collective-permute-start.2 = (bf16[6,2,16,768]{3,2,1,0:T(8,128)(2,1)S(1)}, bf16[6,2,16,768]{3,2,1,0:T(8,128)(2,1)S(1)}, u32[]{:S(2)}, u32[]{:S(2)}) collective-permute-start(bf16[6,2,16,768]{3,2,1,0:T(8,128)(2,1)S(1)} %slice.49), channel_id=1, source_target_pairs={{0,2},{1,3},{2,4},{3,5},{4,6},{5,7},{6,8},{7,9},{8,10},{9,11},{10,... | collective-permute-start | bytes 884744 | tf_op jit(solution)/shard_map/cond/branch_1_fun/ppermute | solution.py:880
  66.3 15.1 %collective-permute-start.6 = (bf16[6,2,16,768]{3,2,1,0:T(8,128)(2,1)S(1)}, bf16[6,2,16,768]{3,2,1,0:T(8,128)(2,1)S(1)}, u32[]{:S(2)}, u32[]{:S(2)}) collective-permute-start(bf16[6,2,16,768]{3,2,1,0:T(8,128)(2,1)S(1)} %slice.52), channel_id=1, source_target_pairs={{0,14},{1,15},{2,0},{3,1},{4,2},{5,3},{6,4},{7,5},{8,6},{9,7},{10,... | collective-permute-start | bytes 884744 | tf_op jit(solution)/shard_map/cond/branch_1_fun/ppermute | solution.py:881
  81.3 9.1 %collective-permute-start.3 = (bf16[4,2,16,768]{3,2,1,0:T(8,128)(2,1)S(1)}, bf16[4,2,16,768]{3,2,1,0:T(8,128)(2,1)S(1)}, u32[]{:S(2)}, u32[]{:S(2)}) collective-permute-start(bf16[4,2,16,768]{3,2,1,0:T(8,128)(2,1)S(1)} %slice.50), channel_id=1, source_target_pairs={{0,2},{1,3},{2,4},{3,5},{4,6},{5,7},{6,8},{7,9},{8,10},{9,11},{10,... | collective-permute-start | bytes 589832 | tf_op jit(solution)/shard_map/cond/branch_1_fun/ppermute | solution.py:880
  81.4 8.9 %collective-permute-start.7 = (bf16[4,2,16,768]{3,2,1,0:T(8,128)(2,1)S(1)}, bf16[4,2,16,768]{3,2,1,0:T(8,128)(2,1)S(1)}, u32[]{:S(2)}, u32[]{:S(2)}) collective-permute-start(bf16[4,2,16,768]{3,2,1,0:T(8,128)(2,1)S(1)} %slice.53), channel_id=1, source_target_pairs={{0,14},{1,15},{2,0},{3,1},{4,2},{5,3},{6,4},{7,5},{8,6},{9,7},{10,... | collective-permute-start | bytes 589832 | tf_op jit(solution)/shard_map/cond/branch_1_fun/ppermute | solution.py:881
  84.7 12.2 %collective-permute-start.17 = (bf16[9,2,16,768]{3,2,1,0:T(8,128)(2,1)S(1)}, bf16[9,2,16,768]{3,2,1,0:T(8,128)(2,1)S(1)}, u32[]{:S(2)}, u32[]{:S(2)}) collective-permute-start(bf16[9,2,16,768]{3,2,1,0:T(8,128)(2,1)S(1)} %slice.58), channel_id=1, source_target_pairs={{0,2},{1,3},{2,4},{3,5},{4,6},{5,7},{6,8},{7,9},{8,10},{9,11},{10,... | collective-permute-start | bytes 1327112 | tf_op jit(solution)/shard_map/cond/branch_1_fun/ppermute | solution.py:880
  84.8 12.2 %collective-permute-start.21 = (bf16[9,2,16,768]{3,2,1,0:T(8,128)(2,1)S(1)}, bf16[9,2,16,768]{3,2,1,0:T(8,128)(2,1)S(1)}, u32[]{:S(2)}, u32[]{:S(2)}) collective-permute-start(bf16[9,2,16,768]{3,2,1,0:T(8,128)(2,1)S(1)} %slice.61), channel_id=1, source_target_pairs={{0,14},{1,15},{2,0},{3,1},{4,2},{5,3},{6,4},{7,5},{8,6},{9,7},{10,... | collective-permute-start | bytes 1327112 | tf_op jit(solution)/shard_map/cond/branch_1_fun/ppermute | solution.py:881
  92.8 12.7 %collective-permute-start.10 = (bf16[10,2,16,768]{3,2,1,0:T(8,128)(2,1)S(1)}, bf16[10,2,16,768]{3,2,1,0:T(8,128)(2,1)S(1)}, u32[]{:S(2)}, u32[]{:S(2)}) collective-permute-start(bf16[10,2,16,768]{3,2,1,0:T(8,128)(2,1)S(1)} %get-tuple-element.29), channel_id=1, source_target_pairs={{0,48},{1,49},{2,50},{3,51},{4,52},{5,53},{6,54},{7,55},{8,56},{9,... | collective-permute-start | bytes 1474568 | tf_op jit(solution)/shard_map/cond/branch_1_fun/ppermute | solution.py:881
  96.6 11.5 %collective-permute-start.8 = (bf16[10,2,16,768]{3,2,1,0:T(8,128)(2,1)S(1)}, bf16[10,2,16,768]{3,2,1,0:T(8,128)(2,1)S(1)}, u32[]{:S(2)}, u32[]{:S(2)}) collective-permute-start(bf16[10,2,16,768]{3,2,1,0:T(8,128)(2,1)S(1)} %get-tuple-element.28), channel_id=1, source_target_pairs={{0,16},{1,17},{2,18},{3,19},{4,20},{5,21},{6,22},{7,23},{8,24},{9,... | collective-permute-start | bytes 1474568 | tf_op jit(solution)/shard_map/cond/branch_1_fun/ppermute | solution.py:880
  96.9 11.3 %collective-permute-start.18 = (bf16[6,2,16,768]{3,2,1,0:T(8,128)(2,1)S(1)}, bf16[6,2,16,768]{3,2,1,0:T(8,128)(2,1)S(1)}, u32[]{:S(2)}, u32[]{:S(2)}) collective-permute-start(bf16[6,2,16,768]{3,2,1,0:T(8,128)(2,1)S(1)} %slice.59), channel_id=1, source_target_pairs={{0,2},{1,3},{2,4},{3,5},{4,6},{5,7},{6,8},{7,9},{8,10},{9,11},{10,... | collective-permute-start | bytes 884744 | tf_op jit(solution)/shard_map/cond/branch_1_fun/ppermute | solution.py:880
  97.1 11.3 %collective-permute-start.22 = (bf16[6,2,16,768]{3,2,1,0:T(8,128)(2,1)S(1)}, bf16[6,2,16,768]{3,2,1,0:T(8,128)(2,1)S(1)}, u32[]{:S(2)}, u32[]{:S(2)}) collective-permute-start(bf16[6,2,16,768]{3,2,1,0:T(8,128)(2,1)S(1)} %slice.62), channel_id=1, source_target_pairs={{0,14},{1,15},{2,0},{3,1},{4,2},{5,3},{6,4},{7,5},{8,6},{9,7},{10,... | collective-permute-start | bytes 884744 | tf_op jit(solution)/shard_map/cond/branch_1_fun/ppermute | solution.py:881
  121.3 34.8 %collective-permute-start.31 = (bf16[512,768]{1,0:T(8,128)(2,1)}, bf16[512,768]{1,0:T(8,128)(2,1)S(1)}, u32[]{:S(2)}, u32[]{:S(2)}) collective-permute-start(bf16[512,768]{1,0:T(8,128)(2,1)} %bitcast.20), channel_id=1, source_target_pairs={{0,64},{64,128},{128,192},{192,0},{1,65},{65,129},{129,193},{193,1... | collective-permute-start | bytes 2359304 | tf_op jit(solution)/shard_map/ppermute | solution.py:453
  122.9 35.0 %collective-permute-start.32 = (bf16[512,768]{1,0:T(8,128)(2,1)}, bf16[512,768]{1,0:T(8,128)(2,1)}, u32[]{:S(2)}, u32[]{:S(2)}) collective-permute-start(bf16[512,768]{1,0:T(8,128)(2,1)} %bitcast.22), channel_id=1, source_target_pairs={{0,64},{64,128},{128,192},{192,0},{1,65},{65,129},{129,193},{193,1... | collective-permute-start | bytes 2359304 | tf_op jit(solution)/shard_map/ppermute | solution.py:453
  143.8 8.0 %collective-permute-start.27 = (bf16[96,128]{1,0:T(8,128)(2,1)}, bf16[96,128]{1,0:T(8,128)(2,1)S(1)}, u32[]{:S(2)}, u32[]{:S(2)}) collective-permute-start(bf16[96,128]{1,0:T(8,128)(2,1)} %get-tuple-element.57), channel_id=1, source_target_pairs={{0,2},{1,3},{2,4},{3,5},{4,6},{5,7},{6,8},{7,9},{8,10},{9,11},{10,... | collective-permute-start | bytes 73736 | tf_op jit(solution)/shard_map/ppermute | solution.py:453
  (19 other events, 270.7 us)
